TPU v7x, 128 devices: a whole 4x4x4 slice. The times are simulated.
128 devices in a mesh: row: 8 (over x, core), col: 16 (over y, z).
Axes of the slice: x: 4, y: 4, z: 4, core: 2. Of those that a mesh axis runs over, the one named last changes fastest.
Arguments:
- hidden_states: bfloat16 [16384, 3072], P(('row', 'col')), may hold values from -27 to 27
- norm_gain: float32 [3072], replicated, may hold values from 0.25 to 1.75
- gate_base: bfloat16 [3072, 8192], P('row', 'col'), may hold values from -0.109375 to 0.109375
- up_base: bfloat16 [3072, 8192], P('row', 'col'), may hold values from -0.109375 to 0.109375
- down_base: bfloat16 [8192, 3072], P('col', 'row'), may hold values from -0.0625 to 0.0625
- shrink_gu: bfloat16 [2048, 3072], P('col'), may hold values from -0.109375 to 0.109375
- expand_gu: bfloat16 [2, 1024, 8192], P(None, None, 'col'), may hold values from -1.5 to 1.5
- down_shrink_maps: bfloat16 [1024, 8192], P(None, 'col'), may hold values from -0.0625 to 0.0625
- down_expand_maps: bfloat16 [1024, 3072], P('col'), may hold values from -1.5 to 1.5
- token_adapter: int32 [16384], P('row'), may hold values from 0 to 63, as said below
- adapter_slot: int32 [64], replicated, may hold values from 0 to 63, as said below
Outputs:
- mlp_out: bfloat16 [16384, 3072], P(('row', 'col'))
Inputs may be any that keep to these rules, and one draw needn't show every extreme that they name: `token_adapter`: split the tokens into aligned blocks of 128 and groups of 16 consecutive blocks: no block has more than 16 tokens whose adapters share one owner, and in each group one owner has exactly 16 tokens in every block. `adapter_slot`: A permutation of the slots.
All inputs are finite; a program needn't handle non-finite values.
Results may differ from a plain program's by a relative error of at most 0.017.
Values may be sent and summed in bfloat16 or wider, within the bound.
No kernel may reach another device: no remote copies, remote signals or barrier semaphores. Data moves between devices by JAX's collectives and lax.ppermute only.
A program may use at most 128 MiB of HBM per device.

v0:
```python
import functools

import jax
import jax.numpy as jnp
from jax import lax
from jax.experimental import pallas as pl
from jax.experimental.pallas import tpu as pltpu
from jax.sharding import Mesh, PartitionSpec as P


eps = 1e-05
ALL = ("x", "c", "y", "h", "l")
GROUP = ("c", "y", "l")

SOURCE = (0, 0, 0, 1, 1, 2, 4)
STEPS = (
    (("y", -1), ("y", 1), ("l", 1), ("y", -1), ("l", 1), ("l", 1), ("l", 1)),
    (("l", 1), ("y", 1), ("y", -1), ("y", 1), ("y", -1), ("y", 1), ("y", 1)),
)
BLOCK_Y = ((0, 1, -1, 0, 2, 1, -1, 2), (0, 0, -1, 1, -1, 1, 2, 2))
BLOCK_L = ((0, 0, 0, 1, 0, 1, 1, 1), (0, 1, 0, 0, 1, 1, 0, 1))
X_ORDER = (0, -1, 1, 2)


def flat(x, c, y, z):
    return (((x % 4) * 2 + c % 2) * 4 + y % 4) * 4 + z % 4


def pairs_of(move):
    return [
        (flat(x, c, y, z), flat(*move(x, c, y, z)))
        for x in range(4)
        for c in range(2)
        for y in range(4)
        for z in range(4)
    ]


def tree_pairs(k):
    def move(x, c, y, z):
        axis, shift = STEPS[c][k]
        return (x, c, y + shift, z) if axis == "y" else (x, c, y, z ^ 1)

    return pairs_of(move)


TREE = [tree_pairs(k) for k in range(7)]
TREE_BACK = [[(b, a) for a, b in pairs] for pairs in TREE]
CORE = pairs_of(lambda x, c, y, z: (x, 1 - c, y, z))
SAME_ROLE = [pair for pair in pairs_of(lambda x, c, y, z: (x, c, y, 3 - z)) if pair[0] // 16 % 2 == 1]
OTHER_ROLE = pairs_of(lambda x, c, y, z: (x, 1 - c, y, 3 - z if c == 0 else z))
X_UP = pairs_of(lambda x, c, y, z: (x + 1, c, y, z))
X_DOWN = pairs_of(lambda x, c, y, z: (x - 1, c, y, z))


HALVES = ((7, 6, 5, 4), (0, 1, 2, 3))
ROW_BLOCKS = tuple(
    half[2 * pair + j] + 8 * part for half in HALVES for pair in range(2) for part in range(2) for j in range(2)
)
LATE_BLOCKS = 4
TILE = 256


def send(value, pairs):
    return lax.ppermute(value, ALL, pairs)


def contract_trailing(left, right):
    return lax.dot_general(
        left, right, (((left.ndim - 1,), (1,)), ((), ())), preferred_element_type=jnp.float32
    )


def dot(left, right):
    return jnp.dot(left, right, preferred_element_type=jnp.float32)


def rms_normed(states, norm_gain):
    values = states.astype(jnp.float32)
    scale_inv = lax.rsqrt(jnp.mean(values * values, axis=-1, keepdims=True) + eps)
    return (values * scale_inv * norm_gain).astype(jnp.bfloat16)


def lanes(rows, count, group):
    return lax.broadcasted_iota(jnp.int32, (rows, count), 1) // group


def kept(mask, values):
    return jnp.where(mask, values, 0.0).astype(jnp.bfloat16)


def place_kernel(at, slot_of, own, other, out, slots):
    ci, yi, hi, li = (at[i] for i in range(4))
    for part, adapters in enumerate((own, other)):
        ids = adapters[...]
        found = jnp.zeros(ids.shape, jnp.int32)
        for adapter in range(slot_of.shape[0]):
            found = jnp.where(ids == adapter, slot_of[adapter], found)
        slots[part] = found
    role_col = yi * 4 + jnp.where(ci == 0, hi * 2 + li, 3 - hi * 2 - li)
    group_at = (ci * 4 + yi) * 2 + li
    earlier = lax.broadcasted_iota(jnp.int32, (128, 128), 0) < lax.broadcasted_iota(jnp.int32, (128, 128), 1)
    for i, k in enumerate(ROW_BLOCKS):
        part, k = k // 8, k % 8
        c = ci if part == 0 else 1 - ci
        y = (yi + 4 + jnp.where(c == 0, BLOCK_Y[0][k], BLOCK_Y[1][k])) & 3
        l = (li + jnp.where(c == 0, BLOCK_L[0][k], BLOCK_L[1][k])) & 1
        block_at = (c * 4 + y) * 2 + l
        slot = slots[part, pl.ds(y * 4 + hi * 2 + l, 1), :]
        owner = slot >> 2
        owner_z = owner & 3
        native = (owner_z >> 1) == hi
        owner_l = jnp.where(native, owner_z, 3 - owner_z) & 1
        owner_at = (jnp.where(native, 0, 4) + (owner >> 2)) * 2 + owner_l
        along = jnp.broadcast_to(owner_at, (128, 128))
        alike = jnp.where((along == along.T) & earlier, 1, 0)
        position = jnp.sum(alike, axis=0, keepdims=True)
        is_mine = owner_at == group_at
        columns = (
            slot,
            owner_at * 64 + block_at * 4 + (position >> 2),
            position & 3,
            owner_at * 32 + block_at * 2 + (position >> 3),
            position & 7,
            jnp.where(is_mine, slot - role_col * 4, -1),
            jnp.where(is_mine, block_at * 4 + (position >> 2), -1),
            jnp.where(is_mine, block_at * 2 + (position >> 3), -1),
        )
        for j, column in enumerate(columns):
            out[i, j : j + 1, :] = column


def places(ints, i, first=0):
    across = jnp.concatenate([ints[first + 2 * i], ints[first + 2 * i + 1]], axis=1)
    return across.T, across


def rank_kernel(first, shrink, ints, fold, *refs):
    shards, (out, rows, sems) = refs[:-3], refs[-3:]
    for i, shard in enumerate(shards):
        pltpu.make_async_copy(shard, rows.at[pl.ds(i * 128, 128)], sems.at[i * 128 // TILE]).start()
    out[...] = jnp.zeros(out.shape, jnp.float32)

    def tile(i, carry):
        part = pl.ds(pl.multiple_of(i * TILE, TILE), TILE)
        down, across = places(ints, i, first)
        pltpu.make_async_copy(rows.at[part], rows.at[part], sems.at[i]).wait()
        group = lanes(TILE, 128, 32)
        values = kept(group == down[:, 5:6], contract_trailing(rows[part, :], shrink[...]))
        values = kept(group == down[:, 2:3], dot(values, fold[...]))
        place = lax.broadcasted_iota(jnp.int32, (64, TILE), 0) == across[6:7]
        out[...] += dot(place.astype(jnp.bfloat16), values)
        return carry

    lax.fori_loop(0, rows.shape[0] // TILE, tile, 0)


def hidden_kernel(slab_at, ranks, ints, expand, down_shrink, to_gate, to_up, fold, *refs):
    shards, pieces, (hidden, packed, rows, weight, total, row_sems, sem) = refs[:16], refs[16:24], refs[24:]
    slab = pieces[0].shape[0]
    for i, piece in enumerate(pieces):
        start = pl.multiple_of(slab_at[i] * slab, 128)
        pltpu.make_async_copy(piece, weight.at[pl.ds(start, slab)], sem.at[0]).start()
    for i, shard in enumerate(shards):
        pltpu.make_async_copy(shard, rows.at[pl.ds(i * 128, 128)], row_sems.at[i * 128 // TILE]).start()
    total[...] = jnp.zeros(total.shape, jnp.float32)
    pltpu.make_async_copy(weight, weight, sem.at[0]).wait()
    units = hidden.shape[1]

    def tile(i, carry):
        part = pl.ds(pl.multiple_of(i * TILE, TILE), TILE)
        down, across = places(ints, i)
        pltpu.make_async_copy(rows.at[part], rows.at[part], row_sems.at[i]).wait()
        both = dot(rows[part, :], weight[...])
        place = lanes(TILE, ranks.shape[0], 1) == down[:, 1:2]
        own = kept(lanes(TILE, 128, 32) == down[:, 2:3], dot(place.astype(jnp.bfloat16), ranks[...]))
        chosen = lanes(TILE, to_gate.shape[1], 16) == down[:, 0:1]
        gate = both[:, :units] + dot(kept(chosen, dot(own, to_gate[...])), expand[0])
        up = both[:, units:] + dot(kept(chosen, dot(own, to_up[...])), expand[1])
        values = (gate / (1.0 + jnp.exp(-gate)) * up).astype(jnp.bfloat16)
        hidden[part, :] = values
        parts = dot(kept(chosen, contract_trailing(values, down_shrink[...])), fold[...])
        parts = kept(lanes(TILE, 128, 16) == down[:, 4:5], parts)
        place = lax.broadcasted_iota(jnp.int32, (total.shape[0], TILE), 0) == across[3:4]
        total[...] += dot(place.astype(jnp.bfloat16), parts)
        return carry

    lax.fori_loop(0, rows.shape[0] // TILE, tile, 0)
    packed[...] = total[...].astype(jnp.bfloat16)


def down_kernel(first, slab_at, hidden, ranks, ints, down_expand, widen, *refs):
    pieces, (mine, theirs, weight, sem) = refs[:8], refs[8:]
    slab = pieces[0].shape[1]
    for i, piece in enumerate(pieces):
        start = pl.multiple_of(slab_at[i] * slab, 128)
        pltpu.make_async_copy(piece, weight.at[:, pl.ds(start, slab)], sem.at[0]).start()
    pltpu.make_async_copy(weight, weight, sem.at[0]).wait()
    for t, out in enumerate((mine, theirs)):

        def tile(i, carry):
            at = pl.ds(pl.multiple_of(i * TILE, TILE), TILE)
            part = pl.ds(pl.multiple_of((2 * i + t) * TILE, TILE), TILE)
            numbers, _ = places(ints, 2 * i + t, first)
            place = lanes(TILE, ranks.shape[0], 1) == numbers[:, 7:8]
            own = kept(lanes(TILE, 128, 16) == numbers[:, 4:5], dot(place.astype(jnp.bfloat16), ranks[...]))
            own = kept(lanes(TILE, 64, 16) == numbers[:, 5:6], dot(own, widen[...]))
            out[at, :] = (dot(hidden[part, :], weight[...]) + dot(own, down_expand[...])).astype(jnp.bfloat16)
            return carry

        lax.fori_loop(0, out.shape[0] // TILE, tile, 0)


def weight_blocks(shard, ci):
    other = send(shard, OTHER_ROLE)
    same = jnp.where(ci == 0, shard, send(shard, SAME_ROLE))
    same_low, other_high = send(same, X_UP), send(other, X_DOWN)
    other_low, same_high = send(other, X_UP), send(same, X_DOWN)
    same_far, other_far = send(same_low, X_UP), send(other_high, X_DOWN)
    return [same, same_low, same_high, same_far, other, other_low, other_high, other_far]


def local(
    hidden_states,
    norm_gain,
    gate_base,
    up_base,
    down_base,
    shrink_gu,
    expand_gu,
    down_shrink_maps,
    down_expand_maps,
    token_adapter,
    adapter_slot,
):
    xi, ci, yi, hi, li = (lax.axis_index(name) for name in ALL)
    own_count, width = hidden_states.shape
    units = gate_base.shape[1]
    adapter_list = adapter_slot.shape[0]
    owner_partial = adapter_list // 16
    rank = down_expand_maps.shape[0] // owner_partial
    total = 16 * own_count
    adapter_range = jnp.arange(adapter_list, dtype=jnp.int32)
    group_range = jnp.arange(16, dtype=jnp.int32)

    slab_at = [((xi + dx) % 4) * 2 + (ci if half == 0 else 1 - ci) for half in range(2) for dx in X_ORDER]

    slab_at = jnp.stack(slab_at).astype(jnp.int32)

    gate_up = weight_blocks(jnp.concatenate([gate_base, up_base], axis=1), ci)
    mine = [rms_normed(hidden_states, norm_gain)]
    for k in range(7):
        mine.append(send(mine[SOURCE[k]], TREE[k]))
    theirs = [send(block, CORE) for block in mine]
    shards = [(mine + theirs)[k] for k in ROW_BLOCKS]

    shrink = send(shrink_gu, OTHER_ROLE)
    expand = send(expand_gu, OTHER_ROLE)
    down = weight_blocks(down_base, ci)
    down_shrink = send(down_shrink_maps, OTHER_ROLE)
    down_expand = send(down_expand_maps, OTHER_ROLE)

    half_count = total // 2
    vmem = pl.BlockSpec(memory_space=pltpu.VMEM)
    smem = pl.BlockSpec(memory_space=pltpu.SMEM)
    stay = pl.BlockSpec(memory_space=pl.ANY)

    def matching(row_count, row_period, column_count, column_period, shift=0):
        row = jnp.arange(row_count)[:, None] % row_period - shift
        return (row == jnp.arange(column_count)[None, :] % column_period).astype(jnp.bfloat16)

    own_adapters = token_adapter.reshape(16, own_count)
    ints = pl.pallas_call(
        place_kernel,
        out_shape=jax.ShapeDtypeStruct((16, 8, own_count), jnp.int32),
        in_specs=[smem, smem, vmem, vmem],
        out_specs=vmem,
        scratch_shapes=[pltpu.VMEM((2, 16, own_count), jnp.int32)],
        name="places",
    )(jnp.stack([ci, yi, hi, li]), adapter_slot, own_adapters, send(own_adapters, CORE))

    def ranks_of(first, last):
        count = (last - first) * own_count
        return pl.pallas_call(
            functools.partial(rank_kernel, first),
            out_shape=jax.ShapeDtypeStruct((64, 128), jnp.float32),
            in_specs=[vmem] * 3 + [stay] * (last - first),
            out_specs=vmem,
            scratch_shapes=[
                pltpu.VMEM((count, width), jnp.bfloat16),
                pltpu.SemaphoreType.DMA((count // TILE,)),
            ],
            name="ranks",
        )(shrink, ints, matching(128, 2 * rank, 128, 2 * rank), *shards[first:last])

    packed = ranks_of(LATE_BLOCKS, 16) + ranks_of(0, LATE_BLOCKS)
    spread = jnp.broadcast_to(packed.astype(jnp.bfloat16)[None], (16, 64, 128))
    ranks = lax.all_to_all(spread, GROUP, split_axis=0, concat_axis=0, tiled=True).reshape(1024, 128)

    hidden, packed_down = pl.pallas_call(
        hidden_kernel,
        out_shape=(jax.ShapeDtypeStruct((total, units), jnp.bfloat16), jax.ShapeDtypeStruct((512, 128), jnp.bfloat16)),
        in_specs=[smem] + [vmem] * 7 + [stay] * 24,
        out_specs=(vmem, vmem),
        scratch_shapes=[
            pltpu.VMEM((total, width), jnp.bfloat16),
            pltpu.VMEM((width, 2 * units), jnp.bfloat16),
            pltpu.VMEM((512, 128), jnp.float32),
            pltpu.SemaphoreType.DMA((total // TILE,)),
            pltpu.SemaphoreType.DMA((1,)),
        ],
        name="hidden",
    )(
        slab_at,
        ranks,
        ints,
        expand,
        down_shrink,
        matching(128, 2 * rank, adapter_list * rank, rank),
        matching(128, 2 * rank, adapter_list * rank, rank, rank),
        matching(adapter_list * rank, rank, 128, rank),
        *shards,
        *gate_up,
    )

    arrived = lax.all_to_all(
        packed_down.reshape(16, 32, 128), GROUP, split_axis=0, concat_axis=0, tiled=True
    )
    down_ranks = jnp.sum(arrived.astype(jnp.float32), axis=0).astype(jnp.bfloat16)

    def down_half(i):
        return pl.pallas_call(
            functools.partial(down_kernel, 8 * i),
            grid=(1,),
            out_shape=(jax.ShapeDtypeStruct((half_count // 2, width), jnp.bfloat16),) * 2,
            in_specs=[smem, pl.BlockSpec((half_count, units), lambda g: (i, 0))] + [vmem] * 4 + [stay] * 8,
            out_specs=(vmem, vmem),
            scratch_shapes=[pltpu.VMEM((units, width), jnp.bfloat16), pltpu.SemaphoreType.DMA((1,))],
            name="down",
        )(
            slab_at,
            hidden,
            down_ranks,
            ints,
            down_expand,
            matching(128, rank, owner_partial * rank, rank),
            *down,
        )

    def add(left, right):
        return (left.astype(jnp.float32) + right.astype(jnp.float32)).astype(jnp.bfloat16)

    sums = [None] * 8
    for i in range(2):
        mine_part, theirs_part = down_half(i)
        swapped = send(theirs_part, CORE)
        added = [
            add(mine_part[j * own_count : (j + 1) * own_count], swapped[j * own_count : (j + 1) * own_count])
            for j in range(4)
        ]
        for k, value in zip(HALVES[i], lax.optimization_barrier(added)):
            sums[k] = value
    for k in (6, 5, 4, 3, 2, 1, 0):
        sums[SOURCE[k]] = add(sums[SOURCE[k]], send(sums[k + 1], TREE_BACK[k]))
    return sums[0]


def solution(mesh):
    fine = Mesh(mesh.devices.reshape(4, 2, 4, 2, 2), ALL)
    row, col = ("x", "c"), ("y", "h", "l")
    in_specs = (
        P(row + col, None),
        P(),
        P(row, col),
        P(row, col),
        P(col, row),
        P(col, None),
        P(None, None, col),
        P(None, col),
        P(col, None),
        P(row),
        P(),
    )
    out_specs = P(row + col, None)
    return jax.shard_map(local, mesh=fine, in_specs=in_specs, out_specs=out_specs, check_vma=False)
```

profile of v0, /device:TPU:1, one launch (start us, length us, event | category | flops | bytes accessed | tf_op | source)
XLA Modules:
  0.0 261.0 jit_solution(15107445168241088941)
XLA Ops:
  6.7 4.1 %collective-permute-start.28 = (bf16[512,384]{1,0:T(8,128)(2,1)S(1)}, bf16[512,384]{1,0:T(8,128)(2,1)S(1)}, u32[]{:S(2)}, u32[]{:S(2)}) collective-permute-start(bf16[512,384]{1,0:T(8,128)(2,1)S(1)} %copy-done.28), channel_id=1, source_target_pairs={{16,19},{17,18},{18,17},{19,16},{20,23},{21,22},{22,21},{23,20},{2... | collective-permute-start | bytes 1179656 | tf_op jit(solution)/shard_map/ppermute | solution.py:65
  14.2 4.5 %collective-permute-done.28 = bf16[512,384]{1,0:T(8,128)(2,1)S(1)} collective-permute-done((bf16[512,384]{1,0:T(8,128)(2,1)S(1)}, bf16[512,384]{1,0:T(8,128)(2,1)S(1)}, u32[]{:S(2)}, u32[]{:S(2)}) %collective-permute-start.28) | collective-permute-done | bytes 393248 | tf_op jit(solution)/shard_map/ppermute | solution.py:65
  22.6 4.1 %collective-permute-start.19 = (bf16[384,1024]{1,0:T(8,128)(2,1)}, bf16[384,1024]{1,0:T(8,128)(2,1)}, u32[]{:S(2)}, u32[]{:S(2)}) collective-permute-start(bf16[384,1024]{1,0:T(8,128)(2,1)} %constant_dynamic-update-slice_fusion), channel_id=1, source_target_pairs={{16,19},{17,18},{18,17},{19,16},{20,23},{21,22},{22,21},{23,20},{2... | collective-permute-start | bytes 2359304 | tf_op jit(solution)/shard_map/ppermute | solution.py:65
  30.0 9.6 %collective-permute-done.shrink = bf16[128,3072]{1,0:T(8,128)(2,1)} collective-permute-done((bf16[128,3072]{1,0:T(8,128)(2,1)}, bf16[128,3072]{1,0:T(8,128)(2,1)}, u32[]{:S(2)}, u32[]{:S(2)}) %collective-permute-start) | collective-permute-done | bytes 786464 | tf_op jit(solution)/shard_map/ppermute | solution.py:65
  41.9 3.4 %collective-permute-done.19 = bf16[384,1024]{1,0:T(8,128)(2,1)} collective-permute-done((bf16[384,1024]{1,0:T(8,128)(2,1)}, bf16[384,1024]{1,0:T(8,128)(2,1)}, u32[]{:S(2)}, u32[]{:S(2)}) %collective-permute-start.19) | collective-permute-done | bytes 786464 | tf_op jit(solution)/shard_map/ppermute | solution.py:65
  46.3 4.5 %collective-permute-done.23.refs_20_ = bf16[384,1024]{1,0:T(8,128)(2,1)} collective-permute-done((bf16[384,1024]{1,0:T(8,128)(2,1)}, bf16[384,1024]{1,0:T(8,128)(2,1)}, u32[]{:S(2)}, u32[]{:S(2)}) %collective-permute-start.23) | collective-permute-done | bytes 786464 | tf_op jit(solution)/shard_map/ppermute | solution.py:65
  52.7 9.3 %collective-permute-done.18.down_shrink = bf16[1024,512]{1,0:T(8,128)(2,1)} collective-permute-done((bf16[1024,512]{1,0:T(8,128)(2,1)}, bf16[1024,512]{1,0:T(8,128)(2,1)}, u32[]{:S(2)}, u32[]{:S(2)}) %collective-permute-start.18) | collective-permute-done | bytes 1048608 | tf_op jit(solution)/shard_map/ppermute | solution.py:65
  69.2 6.7 %collective-permute-done.14.refs_1_ = bf16[128,3072]{1,0:T(8,128)(2,1)S(1)} collective-permute-done((bf16[128,3072]{1,0:T(8,128)(2,1)S(1)}, bf16[128,3072]{1,0:T(8,128)(2,1)S(1)}, u32[]{:S(2)}, u32[]{:S(2)}) %collective-permute-start.14) | collective-permute-done | bytes 786464 | tf_op jit(solution)/shard_map/ppermute | solution.py:65
  75.9 9.3 %collective-permute-done.20.refs_17_ = bf16[384,1024]{1,0:T(8,128)(2,1)} collective-permute-done((bf16[384,1024]{1,0:T(8,128)(2,1)S(1)}, bf16[384,1024]{1,0:T(8,128)(2,1)}, u32[]{:S(2)}, u32[]{:S(2)}) %collective-permute-start.20) | collective-permute-done | bytes 786464 | tf_op jit(solution)/shard_map/ppermute | solution.py:65
  95.8 9.1 %ranks.2 = f32[64,128]{1,0:T(8,128)} custom-call(bf16[128,3072]{1,0:T(8,128)(2,1)} %collective-permute-done.shrink, s32[16,8,128]{2,1,0:T(8,128)} %places.1.ints, bf16[128,128]{1,0:T(8,128)(2,1)} %compare_convert_fusion.4.fold, bf16[128,3072]{1,0:T(8,128)(2,1)} %collective-permute-done.3.refs_0_.refs_4_, ...), custom_call_target="tpu_custom_call" | custom-call | tf_op jit(solution)/shard_map/ranks/pallas_call | solution.py:284
  104.9 5.1 %ranks.3 = f32[64,128]{1,0:T(8,128)} custom-call(bf16[128,3072]{1,0:T(8,128)(2,1)} %collective-permute-done.shrink, s32[16,8,128]{2,1,0:T(8,128)} %places.1.ints, bf16[128,128]{1,0:T(8,128)(2,1)} %compare_convert_fusion.4.fold, bf16[128,3072]{1,0:T(8,128)(2,1)} %collective-permute-done.13.refs_0_, bf16[128,3072]{1,0:T(8,128)(2,1)} %copy-done.11, ...), custom_call_target="tpu_custom_call" | custom-call | tf_op jit(solution)/shard_map/ranks/pallas_call | solution.py:284
  111.6 5.2 %all-to-all-start = ((bf16[16,64,128]{2,1,0:T(8,128)(2,1)}), bf16[16,64,128]{2,1,0:T(8,128)(2,1)}, u32[]{:S(2)}, u32[]{:S(2)}) async-start(bf16[16,64,128]{2,1,0:T(8,128)(2,1)} %broadcast_in_dim.2), calls=%async_computation | async-start | bytes 524288 | tf_op jit(solution)/shard_map/all_to_all | solution.py:298
  118.6 6.8 %collective-permute-done.22.refs_19_ = bf16[384,1024]{1,0:T(8,128)(2,1)} collective-permute-done((bf16[384,1024]{1,0:T(8,128)(2,1)}, bf16[384,1024]{1,0:T(8,128)(2,1)}, u32[]{:S(2)}, u32[]{:S(2)}) %collective-permute-start.22) | collective-permute-done | bytes 786464 | tf_op jit(solution)/shard_map/ppermute | solution.py:65
  125.4 2.7 %collective-permute-start.35 = (bf16[512,384]{1,0:T(8,128)(2,1)S(1)}, bf16[512,384]{1,0:T(8,128)(2,1)S(1)}, u32[]{:S(2)}, u32[]{:S(2)}) collective-permute-start(bf16[512,384]{1,0:T(8,128)(2,1)S(1)} %copy-done.20), channel_id=1, source_target_pairs={{0,96},{1,97},{2,98},{3,99},{4,100},{5,101},{6,102},{7,103},{8,104... | collective-permute-start | bytes 1179656 | tf_op jit(solution)/shard_map/ppermute | solution.py:65
  129.6 39.2 %hidden.1 = (bf16[2048,512]{1,0:T(8,128)(2,1)}, bf16[512,128]{1,0:T(8,128)(2,1)}) custom-call(s32[8]{0:T(128)} %stack.50.slab_at, bf16[1024,128]{1,0:T(8,128)(2,1)} %bitcast.13.ranks, s32[16,8,128]{2,1,0:T(8,128)} %places.1.ints, bf16[2,1024,512]{2,1,0:T(8,128)(2,1)} %collective-permute-done.17.expand, ...), custom_call_target="tpu_custom_call" | custom-call | tf_op jit(solution)/shard_map/hidden/pallas_call | solution.py:300
  168.9 7.3 %all-to-all-start.1 = ((bf16[16,32,128]{2,1,0:T(8,128)(2,1)}), bf16[16,32,128]{2,1,0:T(8,128)(2,1)}, u32[]{:S(2)}, u32[]{:S(2)}) async-start(bf16[16,32,128]{2,1,0:T(8,128)(2,1)} %bitcast.15), calls=%async_computation.1 | async-start | bytes 262144 | tf_op jit(solution)/shard_map/all_to_all | solution.py:326
  176.9 5.5 %all-to-all-done.1 = bf16[16,32,128]{2,1,0:T(8,128)(2,1)} async-done(((bf16[16,32,128]{2,1,0:T(8,128)(2,1)}), bf16[16,32,128]{2,1,0:T(8,128)(2,1)}, u32[]{:S(2)}, u32[]{:S(2)}) %all-to-all-start.1) | async-done | bytes 131104 | tf_op jit(solution)/shard_map/all_to_all | solution.py:326
  185.2 12.1 %down.3 = (bf16[512,3072]{1,0:T(8,128)(2,1)}, bf16[512,3072]{1,0:T(8,128)(2,1)}) custom-call(s32[8]{0:T(128)} %stack.50.slab_at, bf16[2048,512]{1,0:T(8,128)(2,1)} %get-tuple-element.19.hidden, bf16[32,128]{1,0:T(8,128)(2,1)} %reduce_sum.22.ranks, s32[16,8,128]{2,1,0:T(8,128)} %places.1.ints, bf16[64,3072]{1,0:T(8,128)(2,1)} %copy-done.21, ...), custom_call_target="tpu_custom_call" | custom-call | tf_op jit(solution)/shard_map/down/pallas_call | solution.py:332
  198.5 12.0 %down.2 = (bf16[512,3072]{1,0:T(8,128)(2,1)}, bf16[512,3072]{1,0:T(8,128)(2,1)}) custom-call(s32[8]{0:T(128)} %stack.50.slab_at, bf16[2048,512]{1,0:T(8,128)(2,1)} %get-tuple-element.19.hidden, bf16[32,128]{1,0:T(8,128)(2,1)} %reduce_sum.22.ranks, s32[16,8,128]{2,1,0:T(8,128)} %places.1.ints, bf16[64,3072]{1,0:T(8,128)(2,1)} %copy-done.21, ...), custom_call_target="tpu_custom_call" | custom-call | tf_op jit(solution)/shard_map/down/pallas_call | solution.py:332
  210.8 3.1 %add_convert_fusion.6 = (bf16[128,3072]{1,0:T(8,128)(2,1)S(1)}, bf16[128,3072]{1,0:T(8,128)(2,1)S(1)}, bf16[128,3072]{1,0:T(8,128)(2,1)S(1)}, bf16[128,3072]{1,0:T(8,128)(2,1)S(1)}) fusion(bf16[512,3072]{1,0:T(8,128)(2,1)} %collective-permute-done.38, bf16[512,3072]{1,0:T(8,128)(2,1)S(1)} %copy-done.14), kind=kLoop, calls=%fused_computation.11 | loop fusion | flops 6291456 | bytes 9437184 | tf_op jit(solution)/shard_map/convert_element_type | solution.py:351
  216.3 8.8 %collective-permute-done.42 = bf16[128,3072]{1,0:T(8,128)(2,1)S(1)} collective-permute-done((bf16[128,3072]{1,0:T(8,128)(2,1)S(1)}, bf16[128,3072]{1,0:T(8,128)(2,1)S(1)}, u32[]{:S(2)}, u32[]{:S(2)}) %collective-permute-start.42) | collective-permute-done | bytes 786464 | tf_op jit(solution)/shard_map/ppermute | solution.py:65
  228.5 5.1 %collective-permute-done.39 = bf16[128,3072]{1,0:T(8,128)(2,1)S(1)} collective-permute-done((bf16[128,3072]{1,0:T(8,128)(2,1)S(1)}, bf16[128,3072]{1,0:T(8,128)(2,1)S(1)}, u32[]{:S(2)}, u32[]{:S(2)}) %collective-permute-start.39) | collective-permute-done | bytes 786464 | tf_op jit(solution)/shard_map/ppermute | solution.py:65
  235.6 10.2 %collective-permute-done.43 = bf16[128,3072]{1,0:T(8,128)(2,1)S(1)} collective-permute-done((bf16[128,3072]{1,0:T(8,128)(2,1)S(1)}, bf16[128,3072]{1,0:T(8,128)(2,1)S(1)}, u32[]{:S(2)}, u32[]{:S(2)}) %collective-permute-start.43) | collective-permute-done | bytes 786464 | tf_op jit(solution)/shard_map/ppermute | solution.py:65
  247.5 11.3 %collective-permute-done.40 = bf16[128,3072]{1,0:T(8,128)(2,1)S(1)} collective-permute-done((bf16[128,3072]{1,0:T(8,128)(2,1)S(1)}, bf16[128,3072]{1,0:T(8,128)(2,1)S(1)}, u32[]{:S(2)}, u32[]{:S(2)}) %collective-permute-start.40) | collective-permute-done | bytes 786464 | tf_op jit(solution)/shard_map/ppermute | solution.py:65
  (167 shorter events, 61.2 us)
Async XLA Ops:
  2.9 19.7 %collective-permute-start.2 = (bf16[128,3072]{1,0:T(8,128)(2,1)S(1)}, bf16[128,3072]{1,0:T(8,128)(2,1)S(1)}, u32[]{:S(2)}, u32[]{:S(2)}) collective-permute-start(bf16[128,3072]{1,0:T(8,128)(2,1)S(1)} %fusion.2.refs_4_.refs_8_), channel_id=1, source_target_pairs={{0,12},{1,13},{2,14},{3,15},{4,0},{5,1},{6,2},{7,3},{8,4},{9,5},{1... | collective-permute-start | bytes 2359304 | tf_op jit(solution)/shard_map/ppermute | solution.py:65
  5.4 21.3 %collective-permute-start.9 = (bf16[128,3072]{1,0:T(8,128)(2,1)S(1)}, bf16[128,3072]{1,0:T(8,128)(2,1)S(1)}, u32[]{:S(2)}, u32[]{:S(2)}) collective-permute-start(bf16[128,3072]{1,0:T(8,128)(2,1)S(1)} %fusion.2.refs_4_.refs_8_), channel_id=1, source_target_pairs={{0,4},{1,5},{2,6},{3,7},{4,8},{5,9},{6,10},{7,11},{8,12},{9,13},{1... | collective-permute-start | bytes 2359304 | tf_op jit(solution)/shard_map/ppermute | solution.py:65
  22.6 22.7 %collective-permute-start.19 = (bf16[384,1024]{1,0:T(8,128)(2,1)}, bf16[384,1024]{1,0:T(8,128)(2,1)}, u32[]{:S(2)}, u32[]{:S(2)}) collective-permute-start(bf16[384,1024]{1,0:T(8,128)(2,1)} %constant_dynamic-update-slice_fusion), channel_id=1, source_target_pairs={{16,19},{17,18},{18,17},{19,16},{20,23},{21,22},{22,21},{23,20},{2... | collective-permute-start | bytes 2359304 | tf_op jit(solution)/shard_map/ppermute | solution.py:65
  26.8 24.0 %collective-permute-start.23 = (bf16[384,1024]{1,0:T(8,128)(2,1)}, bf16[384,1024]{1,0:T(8,128)(2,1)}, u32[]{:S(2)}, u32[]{:S(2)}) collective-permute-start(bf16[384,1024]{1,0:T(8,128)(2,1)} %constant_dynamic-update-slice_fusion), channel_id=1, source_target_pairs={{0,19},{1,18},{2,17},{3,16},{4,23},{5,22},{6,21},{7,20},{8,27},{9,... | collective-permute-start | bytes 2359304 | tf_op jit(solution)/shard_map/ppermute | solution.py:65
  26.9 35.1 %collective-permute-start.18 = (bf16[1024,512]{1,0:T(8,128)(2,1)}, bf16[1024,512]{1,0:T(8,128)(2,1)}, u32[]{:S(2)}, u32[]{:S(2)}) collective-permute-start(bf16[1024,512]{1,0:T(8,128)(2,1)} %param.18), channel_id=1, source_target_pairs={{0,19},{1,18},{2,17},{3,16},{4,23},{5,22},{6,21},{7,20},{8,27},{9,... | collective-permute-start | bytes 3145736 | tf_op jit(solution)/shard_map/ppermute | solution.py:65
  28.7 23.5 %collective-permute-start.29 = (bf16[512,384]{1,0:T(8,128)(2,1)S(1)}, bf16[512,384]{1,0:T(8,128)(2,1)S(1)}, u32[]{:S(2)}, u32[]{:S(2)}) collective-permute-start(bf16[512,384]{1,0:T(8,128)(2,1)S(1)} %broadcast_select_fusion.1.refs_0_), channel_id=1, source_target_pairs={{0,32},{1,33},{2,34},{3,35},{4,36},{5,37},{6,38},{7,39},{8,40},{9,... | collective-permute-start | bytes 1179656 | tf_op jit(solution)/shard_map/ppermute | solution.py:65
  64.4 20.8 %collective-permute-start.20 = (bf16[384,1024]{1,0:T(8,128)(2,1)S(1)}, bf16[384,1024]{1,0:T(8,128)(2,1)}, u32[]{:S(2)}, u32[]{:S(2)}) collective-permute-start(bf16[384,1024]{1,0:T(8,128)(2,1)S(1)} %broadcast_select_fusion.refs_16_), channel_id=1, source_target_pairs={{0,32},{1,33},{2,34},{3,35},{4,36},{5,37},{6,38},{7,39},{8,40},{9,... | collective-permute-start | bytes 2359304 | tf_op jit(solution)/shard_map/ppermute | solution.py:65
  65.6 20.1 %collective-permute-start.25 = (bf16[384,1024]{1,0:T(8,128)(2,1)}, bf16[384,1024]{1,0:T(8,128)(2,1)}, u32[]{:S(2)}, u32[]{:S(2)}) collective-permute-start(bf16[384,1024]{1,0:T(8,128)(2,1)} %collective-permute-done.23.refs_20_), channel_id=1, source_target_pairs={{0,96},{1,97},{2,98},{3,99},{4,100},{5,101},{6,102},{7,103},{8,104... | collective-permute-start | bytes 2359304 | tf_op jit(solution)/shard_map/ppermute | solution.py:65
  67.1 18.8 %collective-permute-start.13 = (bf16[128,3072]{1,0:T(8,128)(2,1)}, bf16[128,3072]{1,0:T(8,128)(2,1)}, u32[]{:S(2)}, u32[]{:S(2)}) collective-permute-start(bf16[128,3072]{1,0:T(8,128)(2,1)} %collective-permute-done.4.refs_1_.refs_5_), channel_id=1, source_target_pairs={{0,1},{1,0},{2,3},{3,2},{4,5},{5,4},{6,7},{7,6},{8,9},{9,8},{10,11... | collective-permute-start | bytes 2359304 | tf_op jit(solution)/shard_map/ppermute | solution.py:65
  68.1 50.5 %collective-permute-start.17 = (bf16[2,1024,512]{2,1,0:T(8,128)(2,1)}, bf16[2,1024,512]{2,1,0:T(8,128)(2,1)}, u32[]{:S(2)}, u32[]{:S(2)}) collective-permute-start(bf16[2,1024,512]{2,1,0:T(8,128)(2,1)} %param.17), channel_id=1, source_target_pairs={{0,19},{1,18},{2,17},{3,16},{4,23},{5,22},{6,21},{7,20},{8,27},{9,... | collective-permute-start | bytes 6291464 | tf_op jit(solution)/shard_map/ppermute | solution.py:65
  86.2 30.6 %collective-permute-start.21 = (bf16[384,1024]{1,0:T(8,128)(2,1)}, bf16[384,1024]{1,0:T(8,128)(2,1)}, u32[]{:S(2)}, u32[]{:S(2)}) collective-permute-start(bf16[384,1024]{1,0:T(8,128)(2,1)} %copy-done.8), channel_id=1, source_target_pairs={{0,96},{1,97},{2,98},{3,99},{4,100},{5,101},{6,102},{7,103},{8,104... | collective-permute-start | bytes 2359304 | tf_op jit(solution)/shard_map/ppermute | solution.py:65
  88.7 28.4 %collective-permute-start.24 = (bf16[384,1024]{1,0:T(8,128)(2,1)}, bf16[384,1024]{1,0:T(8,128)(2,1)}, u32[]{:S(2)}, u32[]{:S(2)}) collective-permute-start(bf16[384,1024]{1,0:T(8,128)(2,1)} %collective-permute-done.23.refs_20_), channel_id=1, source_target_pairs={{0,32},{1,33},{2,34},{3,35},{4,36},{5,37},{6,38},{7,39},{8,40},{9,... | collective-permute-start | bytes 2359304 | tf_op jit(solution)/shard_map/ppermute | solution.py:65
  88.9 36.5 %collective-permute-start.22 = (bf16[384,1024]{1,0:T(8,128)(2,1)}, bf16[384,1024]{1,0:T(8,128)(2,1)}, u32[]{:S(2)}, u32[]{:S(2)}) collective-permute-start(bf16[384,1024]{1,0:T(8,128)(2,1)} %collective-permute-done.20.refs_17_), channel_id=1, source_target_pairs={{0,32},{1,33},{2,34},{3,35},{4,36},{5,37},{6,38},{7,39},{8,40},{9,... | collective-permute-start | bytes 2359304 | tf_op jit(solution)/shard_map/ppermute | solution.py:65
  90.2 35.2 %collective-permute-start.26 = (bf16[384,1024]{1,0:T(8,128)(2,1)}, bf16[384,1024]{1,0:T(8,128)(2,1)}, u32[]{:S(2)}, u32[]{:S(2)}) collective-permute-start(bf16[384,1024]{1,0:T(8,128)(2,1)} %collective-permute-done.25.refs_22_), channel_id=1, source_target_pairs={{0,96},{1,97},{2,98},{3,99},{4,100},{5,101},{6,102},{7,103},{8,104... | collective-permute-start | bytes 2359304 | tf_op jit(solution)/shard_map/ppermute | solution.py:65
  116.8 67.1 %collective-permute-start.27 = (bf16[64,3072]{1,0:T(8,128)(2,1)}, bf16[64,3072]{1,0:T(8,128)(2,1)S(1)}, u32[]{:S(2)}, u32[]{:S(2)}) collective-permute-start(bf16[64,3072]{1,0:T(8,128)(2,1)} %param.19), channel_id=1, source_target_pairs={{0,19},{1,18},{2,17},{3,16},{4,23},{5,22},{6,21},{7,20},{8,27},{9,... | collective-permute-start | bytes 1179656 | tf_op jit(solution)/shard_map/ppermute | solution.py:65
  117.1 66.8 %collective-permute-start.30 = (bf16[512,384]{1,0:T(8,128)(2,1)S(1)}, bf16[512,384]{1,0:T(8,128)(2,1)S(1)}, u32[]{:S(2)}, u32[]{:S(2)}) collective-permute-start(bf16[512,384]{1,0:T(8,128)(2,1)S(1)} %broadcast_select_fusion.1.refs_0_), channel_id=1, source_target_pairs={{0,96},{1,97},{2,98},{3,99},{4,100},{5,101},{6,102},{7,103},{8,104... | collective-permute-start | bytes 1179656 | tf_op jit(solution)/shard_map/ppermute | solution.py:65
  118.6 65.3 %collective-permute-start.33 = (bf16[512,384]{1,0:T(8,128)(2,1)S(1)}, bf16[512,384]{1,0:T(8,128)(2,1)S(1)}, u32[]{:S(2)}, u32[]{:S(2)}) collective-permute-start(bf16[512,384]{1,0:T(8,128)(2,1)S(1)} %copy-done.16), channel_id=1, source_target_pairs={{0,32},{1,33},{2,34},{3,35},{4,36},{5,37},{6,38},{7,39},{8,40},{9,... | collective-permute-start | bytes 1179656 | tf_op jit(solution)/shard_map/ppermute | solution.py:65
  125.4 58.6 %collective-permute-start.31 = (bf16[512,384]{1,0:T(8,128)(2,1)S(1)}, bf16[512,384]{1,0:T(8,128)(2,1)S(1)}, u32[]{:S(2)}, u32[]{:S(2)}) collective-permute-start(bf16[512,384]{1,0:T(8,128)(2,1)S(1)} %copy-done.18), channel_id=1, source_target_pairs={{0,32},{1,33},{2,34},{3,35},{4,36},{5,37},{6,38},{7,39},{8,40},{9,... | collective-permute-start | bytes 1179656 | tf_op jit(solution)/shard_map/ppermute | solution.py:65
  125.4 58.6 %collective-permute-start.35 = (bf16[512,384]{1,0:T(8,128)(2,1)S(1)}, bf16[512,384]{1,0:T(8,128)(2,1)S(1)}, u32[]{:S(2)}, u32[]{:S(2)}) collective-permute-start(bf16[512,384]{1,0:T(8,128)(2,1)S(1)} %copy-done.20), channel_id=1, source_target_pairs={{0,96},{1,97},{2,98},{3,99},{4,100},{5,101},{6,102},{7,103},{8,104... | collective-permute-start | bytes 1179656 | tf_op jit(solution)/shard_map/ppermute | solution.py:65
  214.9 18.7 %collective-permute-start.39 = (bf16[128,3072]{1,0:T(8,128)(2,1)S(1)}, bf16[128,3072]{1,0:T(8,128)(2,1)S(1)}, u32[]{:S(2)}, u32[]{:S(2)}) collective-permute-start(bf16[128,3072]{1,0:T(8,128)(2,1)S(1)} %get-tuple-element.28), channel_id=1, source_target_pairs={{1,0},{0,1},{3,2},{2,3},{5,4},{4,5},{7,6},{6,7},{9,8},{8,9},{11,10... | collective-permute-start | bytes 2359304 | tf_op jit(solution)/shard_map/ppermute | solution.py:65
  215.3 20.3 %collective-permute-start.41 = (bf16[128,3072]{1,0:T(8,128)(2,1)S(1)}, bf16[128,3072]{1,0:T(8,128)(2,1)S(1)}, u32[]{:S(2)}, u32[]{:S(2)}) collective-permute-start(bf16[128,3072]{1,0:T(8,128)(2,1)S(1)} %get-tuple-element.30), channel_id=1, source_target_pairs={{1,0},{0,1},{3,2},{2,3},{5,4},{4,5},{7,6},{6,7},{9,8},{8,9},{11,10... | collective-permute-start | bytes 2359304 | tf_op jit(solution)/shard_map/ppermute | solution.py:65
  225.4 20.5 %collective-permute-start.43 = (bf16[128,3072]{1,0:T(8,128)(2,1)S(1)}, bf16[128,3072]{1,0:T(8,128)(2,1)S(1)}, u32[]{:S(2)}, u32[]{:S(2)}) collective-permute-start(bf16[128,3072]{1,0:T(8,128)(2,1)S(1)} %add_convert_fusion.2), channel_id=1, source_target_pairs={{12,0},{13,1},{14,2},{15,3},{0,4},{1,5},{2,6},{3,7},{4,8},{5,9},{6... | collective-permute-start | bytes 2359304 | tf_op jit(solution)/shard_map/ppermute | solution.py:65
  228.4 19.1 %collective-permute-start.37 = (bf16[128,3072]{1,0:T(8,128)(2,1)S(1)}, bf16[128,3072]{1,0:T(8,128)(2,1)S(1)}, u32[]{:S(2)}, u32[]{:S(2)}) collective-permute-start(bf16[128,3072]{1,0:T(8,128)(2,1)S(1)} %get-tuple-element.24), channel_id=1, source_target_pairs={{1,0},{0,1},{3,2},{2,3},{5,4},{4,5},{7,6},{6,7},{9,8},{8,9},{11,10... | collective-permute-start | bytes 2359304 | tf_op jit(solution)/shard_map/ppermute | solution.py:65
  233.8 25.1 %collective-permute-start.40 = (bf16[128,3072]{1,0:T(8,128)(2,1)S(1)}, bf16[128,3072]{1,0:T(8,128)(2,1)S(1)}, u32[]{:S(2)}, u32[]{:S(2)}) collective-permute-start(bf16[128,3072]{1,0:T(8,128)(2,1)S(1)} %add_convert_fusion.5), channel_id=1, source_target_pairs={{4,0},{5,1},{6,2},{7,3},{8,4},{9,5},{10,6},{11,7},{12,8},{13,9},{1... | collective-permute-start | bytes 2359304 | tf_op jit(solution)/shard_map/ppermute | solution.py:65
  (55 other events, 831.6 us)
where the time goes:
time: 262 us; the launch traced here: 261 us
  waiting for transfers between devices  101 us (39%)
  Pallas kernels  79.4 us (30%)
  starting transfers between devices  57.6 us (22%)
  other arithmetic  17.8 us (7%)
  local copies, waits for them, and re-layouts  4.24 us (2%)
    ppermute x45, waiting for transfers between devices, send(): return lax.ppermute(value, ALL, pairs)  96 us
    ppermute x45, starting transfers between devices, send(): return lax.ppermute(value, ALL, pairs)  45 us
    pallas_call x1, Pallas kernels, local(): pl.pallas_call(hidden_kernel, out_shape=(jax.ShapeDtypeStruct((total, uni...  39.2 us
    pallas_call x2, Pallas kernels, down_half(): pl.pallas_call(functools.partial(down_kernel, 8 * i), grid=(1,), out_shap...  24.2 us
    pallas_call x2, Pallas kernels, ranks_of(): pl.pallas_call(functools.partial(rank_kernel, first), out_shape=jax.Shape...  14.2 us
    all_to_all x1, starting transfers between devices, local(): lax.all_to_all(packed_down.reshape(16, 32, 128), GROUP, split_axis=0, con...  7.34 us
    convert_element_type x6, other arithmetic, add(): (left.astype(jnp.float32) + right.astype(jnp.float32)).astype(jnp.bfloat16)  6.46 us
    all_to_all x1, waiting for transfers between devices, local(): lax.all_to_all(packed_down.reshape(16, 32, 128), GROUP, split_axis=0, con...  5.5 us
  transfers between devices with their start and end apart: 47, of which 19 were waited for; matrix products, arithmetic and copies ran while one was open for 6% of the time, Pallas kernels for 26%

commit v1 on v0

--- a/solution.py
+++ b/solution.py
@@ -53,7 +53,7 @@
 X_DOWN = pairs_of(lambda x, c, y, z: (x - 1, c, y, z))
 
 
-HALVES = ((7, 6, 5, 4), (0, 1, 2, 3))
+HALVES = ((7, 6, 5, 4), (3, 2, 1, 0))
 ROW_BLOCKS = tuple(
     half[2 * pair + j] + 8 * part for half in HALVES for pair in range(2) for part in range(2) for j in range(2)
 )
@@ -100,6 +100,7 @@
     role_col = yi * 4 + jnp.where(ci == 0, hi * 2 + li, 3 - hi * 2 - li)
     group_at = (ci * 4 + yi) * 2 + li
     earlier = lax.broadcasted_iota(jnp.int32, (128, 128), 0) < lax.broadcasted_iota(jnp.int32, (128, 128), 1)
+    token = lax.broadcasted_iota(jnp.int32, (1, 128), 1)
     for i, k in enumerate(ROW_BLOCKS):
         part, k = k // 8, k % 8
         c = ci if part == 0 else 1 - ci
@@ -120,11 +121,11 @@
             slot,
             owner_at * 64 + block_at * 4 + (position >> 2),
             position & 3,
-            owner_at * 32 + block_at * 2 + (position >> 3),
-            position & 7,
+            block_at * 16 + (token >> 3),
+            token & 7,
             jnp.where(is_mine, slot - role_col * 4, -1),
             jnp.where(is_mine, block_at * 4 + (position >> 2), -1),
-            jnp.where(is_mine, block_at * 2 + (position >> 3), -1),
+            token,
         )
         for j, column in enumerate(columns):
             out[i, j : j + 1, :] = column
@@ -155,21 +156,21 @@
     lax.fori_loop(0, rows.shape[0] // TILE, tile, 0)
 
 
-def hidden_kernel(slab_at, ranks, ints, expand, down_shrink, to_gate, to_up, fold, *refs):
-    shards, pieces, (hidden, packed, rows, weight, total, row_sems, sem) = refs[:16], refs[16:24], refs[24:]
+def hidden_kernel(first, slab_at, ranks, ints, expand, down_shrink, to_gate, to_up, fold, *refs):
+    shards, pieces, (hidden, packed, rows, weight, row_sems, sem) = refs[:8], refs[8:16], refs[16:]
     slab = pieces[0].shape[0]
     for i, piece in enumerate(pieces):
         start = pl.multiple_of(slab_at[i] * slab, 128)
         pltpu.make_async_copy(piece, weight.at[pl.ds(start, slab)], sem.at[0]).start()
     for i, shard in enumerate(shards):
         pltpu.make_async_copy(shard, rows.at[pl.ds(i * 128, 128)], row_sems.at[i * 128 // TILE]).start()
-    total[...] = jnp.zeros(total.shape, jnp.float32)
+    packed[...] = jnp.zeros(packed.shape, jnp.float32)
     pltpu.make_async_copy(weight, weight, sem.at[0]).wait()
     units = hidden.shape[1]
 
     def tile(i, carry):
         part = pl.ds(pl.multiple_of(i * TILE, TILE), TILE)
-        down, across = places(ints, i)
+        down, across = places(ints, i, first)
         pltpu.make_async_copy(rows.at[part], rows.at[part], row_sems.at[i]).wait()
         both = dot(rows[part, :], weight[...])
         place = lanes(TILE, ranks.shape[0], 1) == down[:, 1:2]
@@ -181,34 +182,43 @@
         hidden[part, :] = values
         parts = dot(kept(chosen, contract_trailing(values, down_shrink[...])), fold[...])
         parts = kept(lanes(TILE, 128, 16) == down[:, 4:5], parts)
-        place = lax.broadcasted_iota(jnp.int32, (total.shape[0], TILE), 0) == across[3:4]
-        total[...] += dot(place.astype(jnp.bfloat16), parts)
+        place = lax.broadcasted_iota(jnp.int32, (packed.shape[0], TILE), 0) == across[3:4]
+        packed[...] += dot(place.astype(jnp.bfloat16), parts)
         return carry
 
     lax.fori_loop(0, rows.shape[0] // TILE, tile, 0)
-    packed[...] = total[...].astype(jnp.bfloat16)
-
-
-def down_kernel(first, slab_at, hidden, ranks, ints, down_expand, widen, *refs):
+
+
+def down_kernel(slab_at, hidden, *refs):
     pieces, (mine, theirs, weight, sem) = refs[:8], refs[8:]
     slab = pieces[0].shape[1]
     for i, piece in enumerate(pieces):
         start = pl.multiple_of(slab_at[i] * slab, 128)
         pltpu.make_async_copy(piece, weight.at[:, pl.ds(start, slab)], sem.at[0]).start()
     pltpu.make_async_copy(weight, weight, sem.at[0]).wait()
+    columns = weight.shape[1] // 4
+
+    def chunk(i, carry):
+        part = pl.ds(pl.multiple_of(i * columns, 128), columns)
+        both = dot(hidden[...], weight[:, part]).astype(jnp.bfloat16)
+        mine[:, part] = both[:TILE]
+        theirs[:, part] = both[TILE:]
+        return carry
+
+    lax.fori_loop(0, 4, chunk, 0)
+
+
+def adapter_kernel(ranks, ints, lane_slot, spread, *refs):
+    maps, (mine, theirs, whole, sem) = refs[:8], refs[8:]
+    for i, piece in enumerate(maps):
+        pltpu.make_async_copy(piece, whole.at[pl.ds(i * 64, 64)], sem.at[0]).start()
+    pltpu.make_async_copy(whole, whole, sem.at[0]).wait()
     for t, out in enumerate((mine, theirs)):
-
-        def tile(i, carry):
-            at = pl.ds(pl.multiple_of(i * TILE, TILE), TILE)
-            part = pl.ds(pl.multiple_of((2 * i + t) * TILE, TILE), TILE)
-            numbers, _ = places(ints, 2 * i + t, first)
-            place = lanes(TILE, ranks.shape[0], 1) == numbers[:, 7:8]
-            own = kept(lanes(TILE, 128, 16) == numbers[:, 4:5], dot(place.astype(jnp.bfloat16), ranks[...]))
-            own = kept(lanes(TILE, 64, 16) == numbers[:, 5:6], dot(own, widen[...]))
-            out[at, :] = (dot(hidden[part, :], weight[...]) + dot(own, down_expand[...])).astype(jnp.bfloat16)
-            return carry
-
-        lax.fori_loop(0, out.shape[0] // TILE, tile, 0)
+        down = ints[ROW_BLOCKS.index(8 * t)].T
+        place = lanes(128, 16, 1) == down[:, 7:8] >> 3
+        own = kept(lanes(128, 128, 16) == down[:, 4:5], dot(place.astype(jnp.bfloat16), ranks[t]))
+        own = kept(lane_slot[...] == down[:, 0:1], dot(own, spread[...]))
+        out[...] = dot(own, whole[...]).astype(jnp.bfloat16)
 
 
 def weight_blocks(shard, ci):
@@ -240,8 +250,6 @@
     owner_partial = adapter_list // 16
     rank = down_expand_maps.shape[0] // owner_partial
     total = 16 * own_count
-    adapter_range = jnp.arange(adapter_list, dtype=jnp.int32)
-    group_range = jnp.arange(16, dtype=jnp.int32)
 
     slab_at = [((xi + dx) % 4) * 2 + (ci if half == 0 else 1 - ci) for half in range(2) for dx in X_ORDER]
 
@@ -259,6 +267,20 @@
     down = weight_blocks(down_base, ci)
     down_shrink = send(down_shrink_maps, OTHER_ROLE)
     down_expand = send(down_expand_maps, OTHER_ROLE)
+
+    maps = [down_expand]
+    for k in range(7):
+        maps.append(send(maps[SOURCE[k]], TREE[k]))
+
+    def pick(table, k):
+        return jnp.where(ci == 0, table[0][k], table[1][k])
+
+    map_slots = []
+    for k in range(8):
+        from_y, from_l = (yi + pick(BLOCK_Y, k)) % 4, (li + pick(BLOCK_L, k)) % 2
+        map_slots.append((from_y * 4 + jnp.where(ci == 0, hi * 2 + from_l, 3 - hi * 2 - from_l)) * owner_partial)
+    lane_slot = jnp.stack(map_slots).astype(jnp.int32)[:, None] + jnp.arange(64, dtype=jnp.int32)[None, :] // rank
+    lane_slot = lane_slot.reshape(1, 512)
 
     half_count = total // 2
     vmem = pl.BlockSpec(memory_space=pltpu.VMEM)
@@ -297,72 +319,79 @@
     spread = jnp.broadcast_to(packed.astype(jnp.bfloat16)[None], (16, 64, 128))
     ranks = lax.all_to_all(spread, GROUP, split_axis=0, concat_axis=0, tiled=True).reshape(1024, 128)
 
-    hidden, packed_down = pl.pallas_call(
-        hidden_kernel,
-        out_shape=(jax.ShapeDtypeStruct((total, units), jnp.bfloat16), jax.ShapeDtypeStruct((512, 128), jnp.bfloat16)),
-        in_specs=[smem] + [vmem] * 7 + [stay] * 24,
-        out_specs=(vmem, vmem),
-        scratch_shapes=[
-            pltpu.VMEM((total, width), jnp.bfloat16),
-            pltpu.VMEM((width, 2 * units), jnp.bfloat16),
-            pltpu.VMEM((512, 128), jnp.float32),
-            pltpu.SemaphoreType.DMA((total // TILE,)),
-            pltpu.SemaphoreType.DMA((1,)),
-        ],
-        name="hidden",
-    )(
-        slab_at,
-        ranks,
-        ints,
-        expand,
-        down_shrink,
-        matching(128, 2 * rank, adapter_list * rank, rank),
-        matching(128, 2 * rank, adapter_list * rank, rank, rank),
-        matching(adapter_list * rank, rank, 128, rank),
-        *shards,
-        *gate_up,
-    )
-
-    arrived = lax.all_to_all(
-        packed_down.reshape(16, 32, 128), GROUP, split_axis=0, concat_axis=0, tiled=True
-    )
-    down_ranks = jnp.sum(arrived.astype(jnp.float32), axis=0).astype(jnp.bfloat16)
-
-    def down_half(i):
+    def hidden_half(i):
         return pl.pallas_call(
-            functools.partial(down_kernel, 8 * i),
+            functools.partial(hidden_kernel, 8 * i),
+            out_shape=(
+                jax.ShapeDtypeStruct((half_count, units), jnp.bfloat16),
+                jax.ShapeDtypeStruct((256, 128), jnp.float32),
+            ),
+            in_specs=[smem] + [vmem] * 7 + [stay] * 16,
+            out_specs=(vmem, vmem),
+            scratch_shapes=[
+                pltpu.VMEM((half_count, width), jnp.bfloat16),
+                pltpu.VMEM((width, 2 * units), jnp.bfloat16),
+                pltpu.SemaphoreType.DMA((half_count // TILE,)),
+                pltpu.SemaphoreType.DMA((1,)),
+            ],
+            name="hidden",
+        )(
+            slab_at,
+            ranks,
+            ints,
+            expand,
+            down_shrink,
+            matching(128, 2 * rank, adapter_list * rank, rank),
+            matching(128, 2 * rank, adapter_list * rank, rank, rank),
+            matching(adapter_list * rank, rank, 128, rank),
+            *shards[8 * i : 8 * i + 8],
+            *gate_up,
+        )
+
+    def down_quarter(hidden, i):
+        return pl.pallas_call(
+            down_kernel,
             grid=(1,),
-            out_shape=(jax.ShapeDtypeStruct((half_count // 2, width), jnp.bfloat16),) * 2,
-            in_specs=[smem, pl.BlockSpec((half_count, units), lambda g: (i, 0))] + [vmem] * 4 + [stay] * 8,
+            out_shape=(jax.ShapeDtypeStruct((TILE, width), jnp.bfloat16),) * 2,
+            in_specs=[smem, pl.BlockSpec((2 * TILE, units), lambda g: (i, 0))] + [stay] * 8,
             out_specs=(vmem, vmem),
             scratch_shapes=[pltpu.VMEM((units, width), jnp.bfloat16), pltpu.SemaphoreType.DMA((1,))],
             name="down",
-        )(
-            slab_at,
-            hidden,
-            down_ranks,
-            ints,
-            down_expand,
-            matching(128, rank, owner_partial * rank, rank),
-            *down,
-        )
+        )(slab_at, hidden, *down)
 
     def add(left, right):
         return (left.astype(jnp.float32) + right.astype(jnp.float32)).astype(jnp.bfloat16)
 
     sums = [None] * 8
+    packed_down = []
     for i in range(2):
-        mine_part, theirs_part = down_half(i)
-        swapped = send(theirs_part, CORE)
-        added = [
-            add(mine_part[j * own_count : (j + 1) * own_count], swapped[j * own_count : (j + 1) * own_count])
-            for j in range(4)
-        ]
-        for k, value in zip(HALVES[i], lax.optimization_barrier(added)):
-            sums[k] = value
-    for k in (6, 5, 4, 3, 2, 1, 0):
+        hidden, packed = hidden_half(i)
+        packed_down.append(packed)
+        for j in range(2):
+            mine_part, theirs_part = down_quarter(hidden, j)
+            swapped = send(theirs_part, CORE)
+            added = [add(mine_part[at : at + 128], swapped[at : at + 128]) for at in (0, 128)]
+            for k, value in zip(HALVES[i][2 * j : 2 * j + 2], lax.optimization_barrier(added)):
+                sums[k] = value
+
+    packed_down = (packed_down[0] + packed_down[1]).astype(jnp.bfloat16).reshape(16, 16, 128)
+    arrived = lax.all_to_all(packed_down, GROUP, split_axis=0, concat_axis=0, tiled=True)
+    down_ranks = jnp.sum(arrived.astype(jnp.float32), axis=0).astype(jnp.bfloat16)
+    both_ranks = jnp.stack([down_ranks, send(down_ranks, CORE)])
+    own_adapter, their_adapter = pl.pallas_call(
+        adapter_kernel,
+        out_shape=(jax.ShapeDtypeStruct((own_count, width), jnp.bfloat16),) * 2,
+        in_specs=[vmem] * 4 + [stay] * 8,
+        out_specs=(vmem, vmem),
+        scratch_shapes=[pltpu.VMEM((512, width), jnp.bfloat16), pltpu.SemaphoreType.DMA((1,))],
+        name="adapters",
+    )(both_ranks, ints, lane_slot, matching(128, rank, 512, rank), *maps)
+    adapter_term = own_adapter.astype(jnp.float32) + send(their_adapter, CORE).astype(jnp.float32)
+
+    for k in (6, 5, 4, 3, 2, 1):
         sums[SOURCE[k]] = add(sums[SOURCE[k]], send(sums[k + 1], TREE_BACK[k]))
-    return sums[0]
+    last = send(sums[1], TREE_BACK[0]).astype(jnp.float32)
+    return (sums[0].astype(jnp.float32) + last + adapter_term).astype(jnp.bfloat16)
 
 
 def solution(mesh):

time: 262 us -> 303 us (1.16)
  starting transfers between devices: 57.6 us -> 72.3 us
  Pallas kernels: 79.4 us -> 92.8 us
  waiting for transfers between devices: 101 us -> 106 us
  other arithmetic: 17.8 us -> 21.8 us
  local copies, waits for them, and re-layouts: 4.24 us -> 8.1 us
    ppermute x45 -> x56, starting transfers between devices: 45 us -> 59.5 us  [send(): return lax.ppermute(value, ALL, pairs)]
    pallas_call x3 -> x7, Pallas kernels: 63.4 us -> 76.9 us  [the longest x2 44 us: hidden_half(): pl.pallas_call(functools.partial(hidden_kernel, 8 * i), out_shape=(jax.Sh...]
    all_to_all x1, waiting for transfers between devices: 0.01 us -> 5.47 us  [local(): lax.all_to_all(spread, GROUP, split_axis=0, concat_axis=0, tiled=True)]
    convert_element_type x0 -> x2, other arithmetic: none -> 3.17 us  [the longest x1 1.63 us: local(): (sums[0].astype(jnp.float32) + last + adapter_term).astype(jnp.bfloat16)]
    ppermute x45 -> x56, waiting for transfers between devices: 96 us -> 97.4 us  [send(): return lax.ppermute(value, ALL, pairs)]
    convert_element_type x6 -> x7, other arithmetic: 6.46 us -> 7.28 us  [add(): (left.astype(jnp.float32) + right.astype(jnp.float32)).astype(jnp.bfloat16)]
  transfers between devices with their start and end apart: 47 -> 58, of which waited for: 19 -> 19; matrix products, arithmetic and copies ran while one was open for 6% -> 8% of each run, Pallas kernels for 26% -> 31%
where the time goes in v1:
time: 303 us; the launch traced here: 302 us
  waiting for transfers between devices  106 us (35%)
  Pallas kernels  92.8 us (31%)
  starting transfers between devices  72.3 us (24%)
  other arithmetic  21.8 us (7%)
  local copies, waits for them, and re-layouts  8.1 us (3%)
    ppermute x56, waiting for transfers between devices, send(): return lax.ppermute(value, ALL, pairs)  97.4 us
    ppermute x56, starting transfers between devices, send(): return lax.ppermute(value, ALL, pairs)  59.5 us
    pallas_call x2, Pallas kernels, hidden_half(): pl.pallas_call(functools.partial(hidden_kernel, 8 * i), out_shape=(jax.Sh...  44 us
    pallas_call x4, Pallas kernels, down_quarter(): pl.pallas_call(down_kernel, grid=(1,), out_shape=(jax.ShapeDtypeStruct((T...  27.5 us
    pallas_call x2, Pallas kernels, ranks_of(): pl.pallas_call(functools.partial(rank_kernel, first), out_shape=jax.Shape...  14.1 us
    all_to_all x1, starting transfers between devices, local(): lax.all_to_all(spread, GROUP, split_axis=0, concat_axis=0, tiled=True)  7.78 us
    convert_element_type x7, other arithmetic, add(): (left.astype(jnp.float32) + right.astype(jnp.float32)).astype(jnp.bfloat16)  7.28 us
  transfers between devices with their start and end apart: 58, of which 19 were waited for; matrix products, arithmetic and copies ran while one was open for 8% of the time, Pallas kernels for 31%

profile of v1, /device:TPU:1, one launch (start us, length us, event | category | flops | bytes accessed | tf_op | source)
XLA Modules:
  0.0 301.6 jit_solution(13399095556283948446)
XLA Ops:
  14.4 6.0 %collective-permute-done.27 = bf16[512,384]{1,0:T(8,128)(2,1)S(1)} collective-permute-done((bf16[512,384]{1,0:T(8,128)(2,1)S(1)}, bf16[512,384]{1,0:T(8,128)(2,1)S(1)}, u32[]{:S(2)}, u32[]{:S(2)}) %collective-permute-start.27) | collective-permute-done | bytes 393248 | tf_op jit(solution)/shard_map/ppermute | solution.py:65
  31.1 5.1 %collective-permute-done.8.refs_5_.refs_1_ = bf16[128,3072]{1,0:T(8,128)(2,1)} collective-permute-done((bf16[128,3072]{1,0:T(8,128)(2,1)S(1)}, bf16[128,3072]{1,0:T(8,128)(2,1)}, u32[]{:S(2)}, u32[]{:S(2)}) %collective-permute-start.8) | collective-permute-done | bytes 786464 | tf_op jit(solution)/shard_map/ppermute | solution.py:65
  39.0 6.8 %collective-permute-done.19 = bf16[384,1024]{1,0:T(8,128)(2,1)} collective-permute-done((bf16[384,1024]{1,0:T(8,128)(2,1)}, bf16[384,1024]{1,0:T(8,128)(2,1)}, u32[]{:S(2)}, u32[]{:S(2)}) %collective-permute-start.19) | collective-permute-done | bytes 786464 | tf_op jit(solution)/shard_map/ppermute | solution.py:65
  50.2 8.4 %collective-permute-done.18.down_shrink = bf16[1024,512]{1,0:T(8,128)(2,1)S(1)} collective-permute-done((bf16[1024,512]{1,0:T(8,128)(2,1)}, bf16[1024,512]{1,0:T(8,128)(2,1)S(1)}, u32[]{:S(2)}, u32[]{:S(2)}) %collective-permute-start.18) | collective-permute-done | bytes 1048608 | tf_op jit(solution)/shard_map/ppermute | solution.py:65
  70.3 7.3 %collective-permute-done.14.refs_1_ = bf16[128,3072]{1,0:T(8,128)(2,1)} collective-permute-done((bf16[128,3072]{1,0:T(8,128)(2,1)}, bf16[128,3072]{1,0:T(8,128)(2,1)}, u32[]{:S(2)}, u32[]{:S(2)}) %collective-permute-start.14) | collective-permute-done | bytes 786464 | tf_op jit(solution)/shard_map/ppermute | solution.py:65
  77.6 5.7 %collective-permute-done.20.refs_9_ = bf16[384,1024]{1,0:T(8,128)(2,1)S(1)} collective-permute-done((bf16[384,1024]{1,0:T(8,128)(2,1)S(1)}, bf16[384,1024]{1,0:T(8,128)(2,1)S(1)}, u32[]{:S(2)}, u32[]{:S(2)}) %collective-permute-start.20) | collective-permute-done | bytes 786464 | tf_op jit(solution)/shard_map/ppermute | solution.py:65
  96.5 9.1 %ranks.2 = f32[64,128]{1,0:T(8,128)} custom-call(bf16[128,3072]{1,0:T(8,128)(2,1)} %copy-done.18, s32[16,8,128]{2,1,0:T(8,128)} %places.1.ints, bf16[128,128]{1,0:T(8,128)(2,1)} %compare_convert_fusion.4.fold, bf16[128,3072]{1,0:T(8,128)(2,1)} %collective-permute-done.3.refs_0_.refs_4_, bf16[128,3072]{1,0:T(8,128)(2,1)} %collective-permute-done.4.refs_1_.refs_5_, ...), custom_call_target="tpu_custom_call" | custom-call | tf_op jit(solution)/shard_map/ranks/pallas_call | solution.py:306
  105.6 5.0 %ranks.3 = f32[64,128]{1,0:T(8,128)} custom-call(bf16[128,3072]{1,0:T(8,128)(2,1)} %copy-done.18, s32[16,8,128]{2,1,0:T(8,128)} %places.1.ints, bf16[128,128]{1,0:T(8,128)(2,1)} %compare_convert_fusion.4.fold, bf16[128,3072]{1,0:T(8,128)(2,1)} %collective-permute-done.13.refs_0_, bf16[128,3072]{1,0:T(8,128)(2,1)} %collective-permute-done.14.refs_1_, ...), custom_call_target="tpu_custom_call" | custom-call | tf_op jit(solution)/shard_map/ranks/pallas_call | solution.py:306
  112.3 14.5 %collective-permute-done.22.refs_11_ = bf16[384,1024]{1,0:T(8,128)(2,1)} collective-permute-done((bf16[384,1024]{1,0:T(8,128)(2,1)}, bf16[384,1024]{1,0:T(8,128)(2,1)}, u32[]{:S(2)}, u32[]{:S(2)}) %collective-permute-start.22) | collective-permute-done | bytes 786464 | tf_op jit(solution)/shard_map/ppermute | solution.py:65
  128.3 7.8 %all-to-all-start = ((bf16[16,64,128]{2,1,0:T(8,128)(2,1)}), bf16[16,64,128]{2,1,0:T(8,128)(2,1)S(1)}, u32[]{:S(2)}, u32[]{:S(2)}) async-start(bf16[16,64,128]{2,1,0:T(8,128)(2,1)} %broadcast_in_dim.2), calls=%async_computation | async-start | bytes 524288 | tf_op jit(solution)/shard_map/all_to_all | solution.py:320
  137.8 5.5 %all-to-all-done = bf16[16,64,128]{2,1,0:T(8,128)(2,1)S(1)} async-done(((bf16[16,64,128]{2,1,0:T(8,128)(2,1)}), bf16[16,64,128]{2,1,0:T(8,128)(2,1)S(1)}, u32[]{:S(2)}, u32[]{:S(2)}) %all-to-all-start) | async-done | bytes 262176 | tf_op jit(solution)/shard_map/all_to_all | solution.py:320
  144.0 22.0 %hidden.3 = (bf16[1024,512]{1,0:T(8,128)(2,1)}, f32[256,128]{1,0:T(8,128)}) custom-call(s32[8]{0:T(128)} %stack.86.slab_at, bf16[1024,128]{1,0:T(8,128)(2,1)} %bitcast.25, s32[16,8,128]{2,1,0:T(8,128)} %places.1.ints, bf16[2,1024,512]{2,1,0:T(8,128)(2,1)} %copy-done.1, bf16[1024,512]{1,0:T(8,128)(2,1)} %copy-done.9, ...), custom_call_target="tpu_custom_call" | custom-call | tf_op jit(solution)/shard_map/hidden/pallas_call | solution.py:323
  166.9 6.9 %down.6 = (bf16[256,3072]{1,0:T(8,128)(2,1)}, bf16[256,3072]{1,0:T(8,128)(2,1)}) custom-call(s32[8]{0:T(128)} %stack.86.slab_at, bf16[1024,512]{1,0:T(8,128)(2,1)} %get-tuple-element.35.hidden, bf16[512,384]{1,0:T(8,128)(2,1)} %copy-done, bf16[512,384]{1,0:T(8,128)(2,1)} %copy-done.5, bf16[512,384]{1,0:T(8,128)(2,1)} %copy-done.7, ...), custom_call_target="tpu_custom_call" | custom-call | tf_op jit(solution)/shard_map/down/pallas_call | solution.py:352
  177.9 5.8 %collective-permute-done.48.refs_1_ = bf16[64,3072]{1,0:T(8,128)(2,1)S(1)} collective-permute-done((bf16[64,3072]{1,0:T(8,128)(2,1)}, bf16[64,3072]{1,0:T(8,128)(2,1)S(1)}, u32[]{:S(2)}, u32[]{:S(2)}) %collective-permute-start.48) | collective-permute-done | bytes 393248 | tf_op jit(solution)/shard_map/ppermute | solution.py:65
  186.4 6.9 %down.7 = (bf16[256,3072]{1,0:T(8,128)(2,1)}, bf16[256,3072]{1,0:T(8,128)(2,1)}) custom-call(s32[8]{0:T(128)} %stack.86.slab_at, bf16[1024,512]{1,0:T(8,128)(2,1)} %get-tuple-element.35.hidden, bf16[512,384]{1,0:T(8,128)(2,1)} %copy-done, bf16[512,384]{1,0:T(8,128)(2,1)} %copy-done.5, bf16[512,384]{1,0:T(8,128)(2,1)} %copy-done.7, ...), custom_call_target="tpu_custom_call" | custom-call | tf_op jit(solution)/shard_map/down/pallas_call | solution.py:352
  195.5 22.0 %hidden.2 = (bf16[1024,512]{1,0:T(8,128)(2,1)}, f32[256,128]{1,0:T(8,128)}) custom-call(s32[8]{0:T(128)} %stack.86.slab_at, bf16[1024,128]{1,0:T(8,128)(2,1)} %bitcast.26, s32[16,8,128]{2,1,0:T(8,128)} %places.1.ints, bf16[2,1024,512]{2,1,0:T(8,128)(2,1)} %copy-done.1, bf16[1024,512]{1,0:T(8,128)(2,1)} %copy-done.9, ...), custom_call_target="tpu_custom_call" | custom-call | tf_op jit(solution)/shard_map/hidden/pallas_call | solution.py:323
  219.1 5.0 %all-to-all-start.1 = ((bf16[16,16,128]{2,1,0:T(8,128)(2,1)}), bf16[16,16,128]{2,1,0:T(8,128)(2,1)}, u32[]{:S(2)}, u32[]{:S(2)}) async-start(bf16[16,16,128]{2,1,0:T(8,128)(2,1)} %bitcast.14), calls=%async_computation.1 | async-start | bytes 131072 | tf_op jit(solution)/shard_map/all_to_all | solution.py:378
  232.5 6.9 %down.4 = (bf16[256,3072]{1,0:T(8,128)(2,1)}, bf16[256,3072]{1,0:T(8,128)(2,1)}) custom-call(s32[8]{0:T(128)} %stack.86.slab_at, bf16[1024,512]{1,0:T(8,128)(2,1)} %get-tuple-element.27.hidden, bf16[512,384]{1,0:T(8,128)(2,1)} %copy-done, bf16[512,384]{1,0:T(8,128)(2,1)} %copy-done.5, bf16[512,384]{1,0:T(8,128)(2,1)} %copy-done.7, ...), custom_call_target="tpu_custom_call" | custom-call | tf_op jit(solution)/shard_map/down/pallas_call | solution.py:352
  239.4 6.8 %down.5 = (bf16[256,3072]{1,0:T(8,128)(2,1)}, bf16[256,3072]{1,0:T(8,128)(2,1)}) custom-call(s32[8]{0:T(128)} %stack.86.slab_at, bf16[1024,512]{1,0:T(8,128)(2,1)} %get-tuple-element.27.hidden, bf16[512,384]{1,0:T(8,128)(2,1)} %copy-done, bf16[512,384]{1,0:T(8,128)(2,1)} %copy-done.5, bf16[512,384]{1,0:T(8,128)(2,1)} %copy-done.7, ...), custom_call_target="tpu_custom_call" | custom-call | tf_op jit(solution)/shard_map/down/pallas_call | solution.py:352
  248.2 5.4 %adapters.1 = (bf16[128,3072]{1,0:T(8,128)(2,1)}, bf16[128,3072]{1,0:T(8,128)(2,1)}) custom-call(bf16[2,16,128]{2,1,0:T(8,128)(2,1)} %pad_maximum_fusion.ranks, s32[16,8,128]{2,1,0:T(8,128)} %places.1.ints, s32[1,512]{1,0:T(1,128)} %add.462.lane_slot, bf16[128,512]{1,0:T(8,128)(2,1)} %compare_convert_fusion.3.spread, ...), custom_call_target="tpu_custom_call" | custom-call | tf_op jit(solution)/shard_map/adapters/pallas_call | solution.py:381
  276.0 6.5 %collective-permute-done.44 = bf16[128,3072]{1,0:T(8,128)(2,1)S(1)} collective-permute-done((bf16[128,3072]{1,0:T(8,128)(2,1)S(1)}, bf16[128,3072]{1,0:T(8,128)(2,1)S(1)}, u32[]{:S(2)}, u32[]{:S(2)}) %collective-permute-start.44) | collective-permute-done | bytes 786464 | tf_op jit(solution)/shard_map/ppermute | solution.py:65
  283.2 4.9 %collective-permute-done.37 = bf16[128,3072]{1,0:T(8,128)(2,1)S(1)} collective-permute-done((bf16[128,3072]{1,0:T(8,128)(2,1)S(1)}, bf16[128,3072]{1,0:T(8,128)(2,1)S(1)}, u32[]{:S(2)}, u32[]{:S(2)}) %collective-permute-start.37) | collective-permute-done | bytes 786464 | tf_op jit(solution)/shard_map/ppermute | solution.py:65
  288.1 6.6 %collective-permute-done.40 = bf16[128,3072]{1,0:T(8,128)(2,1)S(1)} collective-permute-done((bf16[128,3072]{1,0:T(8,128)(2,1)S(1)}, bf16[128,3072]{1,0:T(8,128)(2,1)S(1)}, u32[]{:S(2)}, u32[]{:S(2)}) %collective-permute-start.40) | collective-permute-done | bytes 786464 | tf_op jit(solution)/shard_map/ppermute | solution.py:65
  294.7 5.3 %collective-permute-done.45 = bf16[128,3072]{1,0:T(8,128)(2,1)S(1)} collective-permute-done((bf16[128,3072]{1,0:T(8,128)(2,1)S(1)}, bf16[128,3072]{1,0:T(8,128)(2,1)S(1)}, u32[]{:S(2)}, u32[]{:S(2)}) %collective-permute-start.45) | collective-permute-done | bytes 786464 | tf_op jit(solution)/shard_map/ppermute | solution.py:65
  (213 shorter events, 108.7 us)
Async XLA Ops:
  0.0 24.8 %collective-permute-start = (bf16[128,3072]{1,0:T(8,128)(2,1)}, bf16[128,3072]{1,0:T(8,128)(2,1)S(1)}, u32[]{:S(2)}, u32[]{:S(2)}) collective-permute-start(bf16[128,3072]{1,0:T(8,128)(2,1)} %param.16), channel_id=1, source_target_pairs={{0,19},{1,18},{2,17},{3,16},{4,23},{5,22},{6,21},{7,20},{8,27},{9,... | collective-permute-start | bytes 2359304 | tf_op jit(solution)/shard_map/ppermute | solution.py:65
  4.3 24.9 %collective-permute-start.2 = (bf16[128,3072]{1,0:T(8,128)(2,1)S(1)}, bf16[128,3072]{1,0:T(8,128)(2,1)S(1)}, u32[]{:S(2)}, u32[]{:S(2)}) collective-permute-start(bf16[128,3072]{1,0:T(8,128)(2,1)S(1)} %fusion.2.refs_9_.refs_5_), channel_id=1, source_target_pairs={{0,12},{1,13},{2,14},{3,15},{4,0},{5,1},{6,2},{7,3},{8,4},{9,5},{1... | collective-permute-start | bytes 2359304 | tf_op jit(solution)/shard_map/ppermute | solution.py:65
  24.8 21.0 %collective-permute-start.19 = (bf16[384,1024]{1,0:T(8,128)(2,1)}, bf16[384,1024]{1,0:T(8,128)(2,1)}, u32[]{:S(2)}, u32[]{:S(2)}) collective-permute-start(bf16[384,1024]{1,0:T(8,128)(2,1)} %constant_dynamic-update-slice_fusion), channel_id=1, source_target_pairs={{16,19},{17,18},{18,17},{19,16},{20,23},{21,22},{22,21},{23,20},{2... | collective-permute-start | bytes 2359304 | tf_op jit(solution)/shard_map/ppermute | solution.py:65
  30.0 28.6 %collective-permute-start.18 = (bf16[1024,512]{1,0:T(8,128)(2,1)}, bf16[1024,512]{1,0:T(8,128)(2,1)S(1)}, u32[]{:S(2)}, u32[]{:S(2)}) collective-permute-start(bf16[1024,512]{1,0:T(8,128)(2,1)} %param.18), channel_id=1, source_target_pairs={{0,19},{1,18},{2,17},{3,16},{4,23},{5,22},{6,21},{7,20},{8,27},{9,... | collective-permute-start | bytes 3145736 | tf_op jit(solution)/shard_map/ppermute | solution.py:65
  66.0 20.0 %collective-permute-start.25 = (bf16[384,1024]{1,0:T(8,128)(2,1)S(1)}, bf16[384,1024]{1,0:T(8,128)(2,1)S(1)}, u32[]{:S(2)}, u32[]{:S(2)}) collective-permute-start(bf16[384,1024]{1,0:T(8,128)(2,1)S(1)} %copy-done.11), channel_id=1, source_target_pairs={{0,96},{1,97},{2,98},{3,99},{4,100},{5,101},{6,102},{7,103},{8,104... | collective-permute-start | bytes 2359304 | tf_op jit(solution)/shard_map/ppermute | solution.py:65
  67.5 44.7 %collective-permute-start.17 = (bf16[2,1024,512]{2,1,0:T(8,128)(2,1)}, bf16[2,1024,512]{2,1,0:T(8,128)(2,1)S(1)}, u32[]{:S(2)}, u32[]{:S(2)}) collective-permute-start(bf16[2,1024,512]{2,1,0:T(8,128)(2,1)} %param.17), channel_id=1, source_target_pairs={{0,19},{1,18},{2,17},{3,16},{4,23},{5,22},{6,21},{7,20},{8,27},{9,... | collective-permute-start | bytes 6291464 | tf_op jit(solution)/shard_map/ppermute | solution.py:65
  87.8 22.9 %collective-permute-start.21 = (bf16[384,1024]{1,0:T(8,128)(2,1)S(1)}, bf16[384,1024]{1,0:T(8,128)(2,1)}, u32[]{:S(2)}, u32[]{:S(2)}) collective-permute-start(bf16[384,1024]{1,0:T(8,128)(2,1)S(1)} %broadcast_select_fusion.refs_8_), channel_id=1, source_target_pairs={{0,96},{1,97},{2,98},{3,99},{4,100},{5,101},{6,102},{7,103},{8,104... | collective-permute-start | bytes 2359304 | tf_op jit(solution)/shard_map/ppermute | solution.py:65
  89.7 22.5 %collective-permute-start.24 = (bf16[384,1024]{1,0:T(8,128)(2,1)}, bf16[384,1024]{1,0:T(8,128)(2,1)}, u32[]{:S(2)}, u32[]{:S(2)}) collective-permute-start(bf16[384,1024]{1,0:T(8,128)(2,1)} %copy-done.10), channel_id=1, source_target_pairs={{0,32},{1,33},{2,34},{3,35},{4,36},{5,37},{6,38},{7,39},{8,40},{9,... | collective-permute-start | bytes 2359304 | tf_op jit(solution)/shard_map/ppermute | solution.py:65
  89.7 37.1 %collective-permute-start.22 = (bf16[384,1024]{1,0:T(8,128)(2,1)}, bf16[384,1024]{1,0:T(8,128)(2,1)}, u32[]{:S(2)}, u32[]{:S(2)}) collective-permute-start(bf16[384,1024]{1,0:T(8,128)(2,1)} %copy-done.12), channel_id=1, source_target_pairs={{0,32},{1,33},{2,34},{3,35},{4,36},{5,37},{6,38},{7,39},{8,40},{9,... | collective-permute-start | bytes 2359304 | tf_op jit(solution)/shard_map/ppermute | solution.py:65
  90.4 46.4 %collective-permute-start.26 = (bf16[384,1024]{1,0:T(8,128)(2,1)}, bf16[384,1024]{1,0:T(8,128)(2,1)}, u32[]{:S(2)}, u32[]{:S(2)}) collective-permute-start(bf16[384,1024]{1,0:T(8,128)(2,1)} %copy-done.13), channel_id=1, source_target_pairs={{0,96},{1,97},{2,98},{3,99},{4,100},{5,101},{6,102},{7,103},{8,104... | collective-permute-start | bytes 2359304 | tf_op jit(solution)/shard_map/ppermute | solution.py:65
  110.7 55.3 %collective-permute-start.29 = (bf16[512,384]{1,0:T(8,128)(2,1)S(1)}, bf16[512,384]{1,0:T(8,128)(2,1)S(1)}, u32[]{:S(2)}, u32[]{:S(2)}) collective-permute-start(bf16[512,384]{1,0:T(8,128)(2,1)S(1)} %broadcast_select_fusion.1.refs_0_), channel_id=1, source_target_pairs={{0,96},{1,97},{2,98},{3,99},{4,100},{5,101},{6,102},{7,103},{8,104... | collective-permute-start | bytes 1179656 | tf_op jit(solution)/shard_map/ppermute | solution.py:65
  112.2 53.8 %collective-permute-start.32 = (bf16[512,384]{1,0:T(8,128)(2,1)}, bf16[512,384]{1,0:T(8,128)(2,1)S(1)}, u32[]{:S(2)}, u32[]{:S(2)}) collective-permute-start(bf16[512,384]{1,0:T(8,128)(2,1)} %copy-done.4), channel_id=1, source_target_pairs={{0,32},{1,33},{2,34},{3,35},{4,36},{5,37},{6,38},{7,39},{8,40},{9,... | collective-permute-start | bytes 1179656 | tf_op jit(solution)/shard_map/ppermute | solution.py:65
  112.2 53.8 %collective-permute-start.30 = (bf16[512,384]{1,0:T(8,128)(2,1)}, bf16[512,384]{1,0:T(8,128)(2,1)}, u32[]{:S(2)}, u32[]{:S(2)}) collective-permute-start(bf16[512,384]{1,0:T(8,128)(2,1)} %copy-done.5), channel_id=1, source_target_pairs={{0,32},{1,33},{2,34},{3,35},{4,36},{5,37},{6,38},{7,39},{8,40},{9,... | collective-permute-start | bytes 1179656 | tf_op jit(solution)/shard_map/ppermute | solution.py:65
  126.8 39.3 %collective-permute-start.34 = (bf16[512,384]{1,0:T(8,128)(2,1)}, bf16[512,384]{1,0:T(8,128)(2,1)}, u32[]{:S(2)}, u32[]{:S(2)}) collective-permute-start(bf16[512,384]{1,0:T(8,128)(2,1)} %copy-done.6), channel_id=1, source_target_pairs={{0,96},{1,97},{2,98},{3,99},{4,100},{5,101},{6,102},{7,103},{8,104... | collective-permute-start | bytes 1179656 | tf_op jit(solution)/shard_map/ppermute | solution.py:65
  136.8 38.2 %collective-permute-start.47 = (bf16[64,3072]{1,0:T(8,128)(2,1)}, bf16[64,3072]{1,0:T(8,128)(2,1)}, u32[]{:S(2)}, u32[]{:S(2)}) collective-permute-start(bf16[64,3072]{1,0:T(8,128)(2,1)} %param.19), channel_id=1, source_target_pairs={{0,19},{1,18},{2,17},{3,16},{4,23},{5,22},{6,21},{7,20},{8,27},{9,... | collective-permute-start | bytes 1179656 | tf_op jit(solution)/shard_map/ppermute | solution.py:65
  173.8 80.0 %collective-permute-start.38 = (bf16[256,3072]{1,0:T(8,128)(2,1)}, bf16[256,3072]{1,0:T(8,128)(2,1)S(1)}, u32[]{:S(2)}, u32[]{:S(2)}) collective-permute-start(bf16[256,3072]{1,0:T(8,128)(2,1)} %get-tuple-element.37), channel_id=1, source_target_pairs={{0,16},{1,17},{2,18},{3,19},{4,20},{5,21},{6,22},{7,23},{8,24},{9,... | collective-permute-start | bytes 4718600 | tf_op jit(solution)/shard_map/ppermute | solution.py:65
  175.5 48.6 %collective-permute-start.50 = (bf16[64,3072]{1,0:T(8,128)(2,1)}, bf16[64,3072]{1,0:T(8,128)(2,1)S(1)}, u32[]{:S(2)}, u32[]{:S(2)}) collective-permute-start(bf16[64,3072]{1,0:T(8,128)(2,1)} %collective-permute-done.47.refs_0_), channel_id=1, source_target_pairs={{0,1},{1,0},{2,3},{3,2},{4,5},{5,4},{6,7},{7,6},{8,9},{9,8},{10,11... | collective-permute-start | bytes 1179656 | tf_op jit(solution)/shard_map/ppermute | solution.py:65
  183.7 41.9 %collective-permute-start.51 = (bf16[64,3072]{1,0:T(8,128)(2,1)S(1)}, bf16[64,3072]{1,0:T(8,128)(2,1)}, u32[]{:S(2)}, u32[]{:S(2)}) collective-permute-start(bf16[64,3072]{1,0:T(8,128)(2,1)S(1)} %collective-permute-done.48.refs_1_), channel_id=1, source_target_pairs={{0,12},{1,13},{2,14},{3,15},{4,0},{5,1},{6,2},{7,3},{8,4},{9,5},{1... | collective-permute-start | bytes 1179656 | tf_op jit(solution)/shard_map/ppermute | solution.py:65
  184.0 46.8 %collective-permute-start.52 = (bf16[64,3072]{1,0:T(8,128)(2,1)S(1)}, bf16[64,3072]{1,0:T(8,128)(2,1)S(1)}, u32[]{:S(2)}, u32[]{:S(2)}) collective-permute-start(bf16[64,3072]{1,0:T(8,128)(2,1)S(1)} %collective-permute-done.48.refs_1_), channel_id=1, source_target_pairs={{0,1},{1,0},{2,3},{3,2},{4,5},{5,4},{6,7},{7,6},{8,9},{9,8},{10,11... | collective-permute-start | bytes 1179656 | tf_op jit(solution)/shard_map/ppermute | solution.py:65
  193.3 62.0 %collective-permute-start.41 = (bf16[256,3072]{1,0:T(8,128)(2,1)}, bf16[256,3072]{1,0:T(8,128)(2,1)}, u32[]{:S(2)}, u32[]{:S(2)}) collective-permute-start(bf16[256,3072]{1,0:T(8,128)(2,1)} %get-tuple-element.41), channel_id=1, source_target_pairs={{0,16},{1,17},{2,18},{3,19},{4,20},{5,21},{6,22},{7,23},{8,24},{9,... | collective-permute-start | bytes 4718600 | tf_op jit(solution)/shard_map/ppermute | solution.py:65
  224.2 22.8 %collective-permute-start.53 = (bf16[64,3072]{1,0:T(8,128)(2,1)S(1)}, bf16[64,3072]{1,0:T(8,128)(2,1)S(1)}, u32[]{:S(2)}, u32[]{:S(2)}) collective-permute-start(bf16[64,3072]{1,0:T(8,128)(2,1)S(1)} %collective-permute-done.49.refs_2_), channel_id=1, source_target_pairs={{0,1},{1,0},{2,3},{3,2},{4,5},{5,4},{6,7},{7,6},{8,9},{9,8},{10,11... | collective-permute-start | bytes 1179656 | tf_op jit(solution)/shard_map/ppermute | solution.py:65
  225.6 22.7 %collective-permute-start.54 = (bf16[64,3072]{1,0:T(8,128)(2,1)}, bf16[64,3072]{1,0:T(8,128)(2,1)}, u32[]{:S(2)}, u32[]{:S(2)}) collective-permute-start(bf16[64,3072]{1,0:T(8,128)(2,1)} %collective-permute-done.51.refs_4_), channel_id=1, source_target_pairs={{0,1},{1,0},{2,3},{3,2},{4,5},{5,4},{6,7},{7,6},{8,9},{9,8},{10,11... | collective-permute-start | bytes 1179656 | tf_op jit(solution)/shard_map/ppermute | solution.py:65
  253.6 29.6 %collective-permute-start.55 = (bf16[128,3072]{1,0:T(8,128)(2,1)}, bf16[128,3072]{1,0:T(8,128)(2,1)S(1)}, u32[]{:S(2)}, u32[]{:S(2)}) collective-permute-start(bf16[128,3072]{1,0:T(8,128)(2,1)} %get-tuple-element.48), channel_id=1, source_target_pairs={{0,16},{1,17},{2,18},{3,19},{4,20},{5,21},{6,22},{7,23},{8,24},{9,... | collective-permute-start | bytes 2359304 | tf_op jit(solution)/shard_map/ppermute | solution.py:65
  274.3 20.4 %collective-permute-start.40 = (bf16[128,3072]{1,0:T(8,128)(2,1)S(1)}, bf16[128,3072]{1,0:T(8,128)(2,1)S(1)}, u32[]{:S(2)}, u32[]{:S(2)}) collective-permute-start(bf16[128,3072]{1,0:T(8,128)(2,1)S(1)} %add_convert_fusion.7), channel_id=1, source_target_pairs={{4,0},{5,1},{6,2},{7,3},{8,4},{9,5},{10,6},{11,7},{12,8},{13,9},{1... | collective-permute-start | bytes 2359304 | tf_op jit(solution)/shard_map/ppermute | solution.py:65
  (72 other events, 1129.1 us)

commit v2 on v1

--- a/solution.py
+++ b/solution.py
@@ -131,16 +131,23 @@
             out[i, j : j + 1, :] = column
 
 
+def matching(row_count, row_period, column_count, column_period, shift=0):
+    row = lax.broadcasted_iota(jnp.int32, (row_count, column_count), 0) & (row_period - 1)
+    column = lax.broadcasted_iota(jnp.int32, (row_count, column_count), 1) & (column_period - 1)
+    return (row - shift == column).astype(jnp.bfloat16)
+
+
 def places(ints, i, first=0):
     across = jnp.concatenate([ints[first + 2 * i], ints[first + 2 * i + 1]], axis=1)
     return across.T, across
 
 
-def rank_kernel(first, shrink, ints, fold, *refs):
+def rank_kernel(first, shrink, ints, *refs):
     shards, (out, rows, sems) = refs[:-3], refs[-3:]
     for i, shard in enumerate(shards):
         pltpu.make_async_copy(shard, rows.at[pl.ds(i * 128, 128)], sems.at[i * 128 // TILE]).start()
     out[...] = jnp.zeros(out.shape, jnp.float32)
+    fold = matching(128, 32, 128, 32)
 
     def tile(i, carry):
         part = pl.ds(pl.multiple_of(i * TILE, TILE), TILE)
@@ -148,7 +155,7 @@
         pltpu.make_async_copy(rows.at[part], rows.at[part], sems.at[i]).wait()
         group = lanes(TILE, 128, 32)
         values = kept(group == down[:, 5:6], contract_trailing(rows[part, :], shrink[...]))
-        values = kept(group == down[:, 2:3], dot(values, fold[...]))
+        values = kept(group == down[:, 2:3], dot(values, fold))
         place = lax.broadcasted_iota(jnp.int32, (64, TILE), 0) == across[6:7]
         out[...] += dot(place.astype(jnp.bfloat16), values)
         return carry
@@ -156,8 +163,8 @@
     lax.fori_loop(0, rows.shape[0] // TILE, tile, 0)
 
 
-def hidden_kernel(first, slab_at, ranks, ints, expand, down_shrink, to_gate, to_up, fold, *refs):
-    shards, pieces, (hidden, packed, rows, weight, row_sems, sem) = refs[:8], refs[8:16], refs[16:]
+def hidden_kernel(first, slab_at, ranks, ints, expand, down_shrink, *refs):
+    shards, pieces, (hidden, packed, rows, weight, to_gate, to_up, fold, row_sems, sem) = refs[:8], refs[8:16], refs[16:]
     slab = pieces[0].shape[0]
     for i, piece in enumerate(pieces):
         start = pl.multiple_of(slab_at[i] * slab, 128)
@@ -165,19 +172,27 @@
     for i, shard in enumerate(shards):
         pltpu.make_async_copy(shard, rows.at[pl.ds(i * 128, 128)], row_sems.at[i * 128 // TILE]).start()
     packed[...] = jnp.zeros(packed.shape, jnp.float32)
-    pltpu.make_async_copy(weight, weight, sem.at[0]).wait()
+    to_gate[...] = matching(128, 32, 1024, 16)
+    to_up[...] = matching(128, 32, 1024, 16, 16)
+    fold[...] = matching(1024, 16, 128, 16)
     units = hidden.shape[1]
 
     def tile(i, carry):
         part = pl.ds(pl.multiple_of(i * TILE, TILE), TILE)
         down, across = places(ints, i, first)
-        pltpu.make_async_copy(rows.at[part], rows.at[part], row_sems.at[i]).wait()
-        both = dot(rows[part, :], weight[...])
         place = lanes(TILE, ranks.shape[0], 1) == down[:, 1:2]
         own = kept(lanes(TILE, 128, 32) == down[:, 2:3], dot(place.astype(jnp.bfloat16), ranks[...]))
         chosen = lanes(TILE, to_gate.shape[1], 16) == down[:, 0:1]
-        gate = both[:, :units] + dot(kept(chosen, dot(own, to_gate[...])), expand[0])
-        up = both[:, units:] + dot(kept(chosen, dot(own, to_up[...])), expand[1])
+        gate = dot(kept(chosen, dot(own, to_gate[...])), expand[0])
+        up = dot(kept(chosen, dot(own, to_up[...])), expand[1])
+        pltpu.make_async_copy(rows.at[part], rows.at[part], row_sems.at[i]).wait()
+
+        @pl.when(i == 0)
+        def _():
+            pltpu.make_async_copy(weight, weight, sem.at[0]).wait()
+
+        both = dot(rows[part, :], weight[...])
+        gate, up = gate + both[:, :units], up + both[:, units:]
         values = (gate / (1.0 + jnp.exp(-gate)) * up).astype(jnp.bfloat16)
         hidden[part, :] = values
         parts = dot(kept(chosen, contract_trailing(values, down_shrink[...])), fold[...])
@@ -190,34 +205,33 @@
 
 
 def down_kernel(slab_at, hidden, *refs):
-    pieces, (mine, theirs, weight, sem) = refs[:8], refs[8:]
-    slab = pieces[0].shape[1]
-    for i, piece in enumerate(pieces):
-        start = pl.multiple_of(slab_at[i] * slab, 128)
-        pltpu.make_async_copy(piece, weight.at[:, pl.ds(start, slab)], sem.at[0]).start()
-    pltpu.make_async_copy(weight, weight, sem.at[0]).wait()
-    columns = weight.shape[1] // 4
-
-    def chunk(i, carry):
-        part = pl.ds(pl.multiple_of(i * columns, 128), columns)
-        both = dot(hidden[...], weight[:, part]).astype(jnp.bfloat16)
-        mine[:, part] = both[:TILE]
-        theirs[:, part] = both[TILE:]
-        return carry
-
-    lax.fori_loop(0, 4, chunk, 0)
-
-
-def adapter_kernel(ranks, ints, lane_slot, spread, *refs):
+    pieces, (mine, theirs, weight, sems) = refs[:8], refs[8:]
+    slab, step = pieces[0].shape[1], pl.program_id(0)
+
+    @pl.when(step == 0)
+    def _():
+        for i, piece in enumerate(pieces):
+            start = pl.multiple_of((slab_at[i] & 1) * slab, 128)
+            chunk = slab_at[i] >> 1
+            pltpu.make_async_copy(piece, weight.at[chunk, :, pl.ds(start, slab)], sems.at[chunk]).start()
+
+    pltpu.make_async_copy(weight.at[step], weight.at[step], sems.at[step]).wait()
+    both = dot(hidden[...], weight[step]).astype(jnp.bfloat16)
+    mine[...] = both[:TILE]
+    theirs[...] = both[TILE:]
+
+
+def adapter_kernel(ranks, ints, lane_slot, *refs):
     maps, (mine, theirs, whole, sem) = refs[:8], refs[8:]
     for i, piece in enumerate(maps):
         pltpu.make_async_copy(piece, whole.at[pl.ds(i * 64, 64)], sem.at[0]).start()
+    spread = matching(128, 16, 512, 16)
     pltpu.make_async_copy(whole, whole, sem.at[0]).wait()
     for t, out in enumerate((mine, theirs)):
         down = ints[ROW_BLOCKS.index(8 * t)].T
         place = lanes(128, 16, 1) == down[:, 7:8] >> 3
         own = kept(lanes(128, 128, 16) == down[:, 4:5], dot(place.astype(jnp.bfloat16), ranks[t]))
-        own = kept(lane_slot[...] == down[:, 0:1], dot(own, spread[...]))
+        own = kept(lane_slot[...] == down[:, 0:1], dot(own, spread))
         out[...] = dot(own, whole[...]).astype(jnp.bfloat16)
 
 
@@ -287,10 +301,6 @@
     smem = pl.BlockSpec(memory_space=pltpu.SMEM)
     stay = pl.BlockSpec(memory_space=pl.ANY)
 
-    def matching(row_count, row_period, column_count, column_period, shift=0):
-        row = jnp.arange(row_count)[:, None] % row_period - shift
-        return (row == jnp.arange(column_count)[None, :] % column_period).astype(jnp.bfloat16)
-
     own_adapters = token_adapter.reshape(16, own_count)
     ints = pl.pallas_call(
         place_kernel,
@@ -306,14 +316,14 @@
         return pl.pallas_call(
             functools.partial(rank_kernel, first),
             out_shape=jax.ShapeDtypeStruct((64, 128), jnp.float32),
-            in_specs=[vmem] * 3 + [stay] * (last - first),
+            in_specs=[vmem] * 2 + [stay] * (last - first),
             out_specs=vmem,
             scratch_shapes=[
                 pltpu.VMEM((count, width), jnp.bfloat16),
                 pltpu.SemaphoreType.DMA((count // TILE,)),
             ],
             name="ranks",
-        )(shrink, ints, matching(128, 2 * rank, 128, 2 * rank), *shards[first:last])
+        )(shrink, ints, *shards[first:last])
 
     packed = ranks_of(LATE_BLOCKS, 16) + ranks_of(0, LATE_BLOCKS)
     spread = jnp.broadcast_to(packed.astype(jnp.bfloat16)[None], (16, 64, 128))
@@ -326,11 +336,14 @@
                 jax.ShapeDtypeStruct((half_count, units), jnp.bfloat16),
                 jax.ShapeDtypeStruct((256, 128), jnp.float32),
             ),
-            in_specs=[smem] + [vmem] * 7 + [stay] * 16,
+            in_specs=[smem] + [vmem] * 4 + [stay] * 16,
             out_specs=(vmem, vmem),
             scratch_shapes=[
                 pltpu.VMEM((half_count, width), jnp.bfloat16),
                 pltpu.VMEM((width, 2 * units), jnp.bfloat16),
+                pltpu.VMEM((128, 1024), jnp.bfloat16),
+                pltpu.VMEM((128, 1024), jnp.bfloat16),
+                pltpu.VMEM((1024, 128), jnp.bfloat16),
                 pltpu.SemaphoreType.DMA((half_count // TILE,)),
                 pltpu.SemaphoreType.DMA((1,)),
             ],
@@ -341,9 +354,6 @@
             ints,
             expand,
             down_shrink,
-            matching(128, 2 * rank, adapter_list * rank, rank),
-            matching(128, 2 * rank, adapter_list * rank, rank, rank),
-            matching(adapter_list * rank, rank, 128, rank),
             *shards[8 * i : 8 * i + 8],
             *gate_up,
         )
@@ -351,11 +361,11 @@
     def down_quarter(hidden, i):
         return pl.pallas_call(
             down_kernel,
-            grid=(1,),
+            grid=(4,),
             out_shape=(jax.ShapeDtypeStruct((TILE, width), jnp.bfloat16),) * 2,
             in_specs=[smem, pl.BlockSpec((2 * TILE, units), lambda g: (i, 0))] + [stay] * 8,
-            out_specs=(vmem, vmem),
-            scratch_shapes=[pltpu.VMEM((units, width), jnp.bfloat16), pltpu.SemaphoreType.DMA((1,))],
+            out_specs=(pl.BlockSpec((TILE, width // 4), lambda g: (0, g)),) * 2,
+            scratch_shapes=[pltpu.VMEM((4, units, width // 4), jnp.bfloat16), pltpu.SemaphoreType.DMA((4,))],
             name="down",
         )(slab_at, hidden, *down)
 
@@ -381,17 +391,18 @@
     own_adapter, their_adapter = pl.pallas_call(
         adapter_kernel,
         out_shape=(jax.ShapeDtypeStruct((own_count, width), jnp.bfloat16),) * 2,
-        in_specs=[vmem] * 4 + [stay] * 8,
+        in_specs=[vmem] * 3 + [stay] * 8,
         out_specs=(vmem, vmem),
         scratch_shapes=[pltpu.VMEM((512, width), jnp.bfloat16), pltpu.SemaphoreType.DMA((1,))],
         name="adapters",
-    )(both_ranks, ints, lane_slot, matching(128, rank, 512, rank), *maps)
+    )(both_ranks, ints, lane_slot, *maps)
     adapter_term = own_adapter.astype(jnp.float32) + send(their_adapter, CORE).astype(jnp.float32)
 
     for k in (6, 5, 4, 3, 2, 1):
         sums[SOURCE[k]] = add(sums[SOURCE[k]], send(sums[k + 1], TREE_BACK[k]))
     last = send(sums[1], TREE_BACK[0]).astype(jnp.float32)
-    return (sums[0].astype(jnp.float32) + last + adapter_term).astype(jnp.bfloat16)
+    near = lax.optimization_barrier(sums[0].astype(jnp.float32) + adapter_term)
+    return (near + last).astype(jnp.bfloat16)
 
 
 def solution(mesh):

time: 303 us -> 306 us (level); the launches traced: 302 us -> 300 us
  waiting for transfers between devices: 106 us -> 113 us
  other arithmetic: 21.8 us -> 17.5 us
  Pallas kernels: 92.8 us -> 89.4 us
    ppermute x56, waiting for transfers between devices: 97.4 us -> 103 us  [send(): return lax.ppermute(value, ALL, pairs)]
    convert_element_type x5 -> x1, other arithmetic: 4.98 us -> 1.04 us  [local(): return (near + last).astype(jnp.bfloat16)]
  transfers between devices with their start and end apart: 58 -> 58, of which waited for: 19 -> 18; matrix products, arithmetic and copies ran while one was open for 8% -> 7% of each run, Pallas kernels for 31% -> 30%
where the time goes in v2:
time: 306 us; the launch traced here: 300 us
  waiting for transfers between devices  113 us (37%)
  Pallas kernels  89.4 us (29%)
  starting transfers between devices  71.1 us (23%)
  other arithmetic  17.5 us (6%)
  local copies, waits for them, and re-layouts  8.81 us (3%)
    ppermute x56, waiting for transfers between devices, send(): return lax.ppermute(value, ALL, pairs)  103 us
    ppermute x56, starting transfers between devices, send(): return lax.ppermute(value, ALL, pairs)  57.8 us
    pallas_call x2, Pallas kernels, hidden_half(): pl.pallas_call(functools.partial(hidden_kernel, 8 * i), out_shape=(jax.Sh...  43.6 us
    pallas_call x4, Pallas kernels, down_quarter(): pl.pallas_call(down_kernel, grid=(4,), out_shape=(jax.ShapeDtypeStruct((T...  24.8 us
    pallas_call x2, Pallas kernels, ranks_of(): pl.pallas_call(functools.partial(rank_kernel, first), out_shape=jax.Shape...  14 us
    all_to_all x1, starting transfers between devices, local(): lax.all_to_all(spread, GROUP, split_axis=0, concat_axis=0, tiled=True)  8.53 us
    convert_element_type x7, other arithmetic, add(): (left.astype(jnp.float32) + right.astype(jnp.float32)).astype(jnp.bfloat16)  7.27 us
    all_to_all x1, waiting for transfers between devices, local(): lax.all_to_all(spread, GROUP, split_axis=0, concat_axis=0, tiled=True)  6.36 us
  transfers between devices with their start and end apart: 58, of which 18 were waited for; matrix products, arithmetic and copies ran while one was open for 7% of the time, Pallas kernels for 30%

profile of v2, /device:TPU:1, one launch (start us, length us, event | category | flops | bytes accessed | tf_op | source)
XLA Modules:
  0.0 300.2 jit_solution(15648736248025093377)
XLA Ops:
  14.4 6.0 %collective-permute-done.27 = bf16[512,384]{1,0:T(8,128)(2,1)S(1)} collective-permute-done((bf16[512,384]{1,0:T(8,128)(2,1)S(1)}, bf16[512,384]{1,0:T(8,128)(2,1)S(1)}, u32[]{:S(2)}, u32[]{:S(2)}) %collective-permute-start.27) | collective-permute-done | bytes 393248 | tf_op jit(solution)/shard_map/ppermute | solution.py:65
  25.6 4.3 %collective-permute-start.19 = (bf16[384,1024]{1,0:T(8,128)(2,1)}, bf16[384,1024]{1,0:T(8,128)(2,1)}, u32[]{:S(2)}, u32[]{:S(2)}) collective-permute-start(bf16[384,1024]{1,0:T(8,128)(2,1)} %constant_dynamic-update-slice_fusion), channel_id=1, source_target_pairs={{16,19},{17,18},{18,17},{19,16},{20,23},{21,22},{22,21},{23,20},{2... | collective-permute-start | bytes 2359304 | tf_op jit(solution)/shard_map/ppermute | solution.py:65
  31.7 4.6 %collective-permute-done.8.refs_5_.refs_1_ = bf16[128,3072]{1,0:T(8,128)(2,1)} collective-permute-done((bf16[128,3072]{1,0:T(8,128)(2,1)S(1)}, bf16[128,3072]{1,0:T(8,128)(2,1)}, u32[]{:S(2)}, u32[]{:S(2)}) %collective-permute-start.8) | collective-permute-done | bytes 786464 | tf_op jit(solution)/shard_map/ppermute | solution.py:65
  39.0 7.6 %collective-permute-done.19 = bf16[384,1024]{1,0:T(8,128)(2,1)} collective-permute-done((bf16[384,1024]{1,0:T(8,128)(2,1)}, bf16[384,1024]{1,0:T(8,128)(2,1)}, u32[]{:S(2)}, u32[]{:S(2)}) %collective-permute-start.19) | collective-permute-done | bytes 786464 | tf_op jit(solution)/shard_map/ppermute | solution.py:65
  51.1 8.3 %collective-permute-done.18.down_shrink = bf16[1024,512]{1,0:T(8,128)(2,1)S(1)} collective-permute-done((bf16[1024,512]{1,0:T(8,128)(2,1)}, bf16[1024,512]{1,0:T(8,128)(2,1)S(1)}, u32[]{:S(2)}, u32[]{:S(2)}) %collective-permute-start.18) | collective-permute-done | bytes 1048608 | tf_op jit(solution)/shard_map/ppermute | solution.py:65
  70.9 7.6 %collective-permute-done.14.refs_1_ = bf16[128,3072]{1,0:T(8,128)(2,1)S(1)} collective-permute-done((bf16[128,3072]{1,0:T(8,128)(2,1)}, bf16[128,3072]{1,0:T(8,128)(2,1)S(1)}, u32[]{:S(2)}, u32[]{:S(2)}) %collective-permute-start.14) | collective-permute-done | bytes 786464 | tf_op jit(solution)/shard_map/ppermute | solution.py:65
  78.4 5.4 %collective-permute-done.20.refs_9_ = bf16[384,1024]{1,0:T(8,128)(2,1)} collective-permute-done((bf16[384,1024]{1,0:T(8,128)(2,1)S(1)}, bf16[384,1024]{1,0:T(8,128)(2,1)}, u32[]{:S(2)}, u32[]{:S(2)}) %collective-permute-start.20) | collective-permute-done | bytes 786464 | tf_op jit(solution)/shard_map/ppermute | solution.py:65
  96.8 9.0 %ranks.2 = f32[64,128]{1,0:T(8,128)} custom-call(bf16[128,3072]{1,0:T(8,128)(2,1)} %copy-done.23, s32[16,8,128]{2,1,0:T(8,128)} %places.1.ints, bf16[128,3072]{1,0:T(8,128)(2,1)} %copy-done.15, bf16[128,3072]{1,0:T(8,128)(2,1)} %copy-done.16, bf16[128,3072]{1,0:T(8,128)(2,1)} %copy-done.17, bf16[128,3072]{1,0:T(8,128)(2,1)} %copy-done.18, ...), custom_call_target="tpu_custom_call" | custom-call | tf_op jit(solution)/shard_map/ranks/pallas_call | solution.py:316
  105.8 5.0 %ranks.3 = f32[64,128]{1,0:T(8,128)} custom-call(bf16[128,3072]{1,0:T(8,128)(2,1)} %copy-done.23, s32[16,8,128]{2,1,0:T(8,128)} %places.1.ints, bf16[128,3072]{1,0:T(8,128)(2,1)} %copy-done.20, bf16[128,3072]{1,0:T(8,128)(2,1)} %copy-done.19, bf16[128,3072]{1,0:T(8,128)(2,1)} %copy-done.22, bf16[128,3072]{1,0:T(8,128)(2,1)} %copy-done.21), custom_call_target="tpu_custom_call" | custom-call | tf_op jit(solution)/shard_map/ranks/pallas_call | solution.py:316
  112.5 14.1 %collective-permute-done.22.refs_11_ = bf16[384,1024]{1,0:T(8,128)(2,1)} collective-permute-done((bf16[384,1024]{1,0:T(8,128)(2,1)}, bf16[384,1024]{1,0:T(8,128)(2,1)}, u32[]{:S(2)}, u32[]{:S(2)}) %collective-permute-start.22) | collective-permute-done | bytes 786464 | tf_op jit(solution)/shard_map/ppermute | solution.py:65
  128.1 8.5 %all-to-all-start = ((bf16[16,64,128]{2,1,0:T(8,128)(2,1)}), bf16[16,64,128]{2,1,0:T(8,128)(2,1)S(1)}, u32[]{:S(2)}, u32[]{:S(2)}) async-start(bf16[16,64,128]{2,1,0:T(8,128)(2,1)} %broadcast_in_dim.2), calls=%async_computation | async-start | bytes 524288 | tf_op jit(solution)/shard_map/all_to_all | solution.py:330
  137.5 6.4 %all-to-all-done = bf16[16,64,128]{2,1,0:T(8,128)(2,1)S(1)} async-done(((bf16[16,64,128]{2,1,0:T(8,128)(2,1)}), bf16[16,64,128]{2,1,0:T(8,128)(2,1)S(1)}, u32[]{:S(2)}, u32[]{:S(2)}) %all-to-all-start) | async-done | bytes 262176 | tf_op jit(solution)/shard_map/all_to_all | solution.py:330
  144.6 21.8 %hidden.3 = (bf16[1024,512]{1,0:T(8,128)(2,1)}, f32[256,128]{1,0:T(8,128)}) custom-call(s32[8]{0:T(128)} %stack.86.slab_at, bf16[1024,128]{1,0:T(8,128)(2,1)} %bitcast.25, s32[16,8,128]{2,1,0:T(8,128)} %places.1.ints, bf16[2,1024,512]{2,1,0:T(8,128)(2,1)} %copy-done.1, bf16[1024,512]{1,0:T(8,128)(2,1)} %copy-done.9, bf16[128,3072]{1,0:T(8,128)(2,1)} %copy-done.20, ...), custom_call_target="tpu_custom_call" | custom-call | tf_op jit(solution)/shard_map/hidden/pallas_call | solution.py:333
  167.2 6.2 %down.6 = (bf16[256,3072]{1,0:T(8,128)(2,1)}, bf16[256,3072]{1,0:T(8,128)(2,1)}) custom-call(s32[8]{0:T(128)} %stack.86.slab_at, bf16[1024,512]{1,0:T(8,128)(2,1)} %get-tuple-element.35.hidden, bf16[512,384]{1,0:T(8,128)(2,1)} %copy-done, bf16[512,384]{1,0:T(8,128)(2,1)} %copy-done.5, bf16[512,384]{1,0:T(8,128)(2,1)} %copy-done.7, ...), custom_call_target="tpu_custom_call" | custom-call | tf_op jit(solution)/shard_map/down/pallas_call | solution.py:362
  177.5 5.8 %collective-permute-done.43.refs_1_ = bf16[64,3072]{1,0:T(8,128)(2,1)S(1)} collective-permute-done((bf16[64,3072]{1,0:T(8,128)(2,1)}, bf16[64,3072]{1,0:T(8,128)(2,1)S(1)}, u32[]{:S(2)}, u32[]{:S(2)}) %collective-permute-start.43) | collective-permute-done | bytes 393248 | tf_op jit(solution)/shard_map/ppermute | solution.py:65
  183.6 21.8 %hidden.2 = (bf16[1024,512]{1,0:T(8,128)(2,1)}, f32[256,128]{1,0:T(8,128)}) custom-call(s32[8]{0:T(128)} %stack.86.slab_at, bf16[1024,128]{1,0:T(8,128)(2,1)} %bitcast.26, s32[16,8,128]{2,1,0:T(8,128)} %places.1.ints, bf16[2,1024,512]{2,1,0:T(8,128)(2,1)} %copy-done.1, bf16[1024,512]{1,0:T(8,128)(2,1)} %copy-done.9, bf16[128,3072]{1,0:T(8,128)(2,1)} %copy-done.10, ...), custom_call_target="tpu_custom_call" | custom-call | tf_op jit(solution)/shard_map/hidden/pallas_call | solution.py:333
  205.4 6.2 %down.5 = (bf16[256,3072]{1,0:T(8,128)(2,1)}, bf16[256,3072]{1,0:T(8,128)(2,1)}) custom-call(s32[8]{0:T(128)} %stack.86.slab_at, bf16[1024,512]{1,0:T(8,128)(2,1)} %get-tuple-element.27.hidden, bf16[512,384]{1,0:T(8,128)(2,1)} %copy-done, bf16[512,384]{1,0:T(8,128)(2,1)} %copy-done.5, bf16[512,384]{1,0:T(8,128)(2,1)} %copy-done.7, ...), custom_call_target="tpu_custom_call" | custom-call | tf_op jit(solution)/shard_map/down/pallas_call | solution.py:362
  216.2 4.7 %all-to-all-start.1 = ((bf16[16,16,128]{2,1,0:T(8,128)(2,1)}), bf16[16,16,128]{2,1,0:T(8,128)(2,1)}, u32[]{:S(2)}, u32[]{:S(2)}) async-start(bf16[16,16,128]{2,1,0:T(8,128)(2,1)} %bitcast.14), calls=%async_computation.1 | async-start | bytes 131072 | tf_op jit(solution)/shard_map/all_to_all | solution.py:388
  229.3 6.2 %down.4 = (bf16[256,3072]{1,0:T(8,128)(2,1)}, bf16[256,3072]{1,0:T(8,128)(2,1)}) custom-call(s32[8]{0:T(128)} %stack.86.slab_at, bf16[1024,512]{1,0:T(8,128)(2,1)} %get-tuple-element.27.hidden, bf16[512,384]{1,0:T(8,128)(2,1)} %copy-done, bf16[512,384]{1,0:T(8,128)(2,1)} %copy-done.5, bf16[512,384]{1,0:T(8,128)(2,1)} %copy-done.7, ...), custom_call_target="tpu_custom_call" | custom-call | tf_op jit(solution)/shard_map/down/pallas_call | solution.py:362
  235.5 6.2 %down.7 = (bf16[256,3072]{1,0:T(8,128)(2,1)}, bf16[256,3072]{1,0:T(8,128)(2,1)}) custom-call(s32[8]{0:T(128)} %stack.86.slab_at, bf16[1024,512]{1,0:T(8,128)(2,1)} %get-tuple-element.35.hidden, bf16[512,384]{1,0:T(8,128)(2,1)} %copy-done, bf16[512,384]{1,0:T(8,128)(2,1)} %copy-done.5, bf16[512,384]{1,0:T(8,128)(2,1)} %copy-done.7, ...), custom_call_target="tpu_custom_call" | custom-call | tf_op jit(solution)/shard_map/down/pallas_call | solution.py:362
  243.7 5.2 %adapters.1 = (bf16[128,3072]{1,0:T(8,128)(2,1)}, bf16[128,3072]{1,0:T(8,128)(2,1)}) custom-call(bf16[2,16,128]{2,1,0:T(8,128)(2,1)} %pad_maximum_fusion.ranks, s32[16,8,128]{2,1,0:T(8,128)} %places.1.ints, s32[1,512]{1,0:T(1,128)} %add.331.lane_slot, bf16[64,3072]{1,0:T(8,128)(2,1)} %collective-permute-done.42.refs_0_, bf16[64,3072]{1,0:T(8,128)(2,1)} %copy-done.34, ...), custom_call_target="tpu_custom_call" | custom-call | tf_op jit(solution)/shard_map/adapters/pallas_call | solution.py:391
  256.2 13.2 %collective-permute-done.53 = bf16[128,3072]{1,0:T(8,128)(2,1)S(1)} collective-permute-done((bf16[128,3072]{1,0:T(8,128)(2,1)S(1)}, bf16[128,3072]{1,0:T(8,128)(2,1)S(1)}, u32[]{:S(2)}, u32[]{:S(2)}) %collective-permute-start.53) | collective-permute-done | bytes 786464 | tf_op jit(solution)/shard_map/ppermute | solution.py:65
  275.1 12.6 %collective-permute-done.52 = bf16[128,3072]{1,0:T(8,128)(2,1)S(1)} collective-permute-done((bf16[128,3072]{1,0:T(8,128)(2,1)S(1)}, bf16[128,3072]{1,0:T(8,128)(2,1)S(1)}, u32[]{:S(2)}, u32[]{:S(2)}) %collective-permute-start.52) | collective-permute-done | bytes 786464 | tf_op jit(solution)/shard_map/ppermute | solution.py:65
  288.1 10.0 %collective-permute-done.40 = bf16[128,3072]{1,0:T(8,128)(2,1)S(1)} collective-permute-done((bf16[128,3072]{1,0:T(8,128)(2,1)S(1)}, bf16[128,3072]{1,0:T(8,128)(2,1)S(1)}, u32[]{:S(2)}, u32[]{:S(2)}) %collective-permute-start.40) | collective-permute-done | bytes 786464 | tf_op jit(solution)/shard_map/ppermute | solution.py:65
  (217 shorter events, 92.8 us)
Async XLA Ops:
  0.0 25.6 %collective-permute-start = (bf16[128,3072]{1,0:T(8,128)(2,1)}, bf16[128,3072]{1,0:T(8,128)(2,1)S(1)}, u32[]{:S(2)}, u32[]{:S(2)}) collective-permute-start(bf16[128,3072]{1,0:T(8,128)(2,1)} %param.16), channel_id=1, source_target_pairs={{0,19},{1,18},{2,17},{3,16},{4,23},{5,22},{6,21},{7,20},{8,27},{9,... | collective-permute-start | bytes 2359304 | tf_op jit(solution)/shard_map/ppermute | solution.py:65
  4.3 25.6 %collective-permute-start.2 = (bf16[128,3072]{1,0:T(8,128)(2,1)S(1)}, bf16[128,3072]{1,0:T(8,128)(2,1)}, u32[]{:S(2)}, u32[]{:S(2)}) collective-permute-start(bf16[128,3072]{1,0:T(8,128)(2,1)S(1)} %fusion.2.refs_9_.refs_5_), channel_id=1, source_target_pairs={{0,12},{1,13},{2,14},{3,15},{4,0},{5,1},{6,2},{7,3},{8,4},{9,5},{1... | collective-permute-start | bytes 2359304 | tf_op jit(solution)/shard_map/ppermute | solution.py:65
  30.0 29.4 %collective-permute-start.18 = (bf16[1024,512]{1,0:T(8,128)(2,1)}, bf16[1024,512]{1,0:T(8,128)(2,1)S(1)}, u32[]{:S(2)}, u32[]{:S(2)}) collective-permute-start(bf16[1024,512]{1,0:T(8,128)(2,1)} %param.18), channel_id=1, source_target_pairs={{0,19},{1,18},{2,17},{3,16},{4,23},{5,22},{6,21},{7,20},{8,27},{9,... | collective-permute-start | bytes 3145736 | tf_op jit(solution)/shard_map/ppermute | solution.py:65
  68.1 44.3 %collective-permute-start.17 = (bf16[2,1024,512]{2,1,0:T(8,128)(2,1)}, bf16[2,1024,512]{2,1,0:T(8,128)(2,1)S(1)}, u32[]{:S(2)}, u32[]{:S(2)}) collective-permute-start(bf16[2,1024,512]{2,1,0:T(8,128)(2,1)} %param.17), channel_id=1, source_target_pairs={{0,19},{1,18},{2,17},{3,16},{4,23},{5,22},{6,21},{7,20},{8,27},{9,... | collective-permute-start | bytes 6291464 | tf_op jit(solution)/shard_map/ppermute | solution.py:65
  87.2 23.6 %collective-permute-start.21 = (bf16[384,1024]{1,0:T(8,128)(2,1)S(1)}, bf16[384,1024]{1,0:T(8,128)(2,1)}, u32[]{:S(2)}, u32[]{:S(2)}) collective-permute-start(bf16[384,1024]{1,0:T(8,128)(2,1)S(1)} %broadcast_select_fusion.refs_8_), channel_id=1, source_target_pairs={{0,96},{1,97},{2,98},{3,99},{4,100},{5,101},{6,102},{7,103},{8,104... | collective-permute-start | bytes 2359304 | tf_op jit(solution)/shard_map/ppermute | solution.py:65
  89.8 21.8 %collective-permute-start.24 = (bf16[384,1024]{1,0:T(8,128)(2,1)}, bf16[384,1024]{1,0:T(8,128)(2,1)}, u32[]{:S(2)}, u32[]{:S(2)}) collective-permute-start(bf16[384,1024]{1,0:T(8,128)(2,1)} %collective-permute-done.23.refs_12_), channel_id=1, source_target_pairs={{0,32},{1,33},{2,34},{3,35},{4,36},{5,37},{6,38},{7,39},{8,40},{9,... | collective-permute-start | bytes 2359304 | tf_op jit(solution)/shard_map/ppermute | solution.py:65
  89.9 36.7 %collective-permute-start.22 = (bf16[384,1024]{1,0:T(8,128)(2,1)}, bf16[384,1024]{1,0:T(8,128)(2,1)}, u32[]{:S(2)}, u32[]{:S(2)}) collective-permute-start(bf16[384,1024]{1,0:T(8,128)(2,1)} %collective-permute-done.20.refs_9_), channel_id=1, source_target_pairs={{0,32},{1,33},{2,34},{3,35},{4,36},{5,37},{6,38},{7,39},{8,40},{9,... | collective-permute-start | bytes 2359304 | tf_op jit(solution)/shard_map/ppermute | solution.py:65
  91.8 44.8 %collective-permute-start.26 = (bf16[384,1024]{1,0:T(8,128)(2,1)}, bf16[384,1024]{1,0:T(8,128)(2,1)}, u32[]{:S(2)}, u32[]{:S(2)}) collective-permute-start(bf16[384,1024]{1,0:T(8,128)(2,1)} %collective-permute-done.25.refs_14_), channel_id=1, source_target_pairs={{0,96},{1,97},{2,98},{3,99},{4,100},{5,101},{6,102},{7,103},{8,104... | collective-permute-start | bytes 2359304 | tf_op jit(solution)/shard_map/ppermute | solution.py:65
  110.8 55.5 %collective-permute-start.29 = (bf16[512,384]{1,0:T(8,128)(2,1)S(1)}, bf16[512,384]{1,0:T(8,128)(2,1)S(1)}, u32[]{:S(2)}, u32[]{:S(2)}) collective-permute-start(bf16[512,384]{1,0:T(8,128)(2,1)S(1)} %broadcast_select_fusion.1.refs_0_), channel_id=1, source_target_pairs={{0,96},{1,97},{2,98},{3,99},{4,100},{5,101},{6,102},{7,103},{8,104... | collective-permute-start | bytes 1179656 | tf_op jit(solution)/shard_map/ppermute | solution.py:65
  111.6 54.8 %collective-permute-start.32 = (bf16[512,384]{1,0:T(8,128)(2,1)}, bf16[512,384]{1,0:T(8,128)(2,1)S(1)}, u32[]{:S(2)}, u32[]{:S(2)}) collective-permute-start(bf16[512,384]{1,0:T(8,128)(2,1)} %copy-done.4), channel_id=1, source_target_pairs={{0,32},{1,33},{2,34},{3,35},{4,36},{5,37},{6,38},{7,39},{8,40},{9,... | collective-permute-start | bytes 1179656 | tf_op jit(solution)/shard_map/ppermute | solution.py:65
  112.4 54.0 %collective-permute-start.30 = (bf16[512,384]{1,0:T(8,128)(2,1)}, bf16[512,384]{1,0:T(8,128)(2,1)}, u32[]{:S(2)}, u32[]{:S(2)}) collective-permute-start(bf16[512,384]{1,0:T(8,128)(2,1)} %copy-done.5), channel_id=1, source_target_pairs={{0,32},{1,33},{2,34},{3,35},{4,36},{5,37},{6,38},{7,39},{8,40},{9,... | collective-permute-start | bytes 1179656 | tf_op jit(solution)/shard_map/ppermute | solution.py:65
  126.6 39.8 %collective-permute-start.34 = (bf16[512,384]{1,0:T(8,128)(2,1)}, bf16[512,384]{1,0:T(8,128)(2,1)}, u32[]{:S(2)}, u32[]{:S(2)}) collective-permute-start(bf16[512,384]{1,0:T(8,128)(2,1)} %copy-done.6), channel_id=1, source_target_pairs={{0,96},{1,97},{2,98},{3,99},{4,100},{5,101},{6,102},{7,103},{8,104... | collective-permute-start | bytes 1179656 | tf_op jit(solution)/shard_map/ppermute | solution.py:65
  136.7 37.9 %collective-permute-start.42 = (bf16[64,3072]{1,0:T(8,128)(2,1)}, bf16[64,3072]{1,0:T(8,128)(2,1)}, u32[]{:S(2)}, u32[]{:S(2)}) collective-permute-start(bf16[64,3072]{1,0:T(8,128)(2,1)} %param.19), channel_id=1, source_target_pairs={{0,19},{1,18},{2,17},{3,16},{4,23},{5,22},{6,21},{7,20},{8,27},{9,... | collective-permute-start | bytes 1179656 | tf_op jit(solution)/shard_map/ppermute | solution.py:65
  173.4 75.7 %collective-permute-start.38 = (bf16[256,3072]{1,0:T(8,128)(2,1)}, bf16[256,3072]{1,0:T(8,128)(2,1)S(1)}, u32[]{:S(2)}, u32[]{:S(2)}) collective-permute-start(bf16[256,3072]{1,0:T(8,128)(2,1)} %get-tuple-element.37), channel_id=1, source_target_pairs={{0,16},{1,17},{2,18},{3,19},{4,20},{5,21},{6,22},{7,23},{8,24},{9,... | collective-permute-start | bytes 4718600 | tf_op jit(solution)/shard_map/ppermute | solution.py:65
  174.8 40.5 %collective-permute-start.44 = (bf16[64,3072]{1,0:T(8,128)(2,1)}, bf16[64,3072]{1,0:T(8,128)(2,1)S(1)}, u32[]{:S(2)}, u32[]{:S(2)}) collective-permute-start(bf16[64,3072]{1,0:T(8,128)(2,1)} %collective-permute-done.42.refs_0_), channel_id=1, source_target_pairs={{0,4},{1,5},{2,6},{3,7},{4,8},{5,9},{6,10},{7,11},{8,12},{9,13},{1... | collective-permute-start | bytes 1179656 | tf_op jit(solution)/shard_map/ppermute | solution.py:65
  175.1 45.8 %collective-permute-start.45 = (bf16[64,3072]{1,0:T(8,128)(2,1)}, bf16[64,3072]{1,0:T(8,128)(2,1)S(1)}, u32[]{:S(2)}, u32[]{:S(2)}) collective-permute-start(bf16[64,3072]{1,0:T(8,128)(2,1)} %collective-permute-done.42.refs_0_), channel_id=1, source_target_pairs={{0,1},{1,0},{2,3},{3,2},{4,5},{5,4},{6,7},{7,6},{8,9},{9,8},{10,11... | collective-permute-start | bytes 1179656 | tf_op jit(solution)/shard_map/ppermute | solution.py:65
  183.3 39.1 %collective-permute-start.46 = (bf16[64,3072]{1,0:T(8,128)(2,1)S(1)}, bf16[64,3072]{1,0:T(8,128)(2,1)}, u32[]{:S(2)}, u32[]{:S(2)}) collective-permute-start(bf16[64,3072]{1,0:T(8,128)(2,1)S(1)} %collective-permute-done.43.refs_1_), channel_id=1, source_target_pairs={{0,12},{1,13},{2,14},{3,15},{4,0},{5,1},{6,2},{7,3},{8,4},{9,5},{1... | collective-permute-start | bytes 1179656 | tf_op jit(solution)/shard_map/ppermute | solution.py:65
  211.7 38.9 %collective-permute-start.36 = (bf16[256,3072]{1,0:T(8,128)(2,1)}, bf16[256,3072]{1,0:T(8,128)(2,1)}, u32[]{:S(2)}, u32[]{:S(2)}) collective-permute-start(bf16[256,3072]{1,0:T(8,128)(2,1)} %get-tuple-element.32), channel_id=1, source_target_pairs={{0,16},{1,17},{2,18},{3,19},{4,20},{5,21},{6,22},{7,23},{8,24},{9,... | collective-permute-start | bytes 4718600 | tf_op jit(solution)/shard_map/ppermute | solution.py:65
  221.0 21.5 %collective-permute-start.48 = (bf16[64,3072]{1,0:T(8,128)(2,1)S(1)}, bf16[64,3072]{1,0:T(8,128)(2,1)S(1)}, u32[]{:S(2)}, u32[]{:S(2)}) collective-permute-start(bf16[64,3072]{1,0:T(8,128)(2,1)S(1)} %collective-permute-done.44.refs_2_), channel_id=1, source_target_pairs={{0,1},{1,0},{2,3},{3,2},{4,5},{5,4},{6,7},{7,6},{8,9},{9,8},{10,11... | collective-permute-start | bytes 1179656 | tf_op jit(solution)/shard_map/ppermute | solution.py:65
  222.4 21.3 %collective-permute-start.49 = (bf16[64,3072]{1,0:T(8,128)(2,1)}, bf16[64,3072]{1,0:T(8,128)(2,1)}, u32[]{:S(2)}, u32[]{:S(2)}) collective-permute-start(bf16[64,3072]{1,0:T(8,128)(2,1)} %collective-permute-done.46.refs_4_), channel_id=1, source_target_pairs={{0,1},{1,0},{2,3},{3,2},{4,5},{5,4},{6,7},{7,6},{8,9},{9,8},{10,11... | collective-permute-start | bytes 1179656 | tf_op jit(solution)/shard_map/ppermute | solution.py:65
  243.2 29.3 %collective-permute-start.35 = (bf16[256,3072]{1,0:T(8,128)(2,1)}, bf16[256,3072]{1,0:T(8,128)(2,1)}, u32[]{:S(2)}, u32[]{:S(2)}) collective-permute-start(bf16[256,3072]{1,0:T(8,128)(2,1)} %get-tuple-element.29), channel_id=1, source_target_pairs={{0,16},{1,17},{2,18},{3,19},{4,20},{5,21},{6,22},{7,23},{8,24},{9,... | collective-permute-start | bytes 4718600 | tf_op jit(solution)/shard_map/ppermute | solution.py:65
  248.9 39.1 %collective-permute-start.50 = (bf16[128,3072]{1,0:T(8,128)(2,1)}, bf16[128,3072]{1,0:T(8,128)(2,1)S(1)}, u32[]{:S(2)}, u32[]{:S(2)}) collective-permute-start(bf16[128,3072]{1,0:T(8,128)(2,1)} %get-tuple-element.42), channel_id=1, source_target_pairs={{0,16},{1,17},{2,18},{3,19},{4,20},{5,21},{6,22},{7,23},{8,24},{9,... | collective-permute-start | bytes 2359304 | tf_op jit(solution)/shard_map/ppermute | solution.py:65
  253.1 35.0 %collective-permute-start.37 = (bf16[128,3072]{1,0:T(8,128)(2,1)S(1)}, bf16[128,3072]{1,0:T(8,128)(2,1)S(1)}, u32[]{:S(2)}, u32[]{:S(2)}) collective-permute-start(bf16[128,3072]{1,0:T(8,128)(2,1)S(1)} %get-tuple-element.33), channel_id=1, source_target_pairs={{1,0},{0,1},{3,2},{2,3},{5,4},{4,5},{7,6},{6,7},{9,8},{8,9},{11,10... | collective-permute-start | bytes 2359304 | tf_op jit(solution)/shard_map/ppermute | solution.py:65
  272.5 25.6 %collective-permute-start.40 = (bf16[128,3072]{1,0:T(8,128)(2,1)S(1)}, bf16[128,3072]{1,0:T(8,128)(2,1)S(1)}, u32[]{:S(2)}, u32[]{:S(2)}) collective-permute-start(bf16[128,3072]{1,0:T(8,128)(2,1)S(1)} %add_convert_fusion.7), channel_id=1, source_target_pairs={{4,0},{5,1},{6,2},{7,3},{8,4},{9,5},{10,6},{11,7},{12,8},{13,9},{1... | collective-permute-start | bytes 2359304 | tf_op jit(solution)/shard_map/ppermute | solution.py:65
  (78 other events, 1232.2 us)

commit v3 on v2

--- a/solution.py
+++ b/solution.py
@@ -57,7 +57,7 @@
 ROW_BLOCKS = tuple(
     half[2 * pair + j] + 8 * part for half in HALVES for pair in range(2) for part in range(2) for j in range(2)
 )
-LATE_BLOCKS = 4
+LATE_BLOCKS = 8
 TILE = 256
 
 
@@ -221,17 +221,22 @@
     theirs[...] = both[TILE:]
 
 
-def adapter_kernel(ranks, ints, lane_slot, *refs):
+def adapter_kernel(map_slots, ranks, ints, *refs):
     maps, (mine, theirs, whole, sem) = refs[:8], refs[8:]
     for i, piece in enumerate(maps):
         pltpu.make_async_copy(piece, whole.at[pl.ds(i * 64, 64)], sem.at[0]).start()
     spread = matching(128, 16, 512, 16)
+    lane = lax.broadcasted_iota(jnp.int32, (1, 512), 1)
+    first = jnp.zeros((1, 512), jnp.int32)
+    for i in range(8):
+        first = jnp.where(lane >> 6 == i, map_slots[i], first)
+    lane_slot = first + ((lane >> 4) & 3)
     pltpu.make_async_copy(whole, whole, sem.at[0]).wait()
     for t, out in enumerate((mine, theirs)):
         down = ints[ROW_BLOCKS.index(8 * t)].T
         place = lanes(128, 16, 1) == down[:, 7:8] >> 3
         own = kept(lanes(128, 128, 16) == down[:, 4:5], dot(place.astype(jnp.bfloat16), ranks[t]))
-        own = kept(lane_slot[...] == down[:, 0:1], dot(own, spread))
+        own = kept(lane_slot == down[:, 0:1], dot(own, spread))
         out[...] = dot(own, whole[...]).astype(jnp.bfloat16)
 
 
@@ -262,7 +267,6 @@
     units = gate_base.shape[1]
     adapter_list = adapter_slot.shape[0]
     owner_partial = adapter_list // 16
-    rank = down_expand_maps.shape[0] // owner_partial
     total = 16 * own_count
 
     slab_at = [((xi + dx) % 4) * 2 + (ci if half == 0 else 1 - ci) for half in range(2) for dx in X_ORDER]
@@ -293,8 +297,7 @@
     for k in range(8):
         from_y, from_l = (yi + pick(BLOCK_Y, k)) % 4, (li + pick(BLOCK_L, k)) % 2
         map_slots.append((from_y * 4 + jnp.where(ci == 0, hi * 2 + from_l, 3 - hi * 2 - from_l)) * owner_partial)
-    lane_slot = jnp.stack(map_slots).astype(jnp.int32)[:, None] + jnp.arange(64, dtype=jnp.int32)[None, :] // rank
-    lane_slot = lane_slot.reshape(1, 512)
+    map_slots = jnp.stack(map_slots).astype(jnp.int32)
 
     half_count = total // 2
     vmem = pl.BlockSpec(memory_space=pltpu.VMEM)
@@ -391,11 +394,11 @@
     own_adapter, their_adapter = pl.pallas_call(
         adapter_kernel,
         out_shape=(jax.ShapeDtypeStruct((own_count, width), jnp.bfloat16),) * 2,
-        in_specs=[vmem] * 3 + [stay] * 8,
+        in_specs=[smem] + [vmem] * 2 + [stay] * 8,
         out_specs=(vmem, vmem),
         scratch_shapes=[pltpu.VMEM((512, width), jnp.bfloat16), pltpu.SemaphoreType.DMA((1,))],
         name="adapters",
-    )(both_ranks, ints, lane_slot, *maps)
+    )(map_slots, both_ranks, ints, *maps)
     adapter_term = own_adapter.astype(jnp.float32) + send(their_adapter, CORE).astype(jnp.float32)
 
     for k in (6, 5, 4, 3, 2, 1):

time: 306 us -> 311 us (1.016)
    unnamed x89 -> x85, local copies, waits for them, and re-layouts: 5.86 us -> 6.74 us
  transfers between devices with their start and end apart: 58 -> 58, of which waited for: 18 -> 20; matrix products, arithmetic and copies ran while one was open for 7% -> 7% of each run, Pallas kernels for 30% -> 29%
where the time goes in v3:
time: 311 us; the launch traced here: 305 us
  waiting for transfers between devices  114 us (37%)
  Pallas kernels  89.7 us (29%)
  starting transfers between devices  73.2 us (24%)
  other arithmetic  18.4 us (6%)
  local copies, waits for them, and re-layouts  9.62 us (3%)
    ppermute x56, waiting for transfers between devices, send(): return lax.ppermute(value, ALL, pairs)  101 us
    ppermute x56, starting transfers between devices, send(): return lax.ppermute(value, ALL, pairs)  59.5 us
    pallas_call x2, Pallas kernels, hidden_half(): pl.pallas_call(functools.partial(hidden_kernel, 8 * i), out_shape=(jax.Sh...  43.6 us
    pallas_call x4, Pallas kernels, down_quarter(): pl.pallas_call(down_kernel, grid=(4,), out_shape=(jax.ShapeDtypeStruct((T...  24.9 us
    pallas_call x2, Pallas kernels, ranks_of(): pl.pallas_call(functools.partial(rank_kernel, first), out_shape=jax.Shape...  14 us
    all_to_all x1, starting transfers between devices, local(): lax.all_to_all(packed_down, GROUP, split_axis=0, concat_axis=0, tiled=True)  7.44 us
    convert_element_type x7, other arithmetic, add(): (left.astype(jnp.float32) + right.astype(jnp.float32)).astype(jnp.bfloat16)  7.27 us
    unnamed x85, local copies, waits for them, and re-layouts  6.74 us
  transfers between devices with their start and end apart: 58, of which 20 were waited for; matrix products, arithmetic and copies ran while one was open for 7% of the time, Pallas kernels for 29%

profile of v3, /device:TPU:1, one launch (start us, length us, event | category | flops | bytes accessed | tf_op | source)
XLA Modules:
  0.0 305.1 jit_solution(14089342333109162085)
XLA Ops:
  7.2 5.7 %collective-permute-start.27 = (bf16[512,384]{1,0:T(8,128)(2,1)S(1)}, bf16[512,384]{1,0:T(8,128)(2,1)S(1)}, u32[]{:S(2)}, u32[]{:S(2)}) collective-permute-start(bf16[512,384]{1,0:T(8,128)(2,1)S(1)} %copy-done.32), channel_id=1, source_target_pairs={{16,19},{17,18},{18,17},{19,16},{20,23},{21,22},{22,21},{23,20},{2... | collective-permute-start | bytes 1179656 | tf_op jit(solution)/shard_map/ppermute | solution.py:65
  14.4 7.4 %collective-permute-done.27 = bf16[512,384]{1,0:T(8,128)(2,1)S(1)} collective-permute-done((bf16[512,384]{1,0:T(8,128)(2,1)S(1)}, bf16[512,384]{1,0:T(8,128)(2,1)S(1)}, u32[]{:S(2)}, u32[]{:S(2)}) %collective-permute-start.27) | collective-permute-done | bytes 393248 | tf_op jit(solution)/shard_map/ppermute | solution.py:65
  35.4 11.2 %collective-permute-done.19 = bf16[384,1024]{1,0:T(8,128)(2,1)} collective-permute-done((bf16[384,1024]{1,0:T(8,128)(2,1)}, bf16[384,1024]{1,0:T(8,128)(2,1)}, u32[]{:S(2)}, u32[]{:S(2)}) %collective-permute-start.19) | collective-permute-done | bytes 786464 | tf_op jit(solution)/shard_map/ppermute | solution.py:65
  49.7 9.7 %collective-permute-done.18.down_shrink = bf16[1024,512]{1,0:T(8,128)(2,1)S(1)} collective-permute-done((bf16[1024,512]{1,0:T(8,128)(2,1)}, bf16[1024,512]{1,0:T(8,128)(2,1)S(1)}, u32[]{:S(2)}, u32[]{:S(2)}) %collective-permute-start.18) | collective-permute-done | bytes 1048608 | tf_op jit(solution)/shard_map/ppermute | solution.py:65
  67.5 5.9 %collective-permute-done.11.refs_1_ = bf16[128,3072]{1,0:T(8,128)(2,1)S(1)} collective-permute-done((bf16[128,3072]{1,0:T(8,128)(2,1)}, bf16[128,3072]{1,0:T(8,128)(2,1)S(1)}, u32[]{:S(2)}, u32[]{:S(2)}) %collective-permute-start.11) | collective-permute-done | bytes 786464 | tf_op jit(solution)/shard_map/ppermute | solution.py:65
  74.1 6.7 %collective-permute-start.13 = (bf16[128,3072]{1,0:T(8,128)(2,1)S(1)}, bf16[128,3072]{1,0:T(8,128)(2,1)S(1)}, u32[]{:S(2)}, u32[]{:S(2)}) collective-permute-start(bf16[128,3072]{1,0:T(8,128)(2,1)S(1)} %collective-permute-done.11.refs_1_), channel_id=1, source_target_pairs={{0,16},{1,17},{2,18},{3,19},{4,20},{5,21},{6,22},{7,23},{8,24},{9,... | collective-permute-start | bytes 2359304 | tf_op jit(solution)/shard_map/ppermute | solution.py:65
  98.8 7.0 %ranks.2 = f32[64,128]{1,0:T(8,128)} custom-call(bf16[128,3072]{1,0:T(8,128)(2,1)} %copy-done.23, s32[16,8,128]{2,1,0:T(8,128)} %places.1.ints, bf16[128,3072]{1,0:T(8,128)(2,1)} %copy-done.10, bf16[128,3072]{1,0:T(8,128)(2,1)} %collective-permute-done.3.refs_1_, bf16[128,3072]{1,0:T(8,128)(2,1)} %copy-done.12, bf16[128,3072]{1,0:T(8,128)(2,1)} %copy-done.13, ...), custom_call_target="tpu_custom_call" | custom-call | tf_op jit(solution)/shard_map/ranks/pallas_call | solution.py:319
  105.8 7.0 %ranks.3 = f32[64,128]{1,0:T(8,128)} custom-call(bf16[128,3072]{1,0:T(8,128)(2,1)} %copy-done.23, s32[16,8,128]{2,1,0:T(8,128)} %places.1.ints, bf16[128,3072]{1,0:T(8,128)(2,1)} %copy-done.18, bf16[128,3072]{1,0:T(8,128)(2,1)} %copy-done.16, bf16[128,3072]{1,0:T(8,128)(2,1)} %copy-done.22, bf16[128,3072]{1,0:T(8,128)(2,1)} %copy-done.19, ...), custom_call_target="tpu_custom_call" | custom-call | tf_op jit(solution)/shard_map/ranks/pallas_call | solution.py:319
  114.5 14.5 %collective-permute-done.22.refs_11_ = bf16[384,1024]{1,0:T(8,128)(2,1)} collective-permute-done((bf16[384,1024]{1,0:T(8,128)(2,1)}, bf16[384,1024]{1,0:T(8,128)(2,1)}, u32[]{:S(2)}, u32[]{:S(2)}) %collective-permute-start.22) | collective-permute-done | bytes 786464 | tf_op jit(solution)/shard_map/ppermute | solution.py:65
  130.6 6.2 %all-to-all-start = ((bf16[16,64,128]{2,1,0:T(8,128)(2,1)}), bf16[16,64,128]{2,1,0:T(8,128)(2,1)S(1)}, u32[]{:S(2)}, u32[]{:S(2)}) async-start(bf16[16,64,128]{2,1,0:T(8,128)(2,1)} %broadcast_in_dim.2), calls=%async_computation | async-start | bytes 524288 | tf_op jit(solution)/shard_map/all_to_all | solution.py:333
  137.6 6.4 %all-to-all-done = bf16[16,64,128]{2,1,0:T(8,128)(2,1)S(1)} async-done(((bf16[16,64,128]{2,1,0:T(8,128)(2,1)}), bf16[16,64,128]{2,1,0:T(8,128)(2,1)S(1)}, u32[]{:S(2)}, u32[]{:S(2)}) %all-to-all-start) | async-done | bytes 262176 | tf_op jit(solution)/shard_map/all_to_all | solution.py:333
  144.7 21.8 %hidden.3 = (bf16[1024,512]{1,0:T(8,128)(2,1)}, f32[256,128]{1,0:T(8,128)}) custom-call(s32[8]{0:T(128)} %stack.86.slab_at, bf16[1024,128]{1,0:T(8,128)(2,1)} %bitcast.25, s32[16,8,128]{2,1,0:T(8,128)} %places.1.ints, bf16[2,1024,512]{2,1,0:T(8,128)(2,1)} %copy-done.1, bf16[1024,512]{1,0:T(8,128)(2,1)} %copy-done.9, bf16[128,3072]{1,0:T(8,128)(2,1)} %copy-done.18, ...), custom_call_target="tpu_custom_call" | custom-call | tf_op jit(solution)/shard_map/hidden/pallas_call | solution.py:336
  167.4 6.3 %down.6 = (bf16[256,3072]{1,0:T(8,128)(2,1)}, bf16[256,3072]{1,0:T(8,128)(2,1)}) custom-call(s32[8]{0:T(128)} %stack.86.slab_at, bf16[1024,512]{1,0:T(8,128)(2,1)} %get-tuple-element.35.hidden, bf16[512,384]{1,0:T(8,128)(2,1)} %copy-done, bf16[512,384]{1,0:T(8,128)(2,1)} %copy-done.5, bf16[512,384]{1,0:T(8,128)(2,1)} %copy-done.7, ...), custom_call_target="tpu_custom_call" | custom-call | tf_op jit(solution)/shard_map/down/pallas_call | solution.py:365
  175.4 21.8 %hidden.2 = (bf16[1024,512]{1,0:T(8,128)(2,1)}, f32[256,128]{1,0:T(8,128)}) custom-call(s32[8]{0:T(128)} %stack.86.slab_at, bf16[1024,128]{1,0:T(8,128)(2,1)} %bitcast.26, s32[16,8,128]{2,1,0:T(8,128)} %places.1.ints, bf16[2,1024,512]{2,1,0:T(8,128)(2,1)} %copy-done.1, bf16[1024,512]{1,0:T(8,128)(2,1)} %copy-done.9, bf16[128,3072]{1,0:T(8,128)(2,1)} %copy-done.10, ...), custom_call_target="tpu_custom_call" | custom-call | tf_op jit(solution)/shard_map/hidden/pallas_call | solution.py:336
  197.2 6.2 %down.5 = (bf16[256,3072]{1,0:T(8,128)(2,1)}, bf16[256,3072]{1,0:T(8,128)(2,1)}) custom-call(s32[8]{0:T(128)} %stack.86.slab_at, bf16[1024,512]{1,0:T(8,128)(2,1)} %get-tuple-element.27.hidden, bf16[512,384]{1,0:T(8,128)(2,1)} %copy-done, bf16[512,384]{1,0:T(8,128)(2,1)} %copy-done.5, bf16[512,384]{1,0:T(8,128)(2,1)} %copy-done.7, ...), custom_call_target="tpu_custom_call" | custom-call | tf_op jit(solution)/shard_map/down/pallas_call | solution.py:365
  209.5 6.0 %collective-permute-done.45.refs_3_ = bf16[64,3072]{1,0:T(8,128)(2,1)S(1)} collective-permute-done((bf16[64,3072]{1,0:T(8,128)(2,1)}, bf16[64,3072]{1,0:T(8,128)(2,1)S(1)}, u32[]{:S(2)}, u32[]{:S(2)}) %collective-permute-start.45) | collective-permute-done | bytes 393248 | tf_op jit(solution)/shard_map/ppermute | solution.py:65
  218.3 7.4 %all-to-all-start.1 = ((bf16[16,16,128]{2,1,0:T(8,128)(2,1)}), bf16[16,16,128]{2,1,0:T(8,128)(2,1)}, u32[]{:S(2)}, u32[]{:S(2)}) async-start(bf16[16,16,128]{2,1,0:T(8,128)(2,1)} %bitcast.27), calls=%async_computation.1 | async-start | bytes 131072 | tf_op jit(solution)/shard_map/all_to_all | solution.py:391
  225.7 5.8 %all-to-all-done.1 = bf16[16,16,128]{2,1,0:T(8,128)(2,1)} async-done(((bf16[16,16,128]{2,1,0:T(8,128)(2,1)}), bf16[16,16,128]{2,1,0:T(8,128)(2,1)}, u32[]{:S(2)}, u32[]{:S(2)}) %all-to-all-start.1) | async-done | bytes 65568 | tf_op jit(solution)/shard_map/all_to_all | solution.py:391
  234.0 6.2 %down.4 = (bf16[256,3072]{1,0:T(8,128)(2,1)}, bf16[256,3072]{1,0:T(8,128)(2,1)}) custom-call(s32[8]{0:T(128)} %stack.86.slab_at, bf16[1024,512]{1,0:T(8,128)(2,1)} %get-tuple-element.27.hidden, bf16[512,384]{1,0:T(8,128)(2,1)} %copy-done, bf16[512,384]{1,0:T(8,128)(2,1)} %copy-done.5, bf16[512,384]{1,0:T(8,128)(2,1)} %copy-done.7, ...), custom_call_target="tpu_custom_call" | custom-call | tf_op jit(solution)/shard_map/down/pallas_call | solution.py:365
  240.2 6.3 %down.7 = (bf16[256,3072]{1,0:T(8,128)(2,1)}, bf16[256,3072]{1,0:T(8,128)(2,1)}) custom-call(s32[8]{0:T(128)} %stack.86.slab_at, bf16[1024,512]{1,0:T(8,128)(2,1)} %get-tuple-element.35.hidden, bf16[512,384]{1,0:T(8,128)(2,1)} %copy-done, bf16[512,384]{1,0:T(8,128)(2,1)} %copy-done.5, bf16[512,384]{1,0:T(8,128)(2,1)} %copy-done.7, ...), custom_call_target="tpu_custom_call" | custom-call | tf_op jit(solution)/shard_map/down/pallas_call | solution.py:365
  248.5 5.4 %adapters.1 = (bf16[128,3072]{1,0:T(8,128)(2,1)}, bf16[128,3072]{1,0:T(8,128)(2,1)}) custom-call(s32[8]{0:T(128)} %stack.100.map_slots, bf16[2,16,128]{2,1,0:T(8,128)(2,1)} %pad_maximum_fusion.ranks, s32[16,8,128]{2,1,0:T(8,128)} %places.1.ints, bf16[64,3072]{1,0:T(8,128)(2,1)} %collective-permute-done.42.refs_0_, bf16[64,3072]{1,0:T(8,128)(2,1)} %copy-done.34, ...), custom_call_target="tpu_custom_call" | custom-call | tf_op jit(solution)/shard_map/adapters/pallas_call | solution.py:394
  261.4 12.9 %collective-permute-done.53 = bf16[128,3072]{1,0:T(8,128)(2,1)S(1)} collective-permute-done((bf16[128,3072]{1,0:T(8,128)(2,1)S(1)}, bf16[128,3072]{1,0:T(8,128)(2,1)S(1)}, u32[]{:S(2)}, u32[]{:S(2)}) %collective-permute-start.53) | collective-permute-done | bytes 786464 | tf_op jit(solution)/shard_map/ppermute | solution.py:65
  280.0 12.5 %collective-permute-done.52 = bf16[128,3072]{1,0:T(8,128)(2,1)S(1)} collective-permute-done((bf16[128,3072]{1,0:T(8,128)(2,1)S(1)}, bf16[128,3072]{1,0:T(8,128)(2,1)S(1)}, u32[]{:S(2)}, u32[]{:S(2)}) %collective-permute-start.52) | collective-permute-done | bytes 786464 | tf_op jit(solution)/shard_map/ppermute | solution.py:65
  293.0 10.0 %collective-permute-done.40 = bf16[128,3072]{1,0:T(8,128)(2,1)S(1)} collective-permute-done((bf16[128,3072]{1,0:T(8,128)(2,1)S(1)}, bf16[128,3072]{1,0:T(8,128)(2,1)S(1)}, u32[]{:S(2)}, u32[]{:S(2)}) %collective-permute-start.40) | collective-permute-done | bytes 786464 | tf_op jit(solution)/shard_map/ppermute | solution.py:65
  (210 shorter events, 88.1 us)
Async XLA Ops:
  0.0 25.6 %collective-permute-start = (bf16[128,3072]{1,0:T(8,128)(2,1)}, bf16[128,3072]{1,0:T(8,128)(2,1)S(1)}, u32[]{:S(2)}, u32[]{:S(2)}) collective-permute-start(bf16[128,3072]{1,0:T(8,128)(2,1)} %param.16), channel_id=1, source_target_pairs={{0,19},{1,18},{2,17},{3,16},{4,23},{5,22},{6,21},{7,20},{8,27},{9,... | collective-permute-start | bytes 2359304 | tf_op jit(solution)/shard_map/ppermute | solution.py:65
  4.3 25.6 %collective-permute-start.2 = (bf16[128,3072]{1,0:T(8,128)(2,1)S(1)}, bf16[128,3072]{1,0:T(8,128)(2,1)S(1)}, u32[]{:S(2)}, u32[]{:S(2)}) collective-permute-start(bf16[128,3072]{1,0:T(8,128)(2,1)S(1)} %fusion.2.refs_5_), channel_id=1, source_target_pairs={{0,1},{1,0},{2,3},{3,2},{4,5},{5,4},{6,7},{7,6},{8,9},{9,8},{10,11... | collective-permute-start | bytes 2359304 | tf_op jit(solution)/shard_map/ppermute | solution.py:65
  30.0 29.4 %collective-permute-start.18 = (bf16[1024,512]{1,0:T(8,128)(2,1)}, bf16[1024,512]{1,0:T(8,128)(2,1)S(1)}, u32[]{:S(2)}, u32[]{:S(2)}) collective-permute-start(bf16[1024,512]{1,0:T(8,128)(2,1)} %param.18), channel_id=1, source_target_pairs={{0,19},{1,18},{2,17},{3,16},{4,23},{5,22},{6,21},{7,20},{8,27},{9,... | collective-permute-start | bytes 3145736 | tf_op jit(solution)/shard_map/ppermute | solution.py:65
  67.5 47.0 %collective-permute-start.17 = (bf16[2,1024,512]{2,1,0:T(8,128)(2,1)}, bf16[2,1024,512]{2,1,0:T(8,128)(2,1)S(1)}, u32[]{:S(2)}, u32[]{:S(2)}) collective-permute-start(bf16[2,1024,512]{2,1,0:T(8,128)(2,1)} %param.17), channel_id=1, source_target_pairs={{0,19},{1,18},{2,17},{3,16},{4,23},{5,22},{6,21},{7,20},{8,27},{9,... | collective-permute-start | bytes 6291464 | tf_op jit(solution)/shard_map/ppermute | solution.py:65
  89.2 23.6 %collective-permute-start.21 = (bf16[384,1024]{1,0:T(8,128)(2,1)S(1)}, bf16[384,1024]{1,0:T(8,128)(2,1)}, u32[]{:S(2)}, u32[]{:S(2)}) collective-permute-start(bf16[384,1024]{1,0:T(8,128)(2,1)S(1)} %broadcast_select_fusion.refs_8_), channel_id=1, source_target_pairs={{0,96},{1,97},{2,98},{3,99},{4,100},{5,101},{6,102},{7,103},{8,104... | collective-permute-start | bytes 2359304 | tf_op jit(solution)/shard_map/ppermute | solution.py:65
  91.8 21.8 %collective-permute-start.24 = (bf16[384,1024]{1,0:T(8,128)(2,1)}, bf16[384,1024]{1,0:T(8,128)(2,1)}, u32[]{:S(2)}, u32[]{:S(2)}) collective-permute-start(bf16[384,1024]{1,0:T(8,128)(2,1)} %collective-permute-done.23.refs_12_), channel_id=1, source_target_pairs={{0,32},{1,33},{2,34},{3,35},{4,36},{5,37},{6,38},{7,39},{8,40},{9,... | collective-permute-start | bytes 2359304 | tf_op jit(solution)/shard_map/ppermute | solution.py:65
  91.9 37.1 %collective-permute-start.22 = (bf16[384,1024]{1,0:T(8,128)(2,1)}, bf16[384,1024]{1,0:T(8,128)(2,1)}, u32[]{:S(2)}, u32[]{:S(2)}) collective-permute-start(bf16[384,1024]{1,0:T(8,128)(2,1)} %collective-permute-done.20.refs_9_), channel_id=1, source_target_pairs={{0,32},{1,33},{2,34},{3,35},{4,36},{5,37},{6,38},{7,39},{8,40},{9,... | collective-permute-start | bytes 2359304 | tf_op jit(solution)/shard_map/ppermute | solution.py:65
  93.9 42.9 %collective-permute-start.26 = (bf16[384,1024]{1,0:T(8,128)(2,1)}, bf16[384,1024]{1,0:T(8,128)(2,1)}, u32[]{:S(2)}, u32[]{:S(2)}) collective-permute-start(bf16[384,1024]{1,0:T(8,128)(2,1)} %collective-permute-done.25.refs_14_), channel_id=1, source_target_pairs={{0,96},{1,97},{2,98},{3,99},{4,100},{5,101},{6,102},{7,103},{8,104... | collective-permute-start | bytes 2359304 | tf_op jit(solution)/shard_map/ppermute | solution.py:65
  112.9 53.6 %collective-permute-start.29 = (bf16[512,384]{1,0:T(8,128)(2,1)S(1)}, bf16[512,384]{1,0:T(8,128)(2,1)S(1)}, u32[]{:S(2)}, u32[]{:S(2)}) collective-permute-start(bf16[512,384]{1,0:T(8,128)(2,1)S(1)} %broadcast_select_fusion.1.refs_0_), channel_id=1, source_target_pairs={{0,96},{1,97},{2,98},{3,99},{4,100},{5,101},{6,102},{7,103},{8,104... | collective-permute-start | bytes 1179656 | tf_op jit(solution)/shard_map/ppermute | solution.py:65
  113.6 52.9 %collective-permute-start.32 = (bf16[512,384]{1,0:T(8,128)(2,1)}, bf16[512,384]{1,0:T(8,128)(2,1)S(1)}, u32[]{:S(2)}, u32[]{:S(2)}) collective-permute-start(bf16[512,384]{1,0:T(8,128)(2,1)} %copy-done.4), channel_id=1, source_target_pairs={{0,32},{1,33},{2,34},{3,35},{4,36},{5,37},{6,38},{7,39},{8,40},{9,... | collective-permute-start | bytes 1179656 | tf_op jit(solution)/shard_map/ppermute | solution.py:65
  114.4 52.1 %collective-permute-start.30 = (bf16[512,384]{1,0:T(8,128)(2,1)}, bf16[512,384]{1,0:T(8,128)(2,1)}, u32[]{:S(2)}, u32[]{:S(2)}) collective-permute-start(bf16[512,384]{1,0:T(8,128)(2,1)} %copy-done.5), channel_id=1, source_target_pairs={{0,32},{1,33},{2,34},{3,35},{4,36},{5,37},{6,38},{7,39},{8,40},{9,... | collective-permute-start | bytes 1179656 | tf_op jit(solution)/shard_map/ppermute | solution.py:65
  129.1 37.5 %collective-permute-start.34 = (bf16[512,384]{1,0:T(8,128)(2,1)}, bf16[512,384]{1,0:T(8,128)(2,1)}, u32[]{:S(2)}, u32[]{:S(2)}) collective-permute-start(bf16[512,384]{1,0:T(8,128)(2,1)} %copy-done.6), channel_id=1, source_target_pairs={{0,96},{1,97},{2,98},{3,99},{4,100},{5,101},{6,102},{7,103},{8,104... | collective-permute-start | bytes 1179656 | tf_op jit(solution)/shard_map/ppermute | solution.py:65
  136.8 38.0 %collective-permute-start.42 = (bf16[64,3072]{1,0:T(8,128)(2,1)}, bf16[64,3072]{1,0:T(8,128)(2,1)}, u32[]{:S(2)}, u32[]{:S(2)}) collective-permute-start(bf16[64,3072]{1,0:T(8,128)(2,1)} %param.19), channel_id=1, source_target_pairs={{0,19},{1,18},{2,17},{3,16},{4,23},{5,22},{6,21},{7,20},{8,27},{9,... | collective-permute-start | bytes 1179656 | tf_op jit(solution)/shard_map/ppermute | solution.py:65
  173.7 80.4 %collective-permute-start.38 = (bf16[256,3072]{1,0:T(8,128)(2,1)}, bf16[256,3072]{1,0:T(8,128)(2,1)S(1)}, u32[]{:S(2)}, u32[]{:S(2)}) collective-permute-start(bf16[256,3072]{1,0:T(8,128)(2,1)} %get-tuple-element.37), channel_id=1, source_target_pairs={{0,16},{1,17},{2,18},{3,19},{4,20},{5,21},{6,22},{7,23},{8,24},{9,... | collective-permute-start | bytes 4718600 | tf_op jit(solution)/shard_map/ppermute | solution.py:65
  174.8 32.0 %collective-permute-start.43 = (bf16[64,3072]{1,0:T(8,128)(2,1)}, bf16[64,3072]{1,0:T(8,128)(2,1)S(1)}, u32[]{:S(2)}, u32[]{:S(2)}) collective-permute-start(bf16[64,3072]{1,0:T(8,128)(2,1)} %collective-permute-done.42.refs_0_), channel_id=1, source_target_pairs={{0,12},{1,13},{2,14},{3,15},{4,0},{5,1},{6,2},{7,3},{8,4},{9,5},{1... | collective-permute-start | bytes 1179656 | tf_op jit(solution)/shard_map/ppermute | solution.py:65
  175.1 31.7 %collective-permute-start.44 = (bf16[64,3072]{1,0:T(8,128)(2,1)}, bf16[64,3072]{1,0:T(8,128)(2,1)S(1)}, u32[]{:S(2)}, u32[]{:S(2)}) collective-permute-start(bf16[64,3072]{1,0:T(8,128)(2,1)} %collective-permute-done.42.refs_0_), channel_id=1, source_target_pairs={{0,4},{1,5},{2,6},{3,7},{4,8},{5,9},{6,10},{7,11},{8,12},{9,13},{1... | collective-permute-start | bytes 1179656 | tf_op jit(solution)/shard_map/ppermute | solution.py:65
  203.4 52.2 %collective-permute-start.36 = (bf16[256,3072]{1,0:T(8,128)(2,1)}, bf16[256,3072]{1,0:T(8,128)(2,1)}, u32[]{:S(2)}, u32[]{:S(2)}) collective-permute-start(bf16[256,3072]{1,0:T(8,128)(2,1)} %get-tuple-element.32), channel_id=1, source_target_pairs={{0,16},{1,17},{2,18},{3,19},{4,20},{5,21},{6,22},{7,23},{8,24},{9,... | collective-permute-start | bytes 4718600 | tf_op jit(solution)/shard_map/ppermute | solution.py:65
  206.8 25.6 %collective-permute-start.47 = (bf16[64,3072]{1,0:T(8,128)(2,1)S(1)}, bf16[64,3072]{1,0:T(8,128)(2,1)S(1)}, u32[]{:S(2)}, u32[]{:S(2)}) collective-permute-start(bf16[64,3072]{1,0:T(8,128)(2,1)S(1)} %collective-permute-done.43.refs_1_), channel_id=1, source_target_pairs={{0,1},{1,0},{2,3},{3,2},{4,5},{5,4},{6,7},{7,6},{8,9},{9,8},{10,11... | collective-permute-start | bytes 1179656 | tf_op jit(solution)/shard_map/ppermute | solution.py:65
  215.5 31.8 %collective-permute-start.48 = (bf16[64,3072]{1,0:T(8,128)(2,1)S(1)}, bf16[64,3072]{1,0:T(8,128)(2,1)S(1)}, u32[]{:S(2)}, u32[]{:S(2)}) collective-permute-start(bf16[64,3072]{1,0:T(8,128)(2,1)S(1)} %collective-permute-done.44.refs_2_), channel_id=1, source_target_pairs={{0,1},{1,0},{2,3},{3,2},{4,5},{5,4},{6,7},{7,6},{8,9},{9,8},{10,11... | collective-permute-start | bytes 1179656 | tf_op jit(solution)/shard_map/ppermute | solution.py:65
  215.8 32.7 %collective-permute-start.49 = (bf16[64,3072]{1,0:T(8,128)(2,1)}, bf16[64,3072]{1,0:T(8,128)(2,1)}, u32[]{:S(2)}, u32[]{:S(2)}) collective-permute-start(bf16[64,3072]{1,0:T(8,128)(2,1)} %collective-permute-done.46.refs_4_), channel_id=1, source_target_pairs={{0,1},{1,0},{2,3},{3,2},{4,5},{5,4},{6,7},{7,6},{8,9},{9,8},{10,11... | collective-permute-start | bytes 1179656 | tf_op jit(solution)/shard_map/ppermute | solution.py:65
  248.1 29.3 %collective-permute-start.35 = (bf16[256,3072]{1,0:T(8,128)(2,1)}, bf16[256,3072]{1,0:T(8,128)(2,1)}, u32[]{:S(2)}, u32[]{:S(2)}) collective-permute-start(bf16[256,3072]{1,0:T(8,128)(2,1)} %get-tuple-element.29), channel_id=1, source_target_pairs={{0,16},{1,17},{2,18},{3,19},{4,20},{5,21},{6,22},{7,23},{8,24},{9,... | collective-permute-start | bytes 4718600 | tf_op jit(solution)/shard_map/ppermute | solution.py:65
  253.9 39.1 %collective-permute-start.50 = (bf16[128,3072]{1,0:T(8,128)(2,1)}, bf16[128,3072]{1,0:T(8,128)(2,1)S(1)}, u32[]{:S(2)}, u32[]{:S(2)}) collective-permute-start(bf16[128,3072]{1,0:T(8,128)(2,1)} %get-tuple-element.42), channel_id=1, source_target_pairs={{0,16},{1,17},{2,18},{3,19},{4,20},{5,21},{6,22},{7,23},{8,24},{9,... | collective-permute-start | bytes 2359304 | tf_op jit(solution)/shard_map/ppermute | solution.py:65
  258.0 34.9 %collective-permute-start.37 = (bf16[128,3072]{1,0:T(8,128)(2,1)S(1)}, bf16[128,3072]{1,0:T(8,128)(2,1)S(1)}, u32[]{:S(2)}, u32[]{:S(2)}) collective-permute-start(bf16[128,3072]{1,0:T(8,128)(2,1)S(1)} %get-tuple-element.33), channel_id=1, source_target_pairs={{1,0},{0,1},{3,2},{2,3},{5,4},{4,5},{7,6},{6,7},{9,8},{8,9},{11,10... | collective-permute-start | bytes 2359304 | tf_op jit(solution)/shard_map/ppermute | solution.py:65
  277.4 25.6 %collective-permute-start.40 = (bf16[128,3072]{1,0:T(8,128)(2,1)S(1)}, bf16[128,3072]{1,0:T(8,128)(2,1)S(1)}, u32[]{:S(2)}, u32[]{:S(2)}) collective-permute-start(bf16[128,3072]{1,0:T(8,128)(2,1)S(1)} %add_convert_fusion.7), channel_id=1, source_target_pairs={{4,0},{5,1},{6,2},{7,3},{8,4},{9,5},{10,6},{11,7},{12,8},{13,9},{1... | collective-permute-start | bytes 2359304 | tf_op jit(solution)/shard_map/ppermute | solution.py:65
  (76 other events, 1273.3 us)

commit v4 on v3

--- a/solution.py
+++ b/solution.py
@@ -54,9 +54,7 @@
 
 
 HALVES = ((7, 6, 5, 4), (3, 2, 1, 0))
-ROW_BLOCKS = tuple(
-    half[2 * pair + j] + 8 * part for half in HALVES for pair in range(2) for part in range(2) for j in range(2)
-)
+ROW_BLOCKS = tuple(k + 8 * part for half in HALVES for part in range(2) for k in half)
 LATE_BLOCKS = 8
 TILE = 256
 
@@ -142,11 +140,11 @@
     return across.T, across
 
 
-def rank_kernel(first, shrink, ints, *refs):
-    shards, (out, rows, sems) = refs[:-3], refs[-3:]
+def rank_kernel(first, shrink, ints, before, *refs):
+    shards, (out, total, rows, sems) = refs[:-4], refs[-4:]
     for i, shard in enumerate(shards):
         pltpu.make_async_copy(shard, rows.at[pl.ds(i * 128, 128)], sems.at[i * 128 // TILE]).start()
-    out[...] = jnp.zeros(out.shape, jnp.float32)
+    total[...] = before[...]
     fold = matching(128, 32, 128, 32)
 
     def tile(i, carry):
@@ -157,21 +155,22 @@
         values = kept(group == down[:, 5:6], contract_trailing(rows[part, :], shrink[...]))
         values = kept(group == down[:, 2:3], dot(values, fold))
         place = lax.broadcasted_iota(jnp.int32, (64, TILE), 0) == across[6:7]
-        out[...] += dot(place.astype(jnp.bfloat16), values)
+        total[...] += dot(place.astype(jnp.bfloat16), values)
         return carry
 
     lax.fori_loop(0, rows.shape[0] // TILE, tile, 0)
-
-
-def hidden_kernel(first, slab_at, ranks, ints, expand, down_shrink, *refs):
-    shards, pieces, (hidden, packed, rows, weight, to_gate, to_up, fold, row_sems, sem) = refs[:8], refs[8:16], refs[16:]
+    out[...] = jnp.broadcast_to(total[...].astype(out.dtype), out.shape)
+
+
+def hidden_kernel(first, slab_at, ranks, ints, expand, down_shrink, before, *refs):
+    shards, pieces, (hidden, packed, total, rows, weight, to_gate, to_up, fold, row_sems, sem) = refs[:8], refs[8:16], refs[16:]
     slab = pieces[0].shape[0]
     for i, piece in enumerate(pieces):
         start = pl.multiple_of(slab_at[i] * slab, 128)
         pltpu.make_async_copy(piece, weight.at[pl.ds(start, slab)], sem.at[0]).start()
     for i, shard in enumerate(shards):
         pltpu.make_async_copy(shard, rows.at[pl.ds(i * 128, 128)], row_sems.at[i * 128 // TILE]).start()
-    packed[...] = jnp.zeros(packed.shape, jnp.float32)
+    total[...] = before[...]
     to_gate[...] = matching(128, 32, 1024, 16)
     to_up[...] = matching(128, 32, 1024, 16, 16)
     fold[...] = matching(1024, 16, 128, 16)
@@ -198,14 +197,15 @@
         parts = dot(kept(chosen, contract_trailing(values, down_shrink[...])), fold[...])
         parts = kept(lanes(TILE, 128, 16) == down[:, 4:5], parts)
         place = lax.broadcasted_iota(jnp.int32, (packed.shape[0], TILE), 0) == across[3:4]
-        packed[...] += dot(place.astype(jnp.bfloat16), parts)
+        total[...] += dot(place.astype(jnp.bfloat16), parts)
         return carry
 
     lax.fori_loop(0, rows.shape[0] // TILE, tile, 0)
+    packed[...] = total[...].astype(packed.dtype)
 
 
 def down_kernel(slab_at, hidden, *refs):
-    pieces, (mine, theirs, weight, sems) = refs[:8], refs[8:]
+    pieces, (out, weight, sems) = refs[:8], refs[8:]
     slab, step = pieces[0].shape[1], pl.program_id(0)
 
     @pl.when(step == 0)
@@ -216,9 +216,7 @@
             pltpu.make_async_copy(piece, weight.at[chunk, :, pl.ds(start, slab)], sems.at[chunk]).start()
 
     pltpu.make_async_copy(weight.at[step], weight.at[step], sems.at[step]).wait()
-    both = dot(hidden[...], weight[step]).astype(jnp.bfloat16)
-    mine[...] = both[:TILE]
-    theirs[...] = both[TILE:]
+    out[...] = dot(hidden[...], weight[step]).astype(jnp.bfloat16)
 
 
 def adapter_kernel(map_slots, ranks, ints, *refs):
@@ -314,34 +312,35 @@
         name="places",
     )(jnp.stack([ci, yi, hi, li]), adapter_slot, own_adapters, send(own_adapters, CORE))
 
-    def ranks_of(first, last):
+    def ranks_of(first, last, before, out_shape):
         count = (last - first) * own_count
         return pl.pallas_call(
             functools.partial(rank_kernel, first),
-            out_shape=jax.ShapeDtypeStruct((64, 128), jnp.float32),
-            in_specs=[vmem] * 2 + [stay] * (last - first),
+            out_shape=out_shape,
+            in_specs=[vmem] * 3 + [stay] * (last - first),
             out_specs=vmem,
             scratch_shapes=[
+                pltpu.VMEM((64, 128), jnp.float32),
                 pltpu.VMEM((count, width), jnp.bfloat16),
                 pltpu.SemaphoreType.DMA((count // TILE,)),
             ],
             name="ranks",
-        )(shrink, ints, *shards[first:last])
-
-    packed = ranks_of(LATE_BLOCKS, 16) + ranks_of(0, LATE_BLOCKS)
-    spread = jnp.broadcast_to(packed.astype(jnp.bfloat16)[None], (16, 64, 128))
+        )(shrink, ints, before, *shards[first:last])
+
+    packed = jax.ShapeDtypeStruct((64, 128), jnp.float32)
+    packed = ranks_of(LATE_BLOCKS, 16, jnp.zeros((64, 128), jnp.float32), packed)
+    spread = jax.ShapeDtypeStruct((16, 64, 128), jnp.bfloat16)
+    spread = ranks_of(0, LATE_BLOCKS, packed, spread)
     ranks = lax.all_to_all(spread, GROUP, split_axis=0, concat_axis=0, tiled=True).reshape(1024, 128)
 
-    def hidden_half(i):
+    def hidden_half(i, before, kind):
         return pl.pallas_call(
             functools.partial(hidden_kernel, 8 * i),
-            out_shape=(
-                jax.ShapeDtypeStruct((half_count, units), jnp.bfloat16),
-                jax.ShapeDtypeStruct((256, 128), jnp.float32),
-            ),
-            in_specs=[smem] + [vmem] * 4 + [stay] * 16,
+            out_shape=(jax.ShapeDtypeStruct((half_count, units), jnp.bfloat16), jax.ShapeDtypeStruct((256, 128), kind)),
+            in_specs=[smem] + [vmem] * 5 + [stay] * 16,
             out_specs=(vmem, vmem),
             scratch_shapes=[
+                pltpu.VMEM((256, 128), jnp.float32),
                 pltpu.VMEM((half_count, width), jnp.bfloat16),
                 pltpu.VMEM((width, 2 * units), jnp.bfloat16),
                 pltpu.VMEM((128, 1024), jnp.bfloat16),
@@ -357,17 +356,18 @@
             ints,
             expand,
             down_shrink,
+            before,
             *shards[8 * i : 8 * i + 8],
             *gate_up,
         )
 
-    def down_quarter(hidden, i):
+    def down_part(hidden, i):
         return pl.pallas_call(
             down_kernel,
             grid=(4,),
-            out_shape=(jax.ShapeDtypeStruct((TILE, width), jnp.bfloat16),) * 2,
-            in_specs=[smem, pl.BlockSpec((2 * TILE, units), lambda g: (i, 0))] + [stay] * 8,
-            out_specs=(pl.BlockSpec((TILE, width // 4), lambda g: (0, g)),) * 2,
+            out_shape=jax.ShapeDtypeStruct((4 * own_count, width), jnp.bfloat16),
+            in_specs=[smem, pl.BlockSpec((4 * own_count, units), lambda g: (i, 0))] + [stay] * 8,
+            out_specs=pl.BlockSpec((4 * own_count, width // 4), lambda g: (0, g)),
             scratch_shapes=[pltpu.VMEM((4, units, width // 4), jnp.bfloat16), pltpu.SemaphoreType.DMA((4,))],
             name="down",
         )(slab_at, hidden, *down)
@@ -376,18 +376,17 @@
         return (left.astype(jnp.float32) + right.astype(jnp.float32)).astype(jnp.bfloat16)
 
     sums = [None] * 8
-    packed_down = []
-    for i in range(2):
-        hidden, packed = hidden_half(i)
-        packed_down.append(packed)
-        for j in range(2):
-            mine_part, theirs_part = down_quarter(hidden, j)
-            swapped = send(theirs_part, CORE)
-            added = [add(mine_part[at : at + 128], swapped[at : at + 128]) for at in (0, 128)]
-            for k, value in zip(HALVES[i][2 * j : 2 * j + 2], lax.optimization_barrier(added)):
-                sums[k] = value
-
-    packed_down = (packed_down[0] + packed_down[1]).astype(jnp.bfloat16).reshape(16, 16, 128)
+    packed_down = jnp.zeros((256, 128), jnp.float32)
+    for i, kind in enumerate((jnp.float32, jnp.bfloat16)):
+        hidden, packed_down = hidden_half(i, packed_down, kind)
+        swapped = send(down_part(hidden, 1), CORE)
+        own_part = down_part(hidden, 0)
+        spans = [slice(j * own_count, (j + 1) * own_count) for j in range(4)]
+        added = lax.optimization_barrier([add(own_part[span], swapped[span]) for span in spans])
+        for k, value in zip(HALVES[i], added):
+            sums[k] = value
+
+    packed_down = packed_down.reshape(16, 16, 128)
     arrived = lax.all_to_all(packed_down, GROUP, split_axis=0, concat_axis=0, tiled=True)
     down_ranks = jnp.sum(arrived.astype(jnp.float32), axis=0).astype(jnp.bfloat16)
     both_ranks = jnp.stack([down_ranks, send(down_ranks, CORE)])
@@ -404,8 +403,7 @@
     for k in (6, 5, 4, 3, 2, 1):
         sums[SOURCE[k]] = add(sums[SOURCE[k]], send(sums[k + 1], TREE_BACK[k]))
     last = send(sums[1], TREE_BACK[0]).astype(jnp.float32)
-    near = lax.optimization_barrier(sums[0].astype(jnp.float32) + adapter_term)
-    return (near + last).astype(jnp.bfloat16)
+    return (sums[0].astype(jnp.float32) + last + adapter_term).astype(jnp.bfloat16)
 
 
 def solution(mesh):

time: 311 us -> 330 us (1.061); the launches traced: 305 us -> 328 us
  starting transfers between devices: 73.2 us -> 94.7 us
  blocking collectives: 0 us -> 9.87 us
  waiting for transfers between devices: 114 us -> 108 us
    ppermute x56 -> x54, starting transfers between devices: 59.5 us -> 88.9 us  [send(): return lax.ppermute(value, ALL, pairs)]
    all_to_all x0 -> x1, blocking collectives: none -> 9.87 us  [local(): lax.all_to_all(packed_down, GROUP, split_axis=0, concat_axis=0, tiled=True)]
    all_to_all x1 -> x0, starting transfers between devices: 7.44 us -> none  [local(): lax.all_to_all(packed_down, GROUP, split_axis=0, concat_axis=0, tiled=True)]
    all_to_all x1 -> x0, waiting for transfers between devices: 5.8 us -> none  [local(): lax.all_to_all(packed_down, GROUP, split_axis=0, concat_axis=0, tiled=True)]
    unnamed x85 -> x77, local copies, waits for them, and re-layouts: 6.74 us -> 4.33 us
    convert_element_type x7 -> x5, other arithmetic: 7.27 us -> 9.4 us  [add(): (left.astype(jnp.float32) + right.astype(jnp.float32)).astype(jnp.bfloat16)]
    ppermute x56 -> x54, waiting for transfers between devices: 101 us -> 101 us  [send(): return lax.ppermute(value, ALL, pairs)]
  transfers between devices with their start and end apart: 58 -> 55, of which waited for: 20 -> 22; matrix products, arithmetic and copies ran while one was open for 7% -> 6% of each run, Pallas kernels for 29% -> 26%
where the time goes in v4:
time: 330 us; the launch traced here: 328 us
  waiting for transfers between devices  108 us (33%)
  starting transfers between devices  94.7 us (29%)
  Pallas kernels  90.4 us (27%)
  other arithmetic  17.3 us (5%)
  blocking collectives  9.87 us (3%)
  local copies, waits for them, and re-layouts  7.76 us (2%)
    ppermute x54, waiting for transfers between devices, send(): return lax.ppermute(value, ALL, pairs)  101 us
    ppermute x54, starting transfers between devices, send(): return lax.ppermute(value, ALL, pairs)  88.9 us
    pallas_call x2, Pallas kernels, hidden_half(): pl.pallas_call(functools.partial(hidden_kernel, 8 * i), out_shape=(jax.Sh...  43.7 us
    pallas_call x4, Pallas kernels, down_part(): pl.pallas_call(down_kernel, grid=(4,), out_shape=jax.ShapeDtypeStruct((4...  25.2 us
    pallas_call x2, Pallas kernels, ranks_of(): pl.pallas_call(functools.partial(rank_kernel, first), out_shape=out_shape...  14.3 us
    all_to_all x1, blocking collectives, local(): lax.all_to_all(packed_down, GROUP, split_axis=0, concat_axis=0, tiled=True)  9.87 us
    convert_element_type x5, other arithmetic, add(): (left.astype(jnp.float32) + right.astype(jnp.float32)).astype(jnp.bfloat16)  9.4 us
  transfers between devices with their start and end apart: 55, of which 22 were waited for; matrix products, arithmetic and copies ran while one was open for 6% of the time, Pallas kernels for 26%

profile of v4, /device:TPU:1, one launch (start us, length us, event | category | flops | bytes accessed | tf_op | source)
XLA Modules:
  0.0 328.4 jit_solution(9731136530161484169)
XLA Ops:
  7.2 5.7 %collective-permute-start.27 = (bf16[512,384]{1,0:T(8,128)(2,1)S(1)}, bf16[512,384]{1,0:T(8,128)(2,1)S(1)}, u32[]{:S(2)}, u32[]{:S(2)}) collective-permute-start(bf16[512,384]{1,0:T(8,128)(2,1)S(1)} %copy-done.30), channel_id=1, source_target_pairs={{16,19},{17,18},{18,17},{19,16},{20,23},{21,22},{22,21},{23,20},{2... | collective-permute-start | bytes 1179656 | tf_op jit(solution)/shard_map/ppermute | solution.py:63
  15.2 6.6 %collective-permute-done.27 = bf16[512,384]{1,0:T(8,128)(2,1)S(1)} collective-permute-done((bf16[512,384]{1,0:T(8,128)(2,1)S(1)}, bf16[512,384]{1,0:T(8,128)(2,1)S(1)}, u32[]{:S(2)}, u32[]{:S(2)}) %collective-permute-start.27) | collective-permute-done | bytes 393248 | tf_op jit(solution)/shard_map/ppermute | solution.py:63
  28.3 6.1 %collective-permute-done.3.refs_1_ = bf16[128,3072]{1,0:T(8,128)(2,1)S(1)} collective-permute-done((bf16[128,3072]{1,0:T(8,128)(2,1)S(1)}, bf16[128,3072]{1,0:T(8,128)(2,1)S(1)}, u32[]{:S(2)}, u32[]{:S(2)}) %collective-permute-start.3) | collective-permute-done | bytes 786464 | tf_op jit(solution)/shard_map/ppermute | solution.py:63
  38.8 6.0 %collective-permute-done.19 = bf16[384,1024]{1,0:T(8,128)(2,1)} collective-permute-done((bf16[384,1024]{1,0:T(8,128)(2,1)}, bf16[384,1024]{1,0:T(8,128)(2,1)}, u32[]{:S(2)}, u32[]{:S(2)}) %collective-permute-start.19) | collective-permute-done | bytes 786464 | tf_op jit(solution)/shard_map/ppermute | solution.py:63
  49.6 8.4 %collective-permute-done.33.refs_6_ = bf16[512,384]{1,0:T(8,128)(2,1)} collective-permute-done((bf16[512,384]{1,0:T(8,128)(2,1)}, bf16[512,384]{1,0:T(8,128)(2,1)}, u32[]{:S(2)}, u32[]{:S(2)}) %collective-permute-start.33) | collective-permute-done | bytes 393248 | tf_op jit(solution)/shard_map/ppermute | solution.py:63
  74.4 5.3 %collective-permute-done.11.refs_1_ = bf16[128,3072]{1,0:T(8,128)(2,1)S(1)} collective-permute-done((bf16[128,3072]{1,0:T(8,128)(2,1)}, bf16[128,3072]{1,0:T(8,128)(2,1)S(1)}, u32[]{:S(2)}, u32[]{:S(2)}) %collective-permute-start.11) | collective-permute-done | bytes 786464 | tf_op jit(solution)/shard_map/ppermute | solution.py:63
  85.6 16.6 %collective-permute-start.14 = (bf16[128,3072]{1,0:T(8,128)(2,1)S(1)}, bf16[128,3072]{1,0:T(8,128)(2,1)S(1)}, u32[]{:S(2)}, u32[]{:S(2)}) collective-permute-start(bf16[128,3072]{1,0:T(8,128)(2,1)S(1)} %collective-permute-done.11.refs_1_), channel_id=1, source_target_pairs={{0,16},{1,17},{2,18},{3,19},{4,20},{5,21},{6,22},{7,23},{8,24},{9,... | collective-permute-start | bytes 2359304 | tf_op jit(solution)/shard_map/ppermute | solution.py:63
  103.6 7.1 %collective-permute-start.16 = (bf16[128,3072]{1,0:T(8,128)(2,1)S(1)}, bf16[128,3072]{1,0:T(8,128)(2,1)S(1)}, u32[]{:S(2)}, u32[]{:S(2)}) collective-permute-start(bf16[128,3072]{1,0:T(8,128)(2,1)S(1)} %collective-permute-done.9.refs_3_), channel_id=1, source_target_pairs={{0,16},{1,17},{2,18},{3,19},{4,20},{5,21},{6,22},{7,23},{8,24},{9,... | collective-permute-start | bytes 2359304 | tf_op jit(solution)/shard_map/ppermute | solution.py:63
  116.1 15.9 %collective-permute-done.22.refs_11_ = bf16[384,1024]{1,0:T(8,128)(2,1)S(1)} collective-permute-done((bf16[384,1024]{1,0:T(8,128)(2,1)S(1)}, bf16[384,1024]{1,0:T(8,128)(2,1)S(1)}, u32[]{:S(2)}, u32[]{:S(2)}) %collective-permute-start.22) | collective-permute-done | bytes 786464 | tf_op jit(solution)/shard_map/ppermute | solution.py:63
  138.7 7.1 %ranks.2.before = f32[64,128]{1,0:T(8,128)} custom-call(bf16[128,3072]{1,0:T(8,128)(2,1)} %copy-done.25, s32[16,8,128]{2,1,0:T(8,128)} %places.1.ints, f32[64,128]{1,0:T(8,128)} %broadcast_in_dim.8.before, bf16[128,3072]{1,0:T(8,128)(2,1)} %copy-done.12, bf16[128,3072]{1,0:T(8,128)(2,1)} %copy-done.13, bf16[128,3072]{1,0:T(8,128)(2,1)} %collective-permute-done.4.refs_2_, ...), custom_call_target="tpu_custom_call" | custom-call | tf_op jit(solution)/shard_map/ranks/pallas_call | solution.py:317
  145.8 7.2 %ranks.3 = bf16[16,64,128]{2,1,0:T(8,128)(2,1)} custom-call(bf16[128,3072]{1,0:T(8,128)(2,1)} %copy-done.25, s32[16,8,128]{2,1,0:T(8,128)} %places.1.ints, f32[64,128]{1,0:T(8,128)} %ranks.2.before, bf16[128,3072]{1,0:T(8,128)(2,1)} %copy-done.20, bf16[128,3072]{1,0:T(8,128)(2,1)} %copy-done.18, bf16[128,3072]{1,0:T(8,128)(2,1)} %copy-done.19, ...), custom_call_target="tpu_custom_call" | custom-call | tf_op jit(solution)/shard_map/ranks/pallas_call | solution.py:317
  153.0 5.8 %all-to-all-start = ((bf16[16,64,128]{2,1,0:T(8,128)(2,1)}), bf16[16,64,128]{2,1,0:T(8,128)(2,1)S(1)}, u32[]{:S(2)}, u32[]{:S(2)}) async-start(bf16[16,64,128]{2,1,0:T(8,128)(2,1)} %ranks.3), calls=%async_computation | async-start | bytes 524288 | tf_op jit(solution)/shard_map/all_to_all | solution.py:334
  159.5 6.5 %all-to-all-done = bf16[16,64,128]{2,1,0:T(8,128)(2,1)S(1)} async-done(((bf16[16,64,128]{2,1,0:T(8,128)(2,1)}), bf16[16,64,128]{2,1,0:T(8,128)(2,1)S(1)}, u32[]{:S(2)}, u32[]{:S(2)}) %all-to-all-start) | async-done | bytes 262176 | tf_op jit(solution)/shard_map/all_to_all | solution.py:334
  166.8 21.8 %hidden.2 = (bf16[1024,512]{1,0:T(8,128)(2,1)}, f32[256,128]{1,0:T(8,128)}) custom-call(s32[8]{0:T(128)} %stack.86.slab_at, bf16[1024,128]{1,0:T(8,128)(2,1)} %bitcast.25, s32[16,8,128]{2,1,0:T(8,128)} %places.1.ints, bf16[2,1024,512]{2,1,0:T(8,128)(2,1)} %copy-done.2, bf16[1024,512]{1,0:T(8,128)(2,1)} %copy-done.5, f32[256,128]{1,0:T(8,128)} %broadcast_in_dim.9.before, ...), custom_call_target="tpu_custom_call" | custom-call | tf_op jit(solution)/shard_map/hidden/pallas_call | solution.py:337
  188.7 6.3 %down.7 = bf16[512,3072]{1,0:T(8,128)(2,1)} custom-call(s32[8]{0:T(128)} %stack.86.slab_at, bf16[1024,512]{1,0:T(8,128)(2,1)} %get-tuple-element.24.hidden, bf16[512,384]{1,0:T(8,128)(2,1)} %copy-done.1, bf16[512,384]{1,0:T(8,128)(2,1)} %collective-permute-done.28.refs_1_, bf16[512,384]{1,0:T(8,128)(2,1)} %collective-permute-done.29.refs_2_, ...), custom_call_target="tpu_custom_call" | custom-call | tf_op jit(solution)/shard_map/down/pallas_call | solution.py:365
  196.2 21.8 %hidden.3 = (bf16[1024,512]{1,0:T(8,128)(2,1)}, bf16[256,128]{1,0:T(8,128)(2,1)}) custom-call(s32[8]{0:T(128)} %stack.86.slab_at, bf16[1024,128]{1,0:T(8,128)(2,1)} %bitcast.26, s32[16,8,128]{2,1,0:T(8,128)} %places.1.ints, bf16[2,1024,512]{2,1,0:T(8,128)(2,1)} %copy-done.2, bf16[1024,512]{1,0:T(8,128)(2,1)} %copy-done.5, ...), custom_call_target="tpu_custom_call" | custom-call | tf_op jit(solution)/shard_map/hidden/pallas_call | solution.py:337
  218.0 6.3 %down.5 = bf16[512,3072]{1,0:T(8,128)(2,1)} custom-call(s32[8]{0:T(128)} %stack.86.slab_at, bf16[1024,512]{1,0:T(8,128)(2,1)} %get-tuple-element.20.hidden, bf16[512,384]{1,0:T(8,128)(2,1)} %copy-done.1, bf16[512,384]{1,0:T(8,128)(2,1)} %collective-permute-done.28.refs_1_, bf16[512,384]{1,0:T(8,128)(2,1)} %collective-permute-done.29.refs_2_, ...), custom_call_target="tpu_custom_call" | custom-call | tf_op jit(solution)/shard_map/down/pallas_call | solution.py:365
  224.9 8.2 %collective-permute-done.45.refs_0_ = bf16[64,3072]{1,0:T(8,128)(2,1)S(1)} collective-permute-done((bf16[64,3072]{1,0:T(8,128)(2,1)}, bf16[64,3072]{1,0:T(8,128)(2,1)S(1)}, u32[]{:S(2)}, u32[]{:S(2)}) %collective-permute-start.45) | collective-permute-done | bytes 393248 | tf_op jit(solution)/shard_map/ppermute | solution.py:63
  235.8 8.0 %collective-permute-done.46.refs_1_ = bf16[64,3072]{1,0:T(8,128)(2,1)} collective-permute-done((bf16[64,3072]{1,0:T(8,128)(2,1)S(1)}, bf16[64,3072]{1,0:T(8,128)(2,1)}, u32[]{:S(2)}, u32[]{:S(2)}) %collective-permute-start.46) | collective-permute-done | bytes 393248 | tf_op jit(solution)/shard_map/ppermute | solution.py:63
  244.1 6.3 %down.6 = bf16[512,3072]{1,0:T(8,128)(2,1)} custom-call(s32[8]{0:T(128)} %stack.86.slab_at, bf16[1024,512]{1,0:T(8,128)(2,1)} %get-tuple-element.24.hidden, bf16[512,384]{1,0:T(8,128)(2,1)} %copy-done.1, bf16[512,384]{1,0:T(8,128)(2,1)} %collective-permute-done.28.refs_1_, bf16[512,384]{1,0:T(8,128)(2,1)} %collective-permute-done.29.refs_2_, ...), custom_call_target="tpu_custom_call" | custom-call | tf_op jit(solution)/shard_map/down/pallas_call | solution.py:365
  257.1 9.9 %all_to_all.10 = bf16[16,16,128]{2,1,0:T(8,128)(2,1)S(1)} all-to-all(bf16[16,16,128]{2,1,0:T(8,128)(2,1)S(1)} %bitcast.27), channel_id=1, replica_groups=mesh['x'=4,'c'=2,'y'=4,'h'=2,'l'=2] {'c','y','l'}, dimensions={0} | all-to-all | bytes 131072 | tf_op jit(solution)/shard_map/all_to_all | solution.py:390
  271.7 6.3 %down.4 = bf16[512,3072]{1,0:T(8,128)(2,1)} custom-call(s32[8]{0:T(128)} %stack.86.slab_at, bf16[1024,512]{1,0:T(8,128)(2,1)} %get-tuple-element.20.hidden, bf16[512,384]{1,0:T(8,128)(2,1)} %copy-done.1, bf16[512,384]{1,0:T(8,128)(2,1)} %collective-permute-done.28.refs_1_, bf16[512,384]{1,0:T(8,128)(2,1)} %collective-permute-done.29.refs_2_, ...), custom_call_target="tpu_custom_call" | custom-call | tf_op jit(solution)/shard_map/down/pallas_call | solution.py:365
  283.1 5.4 %adapters.1 = (bf16[128,3072]{1,0:T(8,128)(2,1)}, bf16[128,3072]{1,0:T(8,128)(2,1)}) custom-call(s32[8]{0:T(128)} %stack.100.map_slots, bf16[2,16,128]{2,1,0:T(8,128)(2,1)} %pad_maximum_fusion.ranks, s32[16,8,128]{2,1,0:T(8,128)} %places.1.ints, bf16[64,3072]{1,0:T(8,128)(2,1)} %copy-done.32, bf16[64,3072]{1,0:T(8,128)(2,1)} %collective-permute-done.46.refs_1_, ...), custom_call_target="tpu_custom_call" | custom-call | tf_op jit(solution)/shard_map/adapters/pallas_call | solution.py:393
  312.2 7.2 %collective-permute-done.36 = bf16[128,3072]{1,0:T(8,128)(2,1)S(1)} collective-permute-done((bf16[128,3072]{1,0:T(8,128)(2,1)S(1)}, bf16[128,3072]{1,0:T(8,128)(2,1)S(1)}, u32[]{:S(2)}, u32[]{:S(2)}) %collective-permute-start.36) | collective-permute-done | bytes 786464 | tf_op jit(solution)/shard_map/ppermute | solution.py:63
  (193 shorter events, 116.0 us)
Async XLA Ops:
  0.0 23.8 %collective-permute-start = (bf16[128,3072]{1,0:T(8,128)(2,1)}, bf16[128,3072]{1,0:T(8,128)(2,1)S(1)}, u32[]{:S(2)}, u32[]{:S(2)}) collective-permute-start(bf16[128,3072]{1,0:T(8,128)(2,1)} %param.16), channel_id=1, source_target_pairs={{0,19},{1,18},{2,17},{3,16},{4,23},{5,22},{6,21},{7,20},{8,27},{9,... | collective-permute-start | bytes 2359304 | tf_op jit(solution)/shard_map/ppermute | solution.py:63
  4.3 23.9 %collective-permute-start.2 = (bf16[128,3072]{1,0:T(8,128)(2,1)S(1)}, bf16[128,3072]{1,0:T(8,128)(2,1)S(1)}, u32[]{:S(2)}, u32[]{:S(2)}) collective-permute-start(bf16[128,3072]{1,0:T(8,128)(2,1)S(1)} %fusion.2.refs_3_), channel_id=1, source_target_pairs={{0,1},{1,0},{2,3},{3,2},{4,5},{5,4},{6,7},{7,6},{8,9},{9,8},{10,11... | collective-permute-start | bytes 2359304 | tf_op jit(solution)/shard_map/ppermute | solution.py:63
  34.3 24.2 %collective-permute-start.18 = (bf16[1024,512]{1,0:T(8,128)(2,1)}, bf16[1024,512]{1,0:T(8,128)(2,1)S(1)}, u32[]{:S(2)}, u32[]{:S(2)}) collective-permute-start(bf16[1024,512]{1,0:T(8,128)(2,1)} %param.18), channel_id=1, source_target_pairs={{0,19},{1,18},{2,17},{3,16},{4,23},{5,22},{6,21},{7,20},{8,27},{9,... | collective-permute-start | bytes 3145736 | tf_op jit(solution)/shard_map/ppermute | solution.py:63
  37.9 21.7 %collective-permute-start.5 = (bf16[128,3072]{1,0:T(8,128)(2,1)}, bf16[128,3072]{1,0:T(8,128)(2,1)S(1)}, u32[]{:S(2)}, u32[]{:S(2)}) collective-permute-start(bf16[128,3072]{1,0:T(8,128)(2,1)} %copy-done.12), channel_id=1, source_target_pairs={{0,16},{1,17},{2,18},{3,19},{4,20},{5,21},{6,22},{7,23},{8,24},{9,... | collective-permute-start | bytes 2359304 | tf_op jit(solution)/shard_map/ppermute | solution.py:63
  57.9 52.7 %collective-permute-start.17 = (bf16[2,1024,512]{2,1,0:T(8,128)(2,1)}, bf16[2,1024,512]{2,1,0:T(8,128)(2,1)S(1)}, u32[]{:S(2)}, u32[]{:S(2)}) collective-permute-start(bf16[2,1024,512]{2,1,0:T(8,128)(2,1)} %param.17), channel_id=1, source_target_pairs={{0,19},{1,18},{2,17},{3,16},{4,23},{5,22},{6,21},{7,20},{8,27},{9,... | collective-permute-start | bytes 6291464 | tf_op jit(solution)/shard_map/ppermute | solution.py:63
  79.7 22.6 %collective-permute-start.24 = (bf16[384,1024]{1,0:T(8,128)(2,1)S(1)}, bf16[384,1024]{1,0:T(8,128)(2,1)S(1)}, u32[]{:S(2)}, u32[]{:S(2)}) collective-permute-start(bf16[384,1024]{1,0:T(8,128)(2,1)S(1)} %copy-done.7), channel_id=1, source_target_pairs={{0,32},{1,33},{2,34},{3,35},{4,36},{5,37},{6,38},{7,39},{8,40},{9,... | collective-permute-start | bytes 2359304 | tf_op jit(solution)/shard_map/ppermute | solution.py:63
  81.3 22.3 %collective-permute-start.25 = (bf16[384,1024]{1,0:T(8,128)(2,1)S(1)}, bf16[384,1024]{1,0:T(8,128)(2,1)}, u32[]{:S(2)}, u32[]{:S(2)}) collective-permute-start(bf16[384,1024]{1,0:T(8,128)(2,1)S(1)} %copy-done.7), channel_id=1, source_target_pairs={{0,96},{1,97},{2,98},{3,99},{4,100},{5,101},{6,102},{7,103},{8,104... | collective-permute-start | bytes 2359304 | tf_op jit(solution)/shard_map/ppermute | solution.py:63
  84.5 26.2 %collective-permute-start.10 = (bf16[128,3072]{1,0:T(8,128)(2,1)S(1)}, bf16[128,3072]{1,0:T(8,128)(2,1)S(1)}, u32[]{:S(2)}, u32[]{:S(2)}) collective-permute-start(bf16[128,3072]{1,0:T(8,128)(2,1)S(1)} %collective-permute-done.9.refs_3_), channel_id=1, source_target_pairs={{0,1},{1,0},{2,3},{3,2},{4,5},{5,4},{6,7},{7,6},{8,9},{9,8},{10,11... | collective-permute-start | bytes 2359304 | tf_op jit(solution)/shard_map/ppermute | solution.py:63
  85.6 25.5 %collective-permute-start.14 = (bf16[128,3072]{1,0:T(8,128)(2,1)S(1)}, bf16[128,3072]{1,0:T(8,128)(2,1)S(1)}, u32[]{:S(2)}, u32[]{:S(2)}) collective-permute-start(bf16[128,3072]{1,0:T(8,128)(2,1)S(1)} %collective-permute-done.11.refs_1_), channel_id=1, source_target_pairs={{0,16},{1,17},{2,18},{3,19},{4,20},{5,21},{6,22},{7,23},{8,24},{9,... | collective-permute-start | bytes 2359304 | tf_op jit(solution)/shard_map/ppermute | solution.py:63
  110.7 21.4 %collective-permute-start.22 = (bf16[384,1024]{1,0:T(8,128)(2,1)S(1)}, bf16[384,1024]{1,0:T(8,128)(2,1)S(1)}, u32[]{:S(2)}, u32[]{:S(2)}) collective-permute-start(bf16[384,1024]{1,0:T(8,128)(2,1)S(1)} %collective-permute-done.20.refs_9_), channel_id=1, source_target_pairs={{0,32},{1,33},{2,34},{3,35},{4,36},{5,37},{6,38},{7,39},{8,40},{9,... | collective-permute-start | bytes 2359304 | tf_op jit(solution)/shard_map/ppermute | solution.py:63
  110.7 21.3 %collective-permute-start.13 = (bf16[128,3072]{1,0:T(8,128)(2,1)S(1)}, bf16[128,3072]{1,0:T(8,128)(2,1)S(1)}, u32[]{:S(2)}, u32[]{:S(2)}) collective-permute-start(bf16[128,3072]{1,0:T(8,128)(2,1)S(1)} %collective-permute-done.10.refs_0_), channel_id=1, source_target_pairs={{0,16},{1,17},{2,18},{3,19},{4,20},{5,21},{6,22},{7,23},{8,24},{9,... | collective-permute-start | bytes 2359304 | tf_op jit(solution)/shard_map/ppermute | solution.py:63
  111.1 48.4 %collective-permute-start.26 = (bf16[384,1024]{1,0:T(8,128)(2,1)}, bf16[384,1024]{1,0:T(8,128)(2,1)}, u32[]{:S(2)}, u32[]{:S(2)}) collective-permute-start(bf16[384,1024]{1,0:T(8,128)(2,1)} %collective-permute-done.25.refs_14_), channel_id=1, source_target_pairs={{0,96},{1,97},{2,98},{3,99},{4,100},{5,101},{6,102},{7,103},{8,104... | collective-permute-start | bytes 2359304 | tf_op jit(solution)/shard_map/ppermute | solution.py:63
  114.4 74.2 %collective-permute-start.29 = (bf16[512,384]{1,0:T(8,128)(2,1)S(1)}, bf16[512,384]{1,0:T(8,128)(2,1)}, u32[]{:S(2)}, u32[]{:S(2)}) collective-permute-start(bf16[512,384]{1,0:T(8,128)(2,1)S(1)} %broadcast_select_fusion.1.refs_0_), channel_id=1, source_target_pairs={{0,96},{1,97},{2,98},{3,99},{4,100},{5,101},{6,102},{7,103},{8,104... | collective-permute-start | bytes 1179656 | tf_op jit(solution)/shard_map/ppermute | solution.py:63
  116.1 72.6 %collective-permute-start.32 = (bf16[512,384]{1,0:T(8,128)(2,1)}, bf16[512,384]{1,0:T(8,128)(2,1)}, u32[]{:S(2)}, u32[]{:S(2)}) collective-permute-start(bf16[512,384]{1,0:T(8,128)(2,1)} %collective-permute-done.31.refs_4_), channel_id=1, source_target_pairs={{0,32},{1,33},{2,34},{3,35},{4,36},{5,37},{6,38},{7,39},{8,40},{9,... | collective-permute-start | bytes 1179656 | tf_op jit(solution)/shard_map/ppermute | solution.py:63
  132.1 56.6 %collective-permute-start.30 = (bf16[512,384]{1,0:T(8,128)(2,1)}, bf16[512,384]{1,0:T(8,128)(2,1)}, u32[]{:S(2)}, u32[]{:S(2)}) collective-permute-start(bf16[512,384]{1,0:T(8,128)(2,1)} %collective-permute-done.28.refs_1_), channel_id=1, source_target_pairs={{0,32},{1,33},{2,34},{3,35},{4,36},{5,37},{6,38},{7,39},{8,40},{9,... | collective-permute-start | bytes 1179656 | tf_op jit(solution)/shard_map/ppermute | solution.py:63
  133.8 54.9 %collective-permute-start.34 = (bf16[512,384]{1,0:T(8,128)(2,1)}, bf16[512,384]{1,0:T(8,128)(2,1)}, u32[]{:S(2)}, u32[]{:S(2)}) collective-permute-start(bf16[512,384]{1,0:T(8,128)(2,1)} %collective-permute-done.33.refs_6_), channel_id=1, source_target_pairs={{0,96},{1,97},{2,98},{3,99},{4,100},{5,101},{6,102},{7,103},{8,104... | collective-permute-start | bytes 1179656 | tf_op jit(solution)/shard_map/ppermute | solution.py:63
  195.0 55.3 %collective-permute-start.37 = (bf16[512,3072]{1,0:T(8,128)(2,1)}, bf16[512,3072]{1,0:T(8,128)(2,1)S(1)}, u32[]{:S(2)}, u32[]{:S(2)}) collective-permute-start(bf16[512,3072]{1,0:T(8,128)(2,1)} %down.7), channel_id=1, source_target_pairs={{0,16},{1,17},{2,18},{3,19},{4,20},{5,21},{6,22},{7,23},{8,24},{9,... | collective-permute-start | bytes 9437192 | tf_op jit(solution)/shard_map/ppermute | solution.py:63
  224.3 71.7 %collective-permute-start.35 = (bf16[512,3072]{1,0:T(8,128)(2,1)}, bf16[512,3072]{1,0:T(8,128)(2,1)}, u32[]{:S(2)}, u32[]{:S(2)}) collective-permute-start(bf16[512,3072]{1,0:T(8,128)(2,1)} %down.5), channel_id=1, source_target_pairs={{0,16},{1,17},{2,18},{3,19},{4,20},{5,21},{6,22},{7,23},{8,24},{9,... | collective-permute-start | bytes 9437192 | tf_op jit(solution)/shard_map/ppermute | solution.py:63
  233.1 33.9 %collective-permute-start.47 = (bf16[64,3072]{1,0:T(8,128)(2,1)S(1)}, bf16[64,3072]{1,0:T(8,128)(2,1)}, u32[]{:S(2)}, u32[]{:S(2)}) collective-permute-start(bf16[64,3072]{1,0:T(8,128)(2,1)S(1)} %collective-permute-done.45.refs_0_), channel_id=1, source_target_pairs={{0,4},{1,5},{2,6},{3,7},{4,8},{5,9},{6,10},{7,11},{8,12},{9,13},{1... | collective-permute-start | bytes 1179656 | tf_op jit(solution)/shard_map/ppermute | solution.py:63
  233.4 33.7 %collective-permute-start.48 = (bf16[64,3072]{1,0:T(8,128)(2,1)S(1)}, bf16[64,3072]{1,0:T(8,128)(2,1)}, u32[]{:S(2)}, u32[]{:S(2)}) collective-permute-start(bf16[64,3072]{1,0:T(8,128)(2,1)S(1)} %collective-permute-done.45.refs_0_), channel_id=1, source_target_pairs={{0,1},{1,0},{2,3},{3,2},{4,5},{5,4},{6,7},{7,6},{8,9},{9,8},{10,11... | collective-permute-start | bytes 1179656 | tf_op jit(solution)/shard_map/ppermute | solution.py:63
  243.8 27.0 %collective-permute-start.49 = (bf16[64,3072]{1,0:T(8,128)(2,1)}, bf16[64,3072]{1,0:T(8,128)(2,1)}, u32[]{:S(2)}, u32[]{:S(2)}) collective-permute-start(bf16[64,3072]{1,0:T(8,128)(2,1)} %collective-permute-done.46.refs_1_), channel_id=1, source_target_pairs={{0,12},{1,13},{2,14},{3,15},{4,0},{5,1},{6,2},{7,3},{8,4},{9,5},{1... | collective-permute-start | bytes 1179656 | tf_op jit(solution)/shard_map/ppermute | solution.py:63
  254.7 38.2 %collective-permute-start.41 = (bf16[128,3072]{1,0:T(8,128)(2,1)}, bf16[128,3072]{1,0:T(8,128)(2,1)}, u32[]{:S(2)}, u32[]{:S(2)}) collective-permute-start(bf16[128,3072]{1,0:T(8,128)(2,1)} %get-tuple-element.29), channel_id=1, source_target_pairs={{1,0},{0,1},{3,2},{2,3},{5,4},{4,5},{7,6},{6,7},{9,8},{8,9},{11,10... | collective-permute-start | bytes 2359304 | tf_op jit(solution)/shard_map/ppermute | solution.py:63
  288.6 23.6 %collective-permute-start.53 = (bf16[128,3072]{1,0:T(8,128)(2,1)}, bf16[128,3072]{1,0:T(8,128)(2,1)S(1)}, u32[]{:S(2)}, u32[]{:S(2)}) collective-permute-start(bf16[128,3072]{1,0:T(8,128)(2,1)} %get-tuple-element.32), channel_id=1, source_target_pairs={{0,16},{1,17},{2,18},{3,19},{4,20},{5,21},{6,22},{7,23},{8,24},{9,... | collective-permute-start | bytes 2359304 | tf_op jit(solution)/shard_map/ppermute | solution.py:63
  302.3 21.5 %collective-permute-start.39 = (bf16[128,3072]{1,0:T(8,128)(2,1)S(1)}, bf16[128,3072]{1,0:T(8,128)(2,1)S(1)}, u32[]{:S(2)}, u32[]{:S(2)}) collective-permute-start(bf16[128,3072]{1,0:T(8,128)(2,1)S(1)} %add_convert_fusion.5), channel_id=1, source_target_pairs={{4,0},{5,1},{6,2},{7,3},{8,4},{9,5},{10,6},{11,7},{12,8},{13,9},{1... | collective-permute-start | bytes 2359304 | tf_op jit(solution)/shard_map/ppermute | solution.py:63
  (69 other events, 1347.0 us)

commit v5 on v4

--- a/solution.py
+++ b/solution.py
@@ -54,7 +54,9 @@
 
 
 HALVES = ((7, 6, 5, 4), (3, 2, 1, 0))
-ROW_BLOCKS = tuple(k + 8 * part for half in HALVES for part in range(2) for k in half)
+ROW_BLOCKS = tuple(
+    half[2 * pair + j] + 8 * part for half in HALVES for pair in range(2) for part in range(2) for j in range(2)
+)
 LATE_BLOCKS = 8
 TILE = 256
 
@@ -196,7 +198,7 @@
         hidden[part, :] = values
         parts = dot(kept(chosen, contract_trailing(values, down_shrink[...])), fold[...])
         parts = kept(lanes(TILE, 128, 16) == down[:, 4:5], parts)
-        place = lax.broadcasted_iota(jnp.int32, (packed.shape[0], TILE), 0) == across[3:4]
+        place = lax.broadcasted_iota(jnp.int32, (total.shape[0], TILE), 0) == across[3:4]
         total[...] += dot(place.astype(jnp.bfloat16), parts)
         return carry
 
@@ -205,7 +207,7 @@
 
 
 def down_kernel(slab_at, hidden, *refs):
-    pieces, (out, weight, sems) = refs[:8], refs[8:]
+    pieces, (mine, theirs, weight, sems) = refs[:8], refs[8:]
     slab, step = pieces[0].shape[1], pl.program_id(0)
 
     @pl.when(step == 0)
@@ -216,7 +218,9 @@
             pltpu.make_async_copy(piece, weight.at[chunk, :, pl.ds(start, slab)], sems.at[chunk]).start()
 
     pltpu.make_async_copy(weight.at[step], weight.at[step], sems.at[step]).wait()
-    out[...] = dot(hidden[...], weight[step]).astype(jnp.bfloat16)
+    both = dot(hidden[...], weight[step]).astype(jnp.bfloat16)
+    mine[...] = both[:TILE]
+    theirs[...] = both[TILE:]
 
 
 def adapter_kernel(map_slots, ranks, ints, *refs):
@@ -361,13 +365,13 @@
             *gate_up,
         )
 
-    def down_part(hidden, i):
+    def down_quarter(hidden, i):
         return pl.pallas_call(
             down_kernel,
             grid=(4,),
-            out_shape=jax.ShapeDtypeStruct((4 * own_count, width), jnp.bfloat16),
-            in_specs=[smem, pl.BlockSpec((4 * own_count, units), lambda g: (i, 0))] + [stay] * 8,
-            out_specs=pl.BlockSpec((4 * own_count, width // 4), lambda g: (0, g)),
+            out_shape=(jax.ShapeDtypeStruct((TILE, width), jnp.bfloat16),) * 2,
+            in_specs=[smem, pl.BlockSpec((2 * TILE, units), lambda g: (i, 0))] + [stay] * 8,
+            out_specs=(pl.BlockSpec((TILE, width // 4), lambda g: (0, g)),) * 2,
             scratch_shapes=[pltpu.VMEM((4, units, width // 4), jnp.bfloat16), pltpu.SemaphoreType.DMA((4,))],
             name="down",
         )(slab_at, hidden, *down)
@@ -379,12 +383,12 @@
     packed_down = jnp.zeros((256, 128), jnp.float32)
     for i, kind in enumerate((jnp.float32, jnp.bfloat16)):
         hidden, packed_down = hidden_half(i, packed_down, kind)
-        swapped = send(down_part(hidden, 1), CORE)
-        own_part = down_part(hidden, 0)
-        spans = [slice(j * own_count, (j + 1) * own_count) for j in range(4)]
-        added = lax.optimization_barrier([add(own_part[span], swapped[span]) for span in spans])
-        for k, value in zip(HALVES[i], added):
-            sums[k] = value
+        for j in range(2):
+            mine_part, theirs_part = down_quarter(hidden, j)
+            swapped = send(theirs_part, CORE)
+            added = [add(mine_part[at : at + 128], swapped[at : at + 128]) for at in (0, 128)]
+            for k, value in zip(HALVES[i][2 * j : 2 * j + 2], lax.optimization_barrier(added)):
+                sums[k] = value
 
     packed_down = packed_down.reshape(16, 16, 128)
     arrived = lax.all_to_all(packed_down, GROUP, split_axis=0, concat_axis=0, tiled=True)

time: 330 us -> 321 us (0.973)
  blocking collectives: 9.87 us -> 0 us
  starting transfers between devices: 94.7 us -> 98.9 us
    all_to_all x1 -> x0, blocking collectives: 9.87 us -> none  [local(): lax.all_to_all(packed_down, GROUP, split_axis=0, concat_axis=0, tiled=True)]
    all_to_all x0 -> x1, starting transfers between devices: none -> 7.89 us  [local(): lax.all_to_all(packed_down, GROUP, split_axis=0, concat_axis=0, tiled=True)]
    all_to_all x0 -> x1, waiting for transfers between devices: none -> 5.7 us  [local(): lax.all_to_all(packed_down, GROUP, split_axis=0, concat_axis=0, tiled=True)]
    ppermute x54 -> x56, waiting for transfers between devices: 101 us -> 96.1 us  [send(): return lax.ppermute(value, ALL, pairs)]
    ppermute x54 -> x56, starting transfers between devices: 88.9 us -> 85.1 us  [send(): return lax.ppermute(value, ALL, pairs)]
    convert_element_type x5 -> x7, other arithmetic: 9.4 us -> 7.28 us  [add(): (left.astype(jnp.float32) + right.astype(jnp.float32)).astype(jnp.bfloat16)]
  transfers between devices with their start and end apart: 55 -> 58, of which waited for: 22 -> 21; matrix products, arithmetic and copies ran while one was open for 6% -> 6% of each run, Pallas kernels for 26% -> 28%
where the time goes in v5:
time: 321 us; the launch traced here: 320 us
  waiting for transfers between devices  108 us (34%)
  starting transfers between devices  98.9 us (31%)
  Pallas kernels  89.9 us (28%)
  other arithmetic  15.2 us (5%)
  local copies, waits for them, and re-layouts  7.31 us (2%)
    ppermute x56, waiting for transfers between devices, send(): return lax.ppermute(value, ALL, pairs)  96.1 us
    ppermute x56, starting transfers between devices, send(): return lax.ppermute(value, ALL, pairs)  85.1 us
    pallas_call x2, Pallas kernels, hidden_half(): pl.pallas_call(functools.partial(hidden_kernel, 8 * i), out_shape=(jax.Sh...  43.8 us
    pallas_call x4, Pallas kernels, down_quarter(): pl.pallas_call(down_kernel, grid=(4,), out_shape=(jax.ShapeDtypeStruct((T...  24.9 us
    pallas_call x2, Pallas kernels, ranks_of(): pl.pallas_call(functools.partial(rank_kernel, first), out_shape=out_shape...  14.2 us
    all_to_all x1, starting transfers between devices, local(): lax.all_to_all(packed_down, GROUP, split_axis=0, concat_axis=0, tiled=True)  7.89 us
    convert_element_type x7, other arithmetic, add(): (left.astype(jnp.float32) + right.astype(jnp.float32)).astype(jnp.bfloat16)  7.28 us
  transfers between devices with their start and end apart: 58, of which 21 were waited for; matrix products, arithmetic and copies ran while one was open for 6% of the time, Pallas kernels for 28%

profile of v5, /device:TPU:1, one launch (start us, length us, event | category | flops | bytes accessed | tf_op | source)
XLA Modules:
  0.0 320.1 jit_solution(10801158342093036941)
XLA Ops:
  7.2 5.7 %collective-permute-start.27 = (bf16[512,384]{1,0:T(8,128)(2,1)S(1)}, bf16[512,384]{1,0:T(8,128)(2,1)S(1)}, u32[]{:S(2)}, u32[]{:S(2)}) collective-permute-start(bf16[512,384]{1,0:T(8,128)(2,1)S(1)} %copy-done.33), channel_id=1, source_target_pairs={{16,19},{17,18},{18,17},{19,16},{20,23},{21,22},{22,21},{23,20},{2... | collective-permute-start | bytes 1179656 | tf_op jit(solution)/shard_map/ppermute | solution.py:65
  15.2 6.6 %collective-permute-done.27 = bf16[512,384]{1,0:T(8,128)(2,1)S(1)} collective-permute-done((bf16[512,384]{1,0:T(8,128)(2,1)S(1)}, bf16[512,384]{1,0:T(8,128)(2,1)S(1)}, u32[]{:S(2)}, u32[]{:S(2)}) %collective-permute-start.27) | collective-permute-done | bytes 393248 | tf_op jit(solution)/shard_map/ppermute | solution.py:65
  28.3 6.1 %collective-permute-done.3.refs_1_ = bf16[128,3072]{1,0:T(8,128)(2,1)S(1)} collective-permute-done((bf16[128,3072]{1,0:T(8,128)(2,1)S(1)}, bf16[128,3072]{1,0:T(8,128)(2,1)S(1)}, u32[]{:S(2)}, u32[]{:S(2)}) %collective-permute-start.3) | collective-permute-done | bytes 786464 | tf_op jit(solution)/shard_map/ppermute | solution.py:65
  38.8 6.0 %collective-permute-done.19 = bf16[384,1024]{1,0:T(8,128)(2,1)} collective-permute-done((bf16[384,1024]{1,0:T(8,128)(2,1)}, bf16[384,1024]{1,0:T(8,128)(2,1)}, u32[]{:S(2)}, u32[]{:S(2)}) %collective-permute-start.19) | collective-permute-done | bytes 786464 | tf_op jit(solution)/shard_map/ppermute | solution.py:65
  49.6 8.4 %collective-permute-done.33.refs_6_ = bf16[512,384]{1,0:T(8,128)(2,1)} collective-permute-done((bf16[512,384]{1,0:T(8,128)(2,1)}, bf16[512,384]{1,0:T(8,128)(2,1)}, u32[]{:S(2)}, u32[]{:S(2)}) %collective-permute-start.33) | collective-permute-done | bytes 393248 | tf_op jit(solution)/shard_map/ppermute | solution.py:65
  74.4 5.3 %collective-permute-done.11.refs_1_ = bf16[128,3072]{1,0:T(8,128)(2,1)S(1)} collective-permute-done((bf16[128,3072]{1,0:T(8,128)(2,1)}, bf16[128,3072]{1,0:T(8,128)(2,1)S(1)}, u32[]{:S(2)}, u32[]{:S(2)}) %collective-permute-start.11) | collective-permute-done | bytes 786464 | tf_op jit(solution)/shard_map/ppermute | solution.py:65
  85.6 16.6 %collective-permute-start.13 = (bf16[128,3072]{1,0:T(8,128)(2,1)S(1)}, bf16[128,3072]{1,0:T(8,128)(2,1)S(1)}, u32[]{:S(2)}, u32[]{:S(2)}) collective-permute-start(bf16[128,3072]{1,0:T(8,128)(2,1)S(1)} %collective-permute-done.11.refs_1_), channel_id=1, source_target_pairs={{0,16},{1,17},{2,18},{3,19},{4,20},{5,21},{6,22},{7,23},{8,24},{9,... | collective-permute-start | bytes 2359304 | tf_op jit(solution)/shard_map/ppermute | solution.py:65
  103.6 7.1 %collective-permute-start.16 = (bf16[128,3072]{1,0:T(8,128)(2,1)S(1)}, bf16[128,3072]{1,0:T(8,128)(2,1)S(1)}, u32[]{:S(2)}, u32[]{:S(2)}) collective-permute-start(bf16[128,3072]{1,0:T(8,128)(2,1)S(1)} %collective-permute-done.9.refs_5_), channel_id=1, source_target_pairs={{0,16},{1,17},{2,18},{3,19},{4,20},{5,21},{6,22},{7,23},{8,24},{9,... | collective-permute-start | bytes 2359304 | tf_op jit(solution)/shard_map/ppermute | solution.py:65
  116.1 15.9 %collective-permute-done.22.refs_11_ = bf16[384,1024]{1,0:T(8,128)(2,1)S(1)} collective-permute-done((bf16[384,1024]{1,0:T(8,128)(2,1)S(1)}, bf16[384,1024]{1,0:T(8,128)(2,1)S(1)}, u32[]{:S(2)}, u32[]{:S(2)}) %collective-permute-start.22) | collective-permute-done | bytes 786464 | tf_op jit(solution)/shard_map/ppermute | solution.py:65
  138.8 7.1 %ranks.2.before = f32[64,128]{1,0:T(8,128)} custom-call(bf16[128,3072]{1,0:T(8,128)(2,1)} %copy-done.24, s32[16,8,128]{2,1,0:T(8,128)} %places.1.ints, f32[64,128]{1,0:T(8,128)} %broadcast_in_dim.8.before, bf16[128,3072]{1,0:T(8,128)(2,1)} %copy-done.11, bf16[128,3072]{1,0:T(8,128)(2,1)} %copy-done.12, bf16[128,3072]{1,0:T(8,128)(2,1)} %copy-done.13, ...), custom_call_target="tpu_custom_call" | custom-call | tf_op jit(solution)/shard_map/ranks/pallas_call | solution.py:321
  145.9 7.2 %ranks.3 = bf16[16,64,128]{2,1,0:T(8,128)(2,1)} custom-call(bf16[128,3072]{1,0:T(8,128)(2,1)} %copy-done.24, s32[16,8,128]{2,1,0:T(8,128)} %places.1.ints, f32[64,128]{1,0:T(8,128)} %ranks.2.before, bf16[128,3072]{1,0:T(8,128)(2,1)} %copy-done.19, bf16[128,3072]{1,0:T(8,128)(2,1)} %copy-done.17, bf16[128,3072]{1,0:T(8,128)(2,1)} %copy-done.23, ...), custom_call_target="tpu_custom_call" | custom-call | tf_op jit(solution)/shard_map/ranks/pallas_call | solution.py:321
  153.0 5.9 %all-to-all-start = ((bf16[16,64,128]{2,1,0:T(8,128)(2,1)}), bf16[16,64,128]{2,1,0:T(8,128)(2,1)S(1)}, u32[]{:S(2)}, u32[]{:S(2)}) async-start(bf16[16,64,128]{2,1,0:T(8,128)(2,1)} %ranks.3), calls=%async_computation | async-start | bytes 524288 | tf_op jit(solution)/shard_map/all_to_all | solution.py:338
  159.7 6.4 %all-to-all-done = bf16[16,64,128]{2,1,0:T(8,128)(2,1)S(1)} async-done(((bf16[16,64,128]{2,1,0:T(8,128)(2,1)}), bf16[16,64,128]{2,1,0:T(8,128)(2,1)S(1)}, u32[]{:S(2)}, u32[]{:S(2)}) %all-to-all-start) | async-done | bytes 262176 | tf_op jit(solution)/shard_map/all_to_all | solution.py:338
  166.8 21.9 %hidden.2 = (bf16[1024,512]{1,0:T(8,128)(2,1)}, f32[256,128]{1,0:T(8,128)}) custom-call(s32[8]{0:T(128)} %stack.86.slab_at, bf16[1024,128]{1,0:T(8,128)(2,1)} %bitcast.25, s32[16,8,128]{2,1,0:T(8,128)} %places.1.ints, bf16[2,1024,512]{2,1,0:T(8,128)(2,1)} %copy-done.1, bf16[1024,512]{1,0:T(8,128)(2,1)} %copy-done.4, f32[256,128]{1,0:T(8,128)} %broadcast_in_dim.9.before, ...), custom_call_target="tpu_custom_call" | custom-call | tf_op jit(solution)/shard_map/hidden/pallas_call | solution.py:341
  188.7 6.2 %down.6 = (bf16[256,3072]{1,0:T(8,128)(2,1)}, bf16[256,3072]{1,0:T(8,128)(2,1)}) custom-call(s32[8]{0:T(128)} %stack.86.slab_at, bf16[1024,512]{1,0:T(8,128)(2,1)} %get-tuple-element.36.hidden, bf16[512,384]{1,0:T(8,128)(2,1)} %copy-done, bf16[512,384]{1,0:T(8,128)(2,1)} %collective-permute-done.28.refs_1_, ...), custom_call_target="tpu_custom_call" | custom-call | tf_op jit(solution)/shard_map/down/pallas_call | solution.py:369
  196.7 6.2 %down.7 = (bf16[256,3072]{1,0:T(8,128)(2,1)}, bf16[256,3072]{1,0:T(8,128)(2,1)}) custom-call(s32[8]{0:T(128)} %stack.86.slab_at, bf16[1024,512]{1,0:T(8,128)(2,1)} %get-tuple-element.36.hidden, bf16[512,384]{1,0:T(8,128)(2,1)} %copy-done, bf16[512,384]{1,0:T(8,128)(2,1)} %collective-permute-done.28.refs_1_, ...), custom_call_target="tpu_custom_call" | custom-call | tf_op jit(solution)/shard_map/down/pallas_call | solution.py:369
  209.0 5.6 %collective-permute-done.50.refs_3_ = bf16[64,3072]{1,0:T(8,128)(2,1)S(1)} collective-permute-done((bf16[64,3072]{1,0:T(8,128)(2,1)S(1)}, bf16[64,3072]{1,0:T(8,128)(2,1)S(1)}, u32[]{:S(2)}, u32[]{:S(2)}) %collective-permute-start.50) | collective-permute-done | bytes 393248 | tf_op jit(solution)/shard_map/ppermute | solution.py:65
  215.8 21.9 %hidden.3 = (bf16[1024,512]{1,0:T(8,128)(2,1)}, bf16[256,128]{1,0:T(8,128)(2,1)}) custom-call(s32[8]{0:T(128)} %stack.86.slab_at, bf16[1024,128]{1,0:T(8,128)(2,1)} %bitcast.26, s32[16,8,128]{2,1,0:T(8,128)} %places.1.ints, bf16[2,1024,512]{2,1,0:T(8,128)(2,1)} %copy-done.1, bf16[1024,512]{1,0:T(8,128)(2,1)} %copy-done.4, ...), custom_call_target="tpu_custom_call" | custom-call | tf_op jit(solution)/shard_map/hidden/pallas_call | solution.py:341
  237.8 7.9 %all-to-all-start.1 = ((bf16[16,16,128]{2,1,0:T(8,128)(2,1)}), bf16[16,16,128]{2,1,0:T(8,128)(2,1)S(1)}, u32[]{:S(2)}, u32[]{:S(2)}) async-start(bf16[16,16,128]{2,1,0:T(8,128)(2,1)} %bitcast.27), calls=%async_computation.1 | async-start | bytes 131072 | tf_op jit(solution)/shard_map/all_to_all | solution.py:394
  245.7 5.7 %all-to-all-done.1 = bf16[16,16,128]{2,1,0:T(8,128)(2,1)S(1)} async-done(((bf16[16,16,128]{2,1,0:T(8,128)(2,1)}), bf16[16,16,128]{2,1,0:T(8,128)(2,1)S(1)}, u32[]{:S(2)}, u32[]{:S(2)}) %all-to-all-start.1) | async-done | bytes 65568 | tf_op jit(solution)/shard_map/all_to_all | solution.py:394
  252.9 6.2 %down.4 = (bf16[256,3072]{1,0:T(8,128)(2,1)}, bf16[256,3072]{1,0:T(8,128)(2,1)}) custom-call(s32[8]{0:T(128)} %stack.86.slab_at, bf16[1024,512]{1,0:T(8,128)(2,1)} %get-tuple-element.28.hidden, bf16[512,384]{1,0:T(8,128)(2,1)} %copy-done, bf16[512,384]{1,0:T(8,128)(2,1)} %collective-permute-done.28.refs_1_, ...), custom_call_target="tpu_custom_call" | custom-call | tf_op jit(solution)/shard_map/down/pallas_call | solution.py:369
  259.1 6.2 %down.5 = (bf16[256,3072]{1,0:T(8,128)(2,1)}, bf16[256,3072]{1,0:T(8,128)(2,1)}) custom-call(s32[8]{0:T(128)} %stack.86.slab_at, bf16[1024,512]{1,0:T(8,128)(2,1)} %get-tuple-element.28.hidden, bf16[512,384]{1,0:T(8,128)(2,1)} %copy-done, bf16[512,384]{1,0:T(8,128)(2,1)} %collective-permute-done.28.refs_1_, ...), custom_call_target="tpu_custom_call" | custom-call | tf_op jit(solution)/shard_map/down/pallas_call | solution.py:369
  294.9 6.4 %collective-permute-done.44 = bf16[128,3072]{1,0:T(8,128)(2,1)S(1)} collective-permute-done((bf16[128,3072]{1,0:T(8,128)(2,1)S(1)}, bf16[128,3072]{1,0:T(8,128)(2,1)S(1)}, u32[]{:S(2)}, u32[]{:S(2)}) %collective-permute-start.44) | collective-permute-done | bytes 786464 | tf_op jit(solution)/shard_map/ppermute | solution.py:65
  306.6 7.1 %collective-permute-done.40 = bf16[128,3072]{1,0:T(8,128)(2,1)S(1)} collective-permute-done((bf16[128,3072]{1,0:T(8,128)(2,1)S(1)}, bf16[128,3072]{1,0:T(8,128)(2,1)S(1)}, u32[]{:S(2)}, u32[]{:S(2)}) %collective-permute-start.40) | collective-permute-done | bytes 786464 | tf_op jit(solution)/shard_map/ppermute | solution.py:65
  (210 shorter events, 114.0 us)
Async XLA Ops:
  0.0 23.8 %collective-permute-start = (bf16[128,3072]{1,0:T(8,128)(2,1)}, bf16[128,3072]{1,0:T(8,128)(2,1)S(1)}, u32[]{:S(2)}, u32[]{:S(2)}) collective-permute-start(bf16[128,3072]{1,0:T(8,128)(2,1)} %param.16), channel_id=1, source_target_pairs={{0,19},{1,18},{2,17},{3,16},{4,23},{5,22},{6,21},{7,20},{8,27},{9,... | collective-permute-start | bytes 2359304 | tf_op jit(solution)/shard_map/ppermute | solution.py:65
  4.3 23.9 %collective-permute-start.2 = (bf16[128,3072]{1,0:T(8,128)(2,1)S(1)}, bf16[128,3072]{1,0:T(8,128)(2,1)S(1)}, u32[]{:S(2)}, u32[]{:S(2)}) collective-permute-start(bf16[128,3072]{1,0:T(8,128)(2,1)S(1)} %fusion.2.refs_5_), channel_id=1, source_target_pairs={{0,1},{1,0},{2,3},{3,2},{4,5},{5,4},{6,7},{7,6},{8,9},{9,8},{10,11... | collective-permute-start | bytes 2359304 | tf_op jit(solution)/shard_map/ppermute | solution.py:65
  23.8 21.0 %collective-permute-start.19 = (bf16[384,1024]{1,0:T(8,128)(2,1)}, bf16[384,1024]{1,0:T(8,128)(2,1)}, u32[]{:S(2)}, u32[]{:S(2)}) collective-permute-start(bf16[384,1024]{1,0:T(8,128)(2,1)} %constant_dynamic-update-slice_fusion), channel_id=1, source_target_pairs={{16,19},{17,18},{18,17},{19,16},{20,23},{21,22},{22,21},{23,20},{2... | collective-permute-start | bytes 2359304 | tf_op jit(solution)/shard_map/ppermute | solution.py:65
  34.3 24.2 %collective-permute-start.18 = (bf16[1024,512]{1,0:T(8,128)(2,1)}, bf16[1024,512]{1,0:T(8,128)(2,1)S(1)}, u32[]{:S(2)}, u32[]{:S(2)}) collective-permute-start(bf16[1024,512]{1,0:T(8,128)(2,1)} %param.18), channel_id=1, source_target_pairs={{0,19},{1,18},{2,17},{3,16},{4,23},{5,22},{6,21},{7,20},{8,27},{9,... | collective-permute-start | bytes 3145736 | tf_op jit(solution)/shard_map/ppermute | solution.py:65
  37.9 21.7 %collective-permute-start.4 = (bf16[128,3072]{1,0:T(8,128)(2,1)}, bf16[128,3072]{1,0:T(8,128)(2,1)S(1)}, u32[]{:S(2)}, u32[]{:S(2)}) collective-permute-start(bf16[128,3072]{1,0:T(8,128)(2,1)} %copy-done.11), channel_id=1, source_target_pairs={{0,16},{1,17},{2,18},{3,19},{4,20},{5,21},{6,22},{7,23},{8,24},{9,... | collective-permute-start | bytes 2359304 | tf_op jit(solution)/shard_map/ppermute | solution.py:65
  57.9 52.7 %collective-permute-start.17 = (bf16[2,1024,512]{2,1,0:T(8,128)(2,1)}, bf16[2,1024,512]{2,1,0:T(8,128)(2,1)S(1)}, u32[]{:S(2)}, u32[]{:S(2)}) collective-permute-start(bf16[2,1024,512]{2,1,0:T(8,128)(2,1)} %param.17), channel_id=1, source_target_pairs={{0,19},{1,18},{2,17},{3,16},{4,23},{5,22},{6,21},{7,20},{8,27},{9,... | collective-permute-start | bytes 6291464 | tf_op jit(solution)/shard_map/ppermute | solution.py:65
  79.7 22.6 %collective-permute-start.24 = (bf16[384,1024]{1,0:T(8,128)(2,1)S(1)}, bf16[384,1024]{1,0:T(8,128)(2,1)S(1)}, u32[]{:S(2)}, u32[]{:S(2)}) collective-permute-start(bf16[384,1024]{1,0:T(8,128)(2,1)S(1)} %copy-done.6), channel_id=1, source_target_pairs={{0,32},{1,33},{2,34},{3,35},{4,36},{5,37},{6,38},{7,39},{8,40},{9,... | collective-permute-start | bytes 2359304 | tf_op jit(solution)/shard_map/ppermute | solution.py:65
  81.3 22.4 %collective-permute-start.25 = (bf16[384,1024]{1,0:T(8,128)(2,1)S(1)}, bf16[384,1024]{1,0:T(8,128)(2,1)}, u32[]{:S(2)}, u32[]{:S(2)}) collective-permute-start(bf16[384,1024]{1,0:T(8,128)(2,1)S(1)} %copy-done.6), channel_id=1, source_target_pairs={{0,96},{1,97},{2,98},{3,99},{4,100},{5,101},{6,102},{7,103},{8,104... | collective-permute-start | bytes 2359304 | tf_op jit(solution)/shard_map/ppermute | solution.py:65
  84.5 26.2 %collective-permute-start.10 = (bf16[128,3072]{1,0:T(8,128)(2,1)S(1)}, bf16[128,3072]{1,0:T(8,128)(2,1)S(1)}, u32[]{:S(2)}, u32[]{:S(2)}) collective-permute-start(bf16[128,3072]{1,0:T(8,128)(2,1)S(1)} %collective-permute-done.9.refs_5_), channel_id=1, source_target_pairs={{0,1},{1,0},{2,3},{3,2},{4,5},{5,4},{6,7},{7,6},{8,9},{9,8},{10,11... | collective-permute-start | bytes 2359304 | tf_op jit(solution)/shard_map/ppermute | solution.py:65
  85.6 25.5 %collective-permute-start.13 = (bf16[128,3072]{1,0:T(8,128)(2,1)S(1)}, bf16[128,3072]{1,0:T(8,128)(2,1)S(1)}, u32[]{:S(2)}, u32[]{:S(2)}) collective-permute-start(bf16[128,3072]{1,0:T(8,128)(2,1)S(1)} %collective-permute-done.11.refs_1_), channel_id=1, source_target_pairs={{0,16},{1,17},{2,18},{3,19},{4,20},{5,21},{6,22},{7,23},{8,24},{9,... | collective-permute-start | bytes 2359304 | tf_op jit(solution)/shard_map/ppermute | solution.py:65
  110.7 21.4 %collective-permute-start.22 = (bf16[384,1024]{1,0:T(8,128)(2,1)S(1)}, bf16[384,1024]{1,0:T(8,128)(2,1)S(1)}, u32[]{:S(2)}, u32[]{:S(2)}) collective-permute-start(bf16[384,1024]{1,0:T(8,128)(2,1)S(1)} %collective-permute-done.20.refs_9_), channel_id=1, source_target_pairs={{0,32},{1,33},{2,34},{3,35},{4,36},{5,37},{6,38},{7,39},{8,40},{9,... | collective-permute-start | bytes 2359304 | tf_op jit(solution)/shard_map/ppermute | solution.py:65
  110.7 21.3 %collective-permute-start.12 = (bf16[128,3072]{1,0:T(8,128)(2,1)S(1)}, bf16[128,3072]{1,0:T(8,128)(2,1)S(1)}, u32[]{:S(2)}, u32[]{:S(2)}) collective-permute-start(bf16[128,3072]{1,0:T(8,128)(2,1)S(1)} %collective-permute-done.10.refs_0_), channel_id=1, source_target_pairs={{0,16},{1,17},{2,18},{3,19},{4,20},{5,21},{6,22},{7,23},{8,24},{9,... | collective-permute-start | bytes 2359304 | tf_op jit(solution)/shard_map/ppermute | solution.py:65
  111.1 48.5 %collective-permute-start.26 = (bf16[384,1024]{1,0:T(8,128)(2,1)}, bf16[384,1024]{1,0:T(8,128)(2,1)}, u32[]{:S(2)}, u32[]{:S(2)}) collective-permute-start(bf16[384,1024]{1,0:T(8,128)(2,1)} %collective-permute-done.25.refs_14_), channel_id=1, source_target_pairs={{0,96},{1,97},{2,98},{3,99},{4,100},{5,101},{6,102},{7,103},{8,104... | collective-permute-start | bytes 2359304 | tf_op jit(solution)/shard_map/ppermute | solution.py:65
  114.4 74.3 %collective-permute-start.29 = (bf16[512,384]{1,0:T(8,128)(2,1)S(1)}, bf16[512,384]{1,0:T(8,128)(2,1)}, u32[]{:S(2)}, u32[]{:S(2)}) collective-permute-start(bf16[512,384]{1,0:T(8,128)(2,1)S(1)} %broadcast_select_fusion.1.refs_0_), channel_id=1, source_target_pairs={{0,96},{1,97},{2,98},{3,99},{4,100},{5,101},{6,102},{7,103},{8,104... | collective-permute-start | bytes 1179656 | tf_op jit(solution)/shard_map/ppermute | solution.py:65
  116.1 72.6 %collective-permute-start.32 = (bf16[512,384]{1,0:T(8,128)(2,1)}, bf16[512,384]{1,0:T(8,128)(2,1)}, u32[]{:S(2)}, u32[]{:S(2)}) collective-permute-start(bf16[512,384]{1,0:T(8,128)(2,1)} %collective-permute-done.31.refs_4_), channel_id=1, source_target_pairs={{0,32},{1,33},{2,34},{3,35},{4,36},{5,37},{6,38},{7,39},{8,40},{9,... | collective-permute-start | bytes 1179656 | tf_op jit(solution)/shard_map/ppermute | solution.py:65
  132.1 56.7 %collective-permute-start.30 = (bf16[512,384]{1,0:T(8,128)(2,1)}, bf16[512,384]{1,0:T(8,128)(2,1)}, u32[]{:S(2)}, u32[]{:S(2)}) collective-permute-start(bf16[512,384]{1,0:T(8,128)(2,1)} %collective-permute-done.28.refs_1_), channel_id=1, source_target_pairs={{0,32},{1,33},{2,34},{3,35},{4,36},{5,37},{6,38},{7,39},{8,40},{9,... | collective-permute-start | bytes 1179656 | tf_op jit(solution)/shard_map/ppermute | solution.py:65
  133.8 54.9 %collective-permute-start.34 = (bf16[512,384]{1,0:T(8,128)(2,1)}, bf16[512,384]{1,0:T(8,128)(2,1)}, u32[]{:S(2)}, u32[]{:S(2)}) collective-permute-start(bf16[512,384]{1,0:T(8,128)(2,1)} %collective-permute-done.33.refs_6_), channel_id=1, source_target_pairs={{0,96},{1,97},{2,98},{3,99},{4,100},{5,101},{6,102},{7,103},{8,104... | collective-permute-start | bytes 1179656 | tf_op jit(solution)/shard_map/ppermute | solution.py:65
  159.6 36.5 %collective-permute-start.47 = (bf16[64,3072]{1,0:T(8,128)(2,1)}, bf16[64,3072]{1,0:T(8,128)(2,1)S(1)}, u32[]{:S(2)}, u32[]{:S(2)}) collective-permute-start(bf16[64,3072]{1,0:T(8,128)(2,1)} %param.19), channel_id=1, source_target_pairs={{0,19},{1,18},{2,17},{3,16},{4,23},{5,22},{6,21},{7,20},{8,27},{9,... | collective-permute-start | bytes 1179656 | tf_op jit(solution)/shard_map/ppermute | solution.py:65
  195.0 77.7 %collective-permute-start.38 = (bf16[256,3072]{1,0:T(8,128)(2,1)}, bf16[256,3072]{1,0:T(8,128)(2,1)S(1)}, u32[]{:S(2)}, u32[]{:S(2)}) collective-permute-start(bf16[256,3072]{1,0:T(8,128)(2,1)} %get-tuple-element.38), channel_id=1, source_target_pairs={{0,16},{1,17},{2,18},{3,19},{4,20},{5,21},{6,22},{7,23},{8,24},{9,... | collective-permute-start | bytes 4718600 | tf_op jit(solution)/shard_map/ppermute | solution.py:65
  202.9 71.2 %collective-permute-start.41 = (bf16[256,3072]{1,0:T(8,128)(2,1)}, bf16[256,3072]{1,0:T(8,128)(2,1)}, u32[]{:S(2)}, u32[]{:S(2)}) collective-permute-start(bf16[256,3072]{1,0:T(8,128)(2,1)} %get-tuple-element.42), channel_id=1, source_target_pairs={{0,16},{1,17},{2,18},{3,19},{4,20},{5,21},{6,22},{7,23},{8,24},{9,... | collective-permute-start | bytes 4718600 | tf_op jit(solution)/shard_map/ppermute | solution.py:65
  207.6 43.8 %collective-permute-start.52 = (bf16[64,3072]{1,0:T(8,128)(2,1)S(1)}, bf16[64,3072]{1,0:T(8,128)(2,1)S(1)}, u32[]{:S(2)}, u32[]{:S(2)}) collective-permute-start(bf16[64,3072]{1,0:T(8,128)(2,1)S(1)} %collective-permute-done.48.refs_1_), channel_id=1, source_target_pairs={{0,1},{1,0},{2,3},{3,2},{4,5},{5,4},{6,7},{7,6},{8,9},{9,8},{10,11... | collective-permute-start | bytes 1179656 | tf_op jit(solution)/shard_map/ppermute | solution.py:65
  214.7 51.5 %collective-permute-start.53 = (bf16[64,3072]{1,0:T(8,128)(2,1)S(1)}, bf16[64,3072]{1,0:T(8,128)(2,1)S(1)}, u32[]{:S(2)}, u32[]{:S(2)}) collective-permute-start(bf16[64,3072]{1,0:T(8,128)(2,1)S(1)} %collective-permute-done.49.refs_2_), channel_id=1, source_target_pairs={{0,1},{1,0},{2,3},{3,2},{4,5},{5,4},{6,7},{7,6},{8,9},{9,8},{10,11... | collective-permute-start | bytes 1179656 | tf_op jit(solution)/shard_map/ppermute | solution.py:65
  214.9 51.6 %collective-permute-start.54 = (bf16[64,3072]{1,0:T(8,128)(2,1)}, bf16[64,3072]{1,0:T(8,128)(2,1)}, u32[]{:S(2)}, u32[]{:S(2)}) collective-permute-start(bf16[64,3072]{1,0:T(8,128)(2,1)} %collective-permute-done.51.refs_4_), channel_id=1, source_target_pairs={{0,1},{1,0},{2,3},{3,2},{4,5},{5,4},{6,7},{7,6},{8,9},{9,8},{10,11... | collective-permute-start | bytes 1179656 | tf_op jit(solution)/shard_map/ppermute | solution.py:65
  272.2 29.8 %collective-permute-start.55 = (bf16[128,3072]{1,0:T(8,128)(2,1)}, bf16[128,3072]{1,0:T(8,128)(2,1)S(1)}, u32[]{:S(2)}, u32[]{:S(2)}) collective-permute-start(bf16[128,3072]{1,0:T(8,128)(2,1)} %get-tuple-element.48), channel_id=1, source_target_pairs={{0,16},{1,17},{2,18},{3,19},{4,20},{5,21},{6,22},{7,23},{8,24},{9,... | collective-permute-start | bytes 2359304 | tf_op jit(solution)/shard_map/ppermute | solution.py:65
  (77 other events, 1485.7 us)

commit v6 on v5

--- a/solution.py
+++ b/solution.py
@@ -137,8 +137,8 @@
     return (row - shift == column).astype(jnp.bfloat16)
 
 
-def places(ints, i, first=0):
-    across = jnp.concatenate([ints[first + 2 * i], ints[first + 2 * i + 1]], axis=1)
+def places(ints, i, first=0, count=2):
+    across = jnp.concatenate([ints[first + count * i + j] for j in range(count)], axis=1)
     return across.T, across
 
 
@@ -146,7 +146,7 @@
     shards, (out, total, rows, sems) = refs[:-4], refs[-4:]
     for i, shard in enumerate(shards):
         pltpu.make_async_copy(shard, rows.at[pl.ds(i * 128, 128)], sems.at[i * 128 // TILE]).start()
-    total[...] = before[...]
+    total[...] = before[0:64, :]
     fold = matching(128, 32, 128, 32)
 
     def tile(i, carry):
@@ -234,12 +234,23 @@
         first = jnp.where(lane >> 6 == i, map_slots[i], first)
     lane_slot = first + ((lane >> 4) & 3)
     pltpu.make_async_copy(whole, whole, sem.at[0]).wait()
-    for t, out in enumerate((mine, theirs)):
+    chosen = []
+    for t in range(2):
         down = ints[ROW_BLOCKS.index(8 * t)].T
         place = lanes(128, 16, 1) == down[:, 7:8] >> 3
         own = kept(lanes(128, 128, 16) == down[:, 4:5], dot(place.astype(jnp.bfloat16), ranks[t]))
-        own = kept(lane_slot == down[:, 0:1], dot(own, spread))
-        out[...] = dot(own, whole[...]).astype(jnp.bfloat16)
+        chosen.append(kept(lane_slot == down[:, 0:1], dot(own, spread)))
+    chosen = jnp.concatenate(chosen, axis=0)
+    columns = whole.shape[1] // 4
+
+    def chunk(i, carry):
+        part = pl.ds(pl.multiple_of(i * columns, 128), columns)
+        both = dot(chosen, whole[:, part]).astype(jnp.bfloat16)
+        mine[:, part] = both[:128]
+        theirs[:, part] = both[128:]
+        return carry
+
+    lax.fori_loop(0, 4, chunk, 0)
 
 
 def weight_blocks(shard, ci):
@@ -331,8 +342,9 @@
             name="ranks",
         )(shrink, ints, before, *shards[first:last])
 
+    nothing = jnp.zeros((256, 128), jnp.float32)
     packed = jax.ShapeDtypeStruct((64, 128), jnp.float32)
-    packed = ranks_of(LATE_BLOCKS, 16, jnp.zeros((64, 128), jnp.float32), packed)
+    packed = ranks_of(LATE_BLOCKS, 16, nothing, packed)
     spread = jax.ShapeDtypeStruct((16, 64, 128), jnp.bfloat16)
     spread = ranks_of(0, LATE_BLOCKS, packed, spread)
     ranks = lax.all_to_all(spread, GROUP, split_axis=0, concat_axis=0, tiled=True).reshape(1024, 128)
@@ -380,7 +392,7 @@
         return (left.astype(jnp.float32) + right.astype(jnp.float32)).astype(jnp.bfloat16)
 
     sums = [None] * 8
-    packed_down = jnp.zeros((256, 128), jnp.float32)
+    packed_down = nothing
     for i, kind in enumerate((jnp.float32, jnp.bfloat16)):
         hidden, packed_down = hidden_half(i, packed_down, kind)
         for j in range(2):

time: 321 us -> 321 us (level)
  transfers between devices with their start and end apart: 58 -> 58, of which waited for: 21 -> 21; matrix products, arithmetic and copies ran while one was open for 6% -> 5% of each run, Pallas kernels for 28% -> 28%
where the time goes in v6:
time: 321 us
  waiting for transfers between devices  108 us (34%)
  starting transfers between devices  98.8 us (31%)
  Pallas kernels  90.5 us (28%)
  other arithmetic  15.1 us (5%)
  local copies, waits for them, and re-layouts  7.36 us (2%)
    ppermute x56, waiting for transfers between devices, send(): return lax.ppermute(value, ALL, pairs)  96.2 us
    ppermute x56, starting transfers between devices, send(): return lax.ppermute(value, ALL, pairs)  85.1 us
    pallas_call x2, Pallas kernels, hidden_half(): pl.pallas_call(functools.partial(hidden_kernel, 8 * i), out_shape=(jax.Sh...  43.7 us
    pallas_call x4, Pallas kernels, down_quarter(): pl.pallas_call(down_kernel, grid=(4,), out_shape=(jax.ShapeDtypeStruct((T...  24.8 us
    pallas_call x2, Pallas kernels, ranks_of(): pl.pallas_call(functools.partial(rank_kernel, first), out_shape=out_shape...  14.2 us
    all_to_all x1, starting transfers between devices, local(): lax.all_to_all(packed_down, GROUP, split_axis=0, concat_axis=0, tiled=True)  7.87 us
    convert_element_type x7, other arithmetic, add(): (left.astype(jnp.float32) + right.astype(jnp.float32)).astype(jnp.bfloat16)  7.28 us
  transfers between devices with their start and end apart: 58, of which 21 were waited for; matrix products, arithmetic and copies ran while one was open for 5% of the time, Pallas kernels for 28%

profile of v6, /device:TPU:1, one launch (start us, length us, event | category | flops | bytes accessed | tf_op | source)
XLA Modules:
  0.0 320.6 jit_solution(9806984336494351573)
XLA Ops:
  7.2 5.7 %collective-permute-start.27 = (bf16[512,384]{1,0:T(8,128)(2,1)S(1)}, bf16[512,384]{1,0:T(8,128)(2,1)S(1)}, u32[]{:S(2)}, u32[]{:S(2)}) collective-permute-start(bf16[512,384]{1,0:T(8,128)(2,1)S(1)} %copy-done.33), channel_id=1, source_target_pairs={{16,19},{17,18},{18,17},{19,16},{20,23},{21,22},{22,21},{23,20},{2... | collective-permute-start | bytes 1179656 | tf_op jit(solution)/shard_map/ppermute | solution.py:65
  15.2 6.6 %collective-permute-done.27 = bf16[512,384]{1,0:T(8,128)(2,1)S(1)} collective-permute-done((bf16[512,384]{1,0:T(8,128)(2,1)S(1)}, bf16[512,384]{1,0:T(8,128)(2,1)S(1)}, u32[]{:S(2)}, u32[]{:S(2)}) %collective-permute-start.27) | collective-permute-done | bytes 393248 | tf_op jit(solution)/shard_map/ppermute | solution.py:65
  28.3 6.1 %collective-permute-done.3.refs_1_ = bf16[128,3072]{1,0:T(8,128)(2,1)S(1)} collective-permute-done((bf16[128,3072]{1,0:T(8,128)(2,1)S(1)}, bf16[128,3072]{1,0:T(8,128)(2,1)S(1)}, u32[]{:S(2)}, u32[]{:S(2)}) %collective-permute-start.3) | collective-permute-done | bytes 786464 | tf_op jit(solution)/shard_map/ppermute | solution.py:65
  38.8 6.0 %collective-permute-done.19 = bf16[384,1024]{1,0:T(8,128)(2,1)} collective-permute-done((bf16[384,1024]{1,0:T(8,128)(2,1)}, bf16[384,1024]{1,0:T(8,128)(2,1)}, u32[]{:S(2)}, u32[]{:S(2)}) %collective-permute-start.19) | collective-permute-done | bytes 786464 | tf_op jit(solution)/shard_map/ppermute | solution.py:65
  49.6 8.4 %collective-permute-done.33.refs_6_ = bf16[512,384]{1,0:T(8,128)(2,1)} collective-permute-done((bf16[512,384]{1,0:T(8,128)(2,1)}, bf16[512,384]{1,0:T(8,128)(2,1)}, u32[]{:S(2)}, u32[]{:S(2)}) %collective-permute-start.33) | collective-permute-done | bytes 393248 | tf_op jit(solution)/shard_map/ppermute | solution.py:65
  85.6 16.6 %collective-permute-start.13 = (bf16[128,3072]{1,0:T(8,128)(2,1)S(1)}, bf16[128,3072]{1,0:T(8,128)(2,1)S(1)}, u32[]{:S(2)}, u32[]{:S(2)}) collective-permute-start(bf16[128,3072]{1,0:T(8,128)(2,1)S(1)} %collective-permute-done.11.refs_1_), channel_id=1, source_target_pairs={{0,16},{1,17},{2,18},{3,19},{4,20},{5,21},{6,22},{7,23},{8,24},{9,... | collective-permute-start | bytes 2359304 | tf_op jit(solution)/shard_map/ppermute | solution.py:65
  103.6 7.1 %collective-permute-start.16 = (bf16[128,3072]{1,0:T(8,128)(2,1)S(1)}, bf16[128,3072]{1,0:T(8,128)(2,1)S(1)}, u32[]{:S(2)}, u32[]{:S(2)}) collective-permute-start(bf16[128,3072]{1,0:T(8,128)(2,1)S(1)} %collective-permute-done.9.refs_5_), channel_id=1, source_target_pairs={{0,16},{1,17},{2,18},{3,19},{4,20},{5,21},{6,22},{7,23},{8,24},{9,... | collective-permute-start | bytes 2359304 | tf_op jit(solution)/shard_map/ppermute | solution.py:65
  116.1 15.9 %collective-permute-done.22.refs_11_ = bf16[384,1024]{1,0:T(8,128)(2,1)S(1)} collective-permute-done((bf16[384,1024]{1,0:T(8,128)(2,1)S(1)}, bf16[384,1024]{1,0:T(8,128)(2,1)S(1)}, u32[]{:S(2)}, u32[]{:S(2)}) %collective-permute-start.22) | collective-permute-done | bytes 786464 | tf_op jit(solution)/shard_map/ppermute | solution.py:65
  138.7 7.1 %ranks.2.before = f32[64,128]{1,0:T(8,128)} custom-call(bf16[128,3072]{1,0:T(8,128)(2,1)} %copy-done.24, s32[16,8,128]{2,1,0:T(8,128)} %places.1.ints, f32[256,128]{1,0:T(8,128)} %broadcast_in_dim.2.before, bf16[128,3072]{1,0:T(8,128)(2,1)} %copy-done.11, bf16[128,3072]{1,0:T(8,128)(2,1)} %copy-done.12, bf16[128,3072]{1,0:T(8,128)(2,1)} %copy-done.13, ...), custom_call_target="tpu_custom_call" | custom-call | tf_op jit(solution)/shard_map/ranks/pallas_call | solution.py:332
  145.8 7.2 %ranks.3 = bf16[16,64,128]{2,1,0:T(8,128)(2,1)} custom-call(bf16[128,3072]{1,0:T(8,128)(2,1)} %copy-done.24, s32[16,8,128]{2,1,0:T(8,128)} %places.1.ints, f32[64,128]{1,0:T(8,128)} %ranks.2.before, bf16[128,3072]{1,0:T(8,128)(2,1)} %copy-done.19, bf16[128,3072]{1,0:T(8,128)(2,1)} %copy-done.17, bf16[128,3072]{1,0:T(8,128)(2,1)} %copy-done.23, ...), custom_call_target="tpu_custom_call" | custom-call | tf_op jit(solution)/shard_map/ranks/pallas_call | solution.py:332
  153.0 5.8 %all-to-all-start = ((bf16[16,64,128]{2,1,0:T(8,128)(2,1)}), bf16[16,64,128]{2,1,0:T(8,128)(2,1)S(1)}, u32[]{:S(2)}, u32[]{:S(2)}) async-start(bf16[16,64,128]{2,1,0:T(8,128)(2,1)} %ranks.3), calls=%async_computation | async-start | bytes 524288 | tf_op jit(solution)/shard_map/all_to_all | solution.py:350
  159.7 6.4 %all-to-all-done = bf16[16,64,128]{2,1,0:T(8,128)(2,1)S(1)} async-done(((bf16[16,64,128]{2,1,0:T(8,128)(2,1)}), bf16[16,64,128]{2,1,0:T(8,128)(2,1)S(1)}, u32[]{:S(2)}, u32[]{:S(2)}) %all-to-all-start) | async-done | bytes 262176 | tf_op jit(solution)/shard_map/all_to_all | solution.py:350
  166.8 21.9 %hidden.2 = (bf16[1024,512]{1,0:T(8,128)(2,1)}, f32[256,128]{1,0:T(8,128)}) custom-call(s32[8]{0:T(128)} %stack.86.slab_at, bf16[1024,128]{1,0:T(8,128)(2,1)} %bitcast.25, s32[16,8,128]{2,1,0:T(8,128)} %places.1.ints, bf16[2,1024,512]{2,1,0:T(8,128)(2,1)} %copy-done.1, bf16[1024,512]{1,0:T(8,128)(2,1)} %copy-done.4, f32[256,128]{1,0:T(8,128)} %broadcast_in_dim.2.before, ...), custom_call_target="tpu_custom_call" | custom-call | tf_op jit(solution)/shard_map/hidden/pallas_call | solution.py:353
  188.7 6.2 %down.6 = (bf16[256,3072]{1,0:T(8,128)(2,1)}, bf16[256,3072]{1,0:T(8,128)(2,1)}) custom-call(s32[8]{0:T(128)} %stack.86.slab_at, bf16[1024,512]{1,0:T(8,128)(2,1)} %get-tuple-element.36.hidden, bf16[512,384]{1,0:T(8,128)(2,1)} %copy-done, bf16[512,384]{1,0:T(8,128)(2,1)} %collective-permute-done.28.refs_1_, ...), custom_call_target="tpu_custom_call" | custom-call | tf_op jit(solution)/shard_map/down/pallas_call | solution.py:381
  196.6 6.1 %down.7 = (bf16[256,3072]{1,0:T(8,128)(2,1)}, bf16[256,3072]{1,0:T(8,128)(2,1)}) custom-call(s32[8]{0:T(128)} %stack.86.slab_at, bf16[1024,512]{1,0:T(8,128)(2,1)} %get-tuple-element.36.hidden, bf16[512,384]{1,0:T(8,128)(2,1)} %copy-done, bf16[512,384]{1,0:T(8,128)(2,1)} %collective-permute-done.28.refs_1_, ...), custom_call_target="tpu_custom_call" | custom-call | tf_op jit(solution)/shard_map/down/pallas_call | solution.py:381
  208.9 5.6 %collective-permute-done.50.refs_3_ = bf16[64,3072]{1,0:T(8,128)(2,1)S(1)} collective-permute-done((bf16[64,3072]{1,0:T(8,128)(2,1)S(1)}, bf16[64,3072]{1,0:T(8,128)(2,1)S(1)}, u32[]{:S(2)}, u32[]{:S(2)}) %collective-permute-start.50) | collective-permute-done | bytes 393248 | tf_op jit(solution)/shard_map/ppermute | solution.py:65
  215.7 21.8 %hidden.3 = (bf16[1024,512]{1,0:T(8,128)(2,1)}, bf16[256,128]{1,0:T(8,128)(2,1)}) custom-call(s32[8]{0:T(128)} %stack.86.slab_at, bf16[1024,128]{1,0:T(8,128)(2,1)} %bitcast.26, s32[16,8,128]{2,1,0:T(8,128)} %places.1.ints, bf16[2,1024,512]{2,1,0:T(8,128)(2,1)} %copy-done.1, bf16[1024,512]{1,0:T(8,128)(2,1)} %copy-done.4, ...), custom_call_target="tpu_custom_call" | custom-call | tf_op jit(solution)/shard_map/hidden/pallas_call | solution.py:353
  237.5 7.9 %all-to-all-start.1 = ((bf16[16,16,128]{2,1,0:T(8,128)(2,1)}), bf16[16,16,128]{2,1,0:T(8,128)(2,1)S(1)}, u32[]{:S(2)}, u32[]{:S(2)}) async-start(bf16[16,16,128]{2,1,0:T(8,128)(2,1)} %bitcast.27), calls=%async_computation.1 | async-start | bytes 131072 | tf_op jit(solution)/shard_map/all_to_all | solution.py:406
  245.4 5.7 %all-to-all-done.1 = bf16[16,16,128]{2,1,0:T(8,128)(2,1)S(1)} async-done(((bf16[16,16,128]{2,1,0:T(8,128)(2,1)}), bf16[16,16,128]{2,1,0:T(8,128)(2,1)S(1)}, u32[]{:S(2)}, u32[]{:S(2)}) %all-to-all-start.1) | async-done | bytes 65568 | tf_op jit(solution)/shard_map/all_to_all | solution.py:406
  252.7 6.2 %down.4 = (bf16[256,3072]{1,0:T(8,128)(2,1)}, bf16[256,3072]{1,0:T(8,128)(2,1)}) custom-call(s32[8]{0:T(128)} %stack.86.slab_at, bf16[1024,512]{1,0:T(8,128)(2,1)} %get-tuple-element.28.hidden, bf16[512,384]{1,0:T(8,128)(2,1)} %copy-done, bf16[512,384]{1,0:T(8,128)(2,1)} %collective-permute-done.28.refs_1_, ...), custom_call_target="tpu_custom_call" | custom-call | tf_op jit(solution)/shard_map/down/pallas_call | solution.py:381
  258.9 6.2 %down.5 = (bf16[256,3072]{1,0:T(8,128)(2,1)}, bf16[256,3072]{1,0:T(8,128)(2,1)}) custom-call(s32[8]{0:T(128)} %stack.86.slab_at, bf16[1024,512]{1,0:T(8,128)(2,1)} %get-tuple-element.28.hidden, bf16[512,384]{1,0:T(8,128)(2,1)} %copy-done, bf16[512,384]{1,0:T(8,128)(2,1)} %collective-permute-done.28.refs_1_, ...), custom_call_target="tpu_custom_call" | custom-call | tf_op jit(solution)/shard_map/down/pallas_call | solution.py:381
  266.7 6.0 %adapters.1 = (bf16[128,3072]{1,0:T(8,128)(2,1)}, bf16[128,3072]{1,0:T(8,128)(2,1)}) custom-call(s32[8]{0:T(128)} %stack.100.map_slots, bf16[2,16,128]{2,1,0:T(8,128)(2,1)} %pad_maximum_fusion.ranks, s32[16,8,128]{2,1,0:T(8,128)} %places.1.ints, bf16[64,3072]{1,0:T(8,128)(2,1)} %copy-done.35, bf16[64,3072]{1,0:T(8,128)(2,1)} %copy-done.36, ...), custom_call_target="tpu_custom_call" | custom-call | tf_op jit(solution)/shard_map/adapters/pallas_call | solution.py:409
  295.4 6.4 %collective-permute-done.44 = bf16[128,3072]{1,0:T(8,128)(2,1)S(1)} collective-permute-done((bf16[128,3072]{1,0:T(8,128)(2,1)S(1)}, bf16[128,3072]{1,0:T(8,128)(2,1)S(1)}, u32[]{:S(2)}, u32[]{:S(2)}) %collective-permute-start.44) | collective-permute-done | bytes 786464 | tf_op jit(solution)/shard_map/ppermute | solution.py:65
  307.2 7.0 %collective-permute-done.40 = bf16[128,3072]{1,0:T(8,128)(2,1)S(1)} collective-permute-done((bf16[128,3072]{1,0:T(8,128)(2,1)S(1)}, bf16[128,3072]{1,0:T(8,128)(2,1)S(1)}, u32[]{:S(2)}, u32[]{:S(2)}) %collective-permute-start.40) | collective-permute-done | bytes 786464 | tf_op jit(solution)/shard_map/ppermute | solution.py:65
  (209 shorter events, 114.1 us)
Async XLA Ops:
  0.0 23.8 %collective-permute-start = (bf16[128,3072]{1,0:T(8,128)(2,1)}, bf16[128,3072]{1,0:T(8,128)(2,1)S(1)}, u32[]{:S(2)}, u32[]{:S(2)}) collective-permute-start(bf16[128,3072]{1,0:T(8,128)(2,1)} %param.16), channel_id=1, source_target_pairs={{0,19},{1,18},{2,17},{3,16},{4,23},{5,22},{6,21},{7,20},{8,27},{9,... | collective-permute-start | bytes 2359304 | tf_op jit(solution)/shard_map/ppermute | solution.py:65
  4.3 23.9 %collective-permute-start.2 = (bf16[128,3072]{1,0:T(8,128)(2,1)S(1)}, bf16[128,3072]{1,0:T(8,128)(2,1)S(1)}, u32[]{:S(2)}, u32[]{:S(2)}) collective-permute-start(bf16[128,3072]{1,0:T(8,128)(2,1)S(1)} %fusion.2.refs_5_), channel_id=1, source_target_pairs={{0,1},{1,0},{2,3},{3,2},{4,5},{5,4},{6,7},{7,6},{8,9},{9,8},{10,11... | collective-permute-start | bytes 2359304 | tf_op jit(solution)/shard_map/ppermute | solution.py:65
  23.8 21.0 %collective-permute-start.19 = (bf16[384,1024]{1,0:T(8,128)(2,1)}, bf16[384,1024]{1,0:T(8,128)(2,1)}, u32[]{:S(2)}, u32[]{:S(2)}) collective-permute-start(bf16[384,1024]{1,0:T(8,128)(2,1)} %constant_dynamic-update-slice_fusion), channel_id=1, source_target_pairs={{16,19},{17,18},{18,17},{19,16},{20,23},{21,22},{22,21},{23,20},{2... | collective-permute-start | bytes 2359304 | tf_op jit(solution)/shard_map/ppermute | solution.py:65
  34.3 24.2 %collective-permute-start.18 = (bf16[1024,512]{1,0:T(8,128)(2,1)}, bf16[1024,512]{1,0:T(8,128)(2,1)S(1)}, u32[]{:S(2)}, u32[]{:S(2)}) collective-permute-start(bf16[1024,512]{1,0:T(8,128)(2,1)} %param.18), channel_id=1, source_target_pairs={{0,19},{1,18},{2,17},{3,16},{4,23},{5,22},{6,21},{7,20},{8,27},{9,... | collective-permute-start | bytes 3145736 | tf_op jit(solution)/shard_map/ppermute | solution.py:65
  37.9 21.7 %collective-permute-start.4 = (bf16[128,3072]{1,0:T(8,128)(2,1)}, bf16[128,3072]{1,0:T(8,128)(2,1)S(1)}, u32[]{:S(2)}, u32[]{:S(2)}) collective-permute-start(bf16[128,3072]{1,0:T(8,128)(2,1)} %copy-done.11), channel_id=1, source_target_pairs={{0,16},{1,17},{2,18},{3,19},{4,20},{5,21},{6,22},{7,23},{8,24},{9,... | collective-permute-start | bytes 2359304 | tf_op jit(solution)/shard_map/ppermute | solution.py:65
  57.9 52.7 %collective-permute-start.17 = (bf16[2,1024,512]{2,1,0:T(8,128)(2,1)}, bf16[2,1024,512]{2,1,0:T(8,128)(2,1)S(1)}, u32[]{:S(2)}, u32[]{:S(2)}) collective-permute-start(bf16[2,1024,512]{2,1,0:T(8,128)(2,1)} %param.17), channel_id=1, source_target_pairs={{0,19},{1,18},{2,17},{3,16},{4,23},{5,22},{6,21},{7,20},{8,27},{9,... | collective-permute-start | bytes 6291464 | tf_op jit(solution)/shard_map/ppermute | solution.py:65
  79.7 22.6 %collective-permute-start.24 = (bf16[384,1024]{1,0:T(8,128)(2,1)S(1)}, bf16[384,1024]{1,0:T(8,128)(2,1)S(1)}, u32[]{:S(2)}, u32[]{:S(2)}) collective-permute-start(bf16[384,1024]{1,0:T(8,128)(2,1)S(1)} %copy-done.6), channel_id=1, source_target_pairs={{0,32},{1,33},{2,34},{3,35},{4,36},{5,37},{6,38},{7,39},{8,40},{9,... | collective-permute-start | bytes 2359304 | tf_op jit(solution)/shard_map/ppermute | solution.py:65
  81.3 22.4 %collective-permute-start.25 = (bf16[384,1024]{1,0:T(8,128)(2,1)S(1)}, bf16[384,1024]{1,0:T(8,128)(2,1)}, u32[]{:S(2)}, u32[]{:S(2)}) collective-permute-start(bf16[384,1024]{1,0:T(8,128)(2,1)S(1)} %copy-done.6), channel_id=1, source_target_pairs={{0,96},{1,97},{2,98},{3,99},{4,100},{5,101},{6,102},{7,103},{8,104... | collective-permute-start | bytes 2359304 | tf_op jit(solution)/shard_map/ppermute | solution.py:65
  84.5 26.2 %collective-permute-start.10 = (bf16[128,3072]{1,0:T(8,128)(2,1)S(1)}, bf16[128,3072]{1,0:T(8,128)(2,1)S(1)}, u32[]{:S(2)}, u32[]{:S(2)}) collective-permute-start(bf16[128,3072]{1,0:T(8,128)(2,1)S(1)} %collective-permute-done.9.refs_5_), channel_id=1, source_target_pairs={{0,1},{1,0},{2,3},{3,2},{4,5},{5,4},{6,7},{7,6},{8,9},{9,8},{10,11... | collective-permute-start | bytes 2359304 | tf_op jit(solution)/shard_map/ppermute | solution.py:65
  85.6 25.5 %collective-permute-start.13 = (bf16[128,3072]{1,0:T(8,128)(2,1)S(1)}, bf16[128,3072]{1,0:T(8,128)(2,1)S(1)}, u32[]{:S(2)}, u32[]{:S(2)}) collective-permute-start(bf16[128,3072]{1,0:T(8,128)(2,1)S(1)} %collective-permute-done.11.refs_1_), channel_id=1, source_target_pairs={{0,16},{1,17},{2,18},{3,19},{4,20},{5,21},{6,22},{7,23},{8,24},{9,... | collective-permute-start | bytes 2359304 | tf_op jit(solution)/shard_map/ppermute | solution.py:65
  110.7 21.4 %collective-permute-start.22 = (bf16[384,1024]{1,0:T(8,128)(2,1)S(1)}, bf16[384,1024]{1,0:T(8,128)(2,1)S(1)}, u32[]{:S(2)}, u32[]{:S(2)}) collective-permute-start(bf16[384,1024]{1,0:T(8,128)(2,1)S(1)} %collective-permute-done.20.refs_9_), channel_id=1, source_target_pairs={{0,32},{1,33},{2,34},{3,35},{4,36},{5,37},{6,38},{7,39},{8,40},{9,... | collective-permute-start | bytes 2359304 | tf_op jit(solution)/shard_map/ppermute | solution.py:65
  110.7 21.3 %collective-permute-start.12 = (bf16[128,3072]{1,0:T(8,128)(2,1)S(1)}, bf16[128,3072]{1,0:T(8,128)(2,1)S(1)}, u32[]{:S(2)}, u32[]{:S(2)}) collective-permute-start(bf16[128,3072]{1,0:T(8,128)(2,1)S(1)} %collective-permute-done.10.refs_0_), channel_id=1, source_target_pairs={{0,16},{1,17},{2,18},{3,19},{4,20},{5,21},{6,22},{7,23},{8,24},{9,... | collective-permute-start | bytes 2359304 | tf_op jit(solution)/shard_map/ppermute | solution.py:65
  111.1 48.4 %collective-permute-start.26 = (bf16[384,1024]{1,0:T(8,128)(2,1)}, bf16[384,1024]{1,0:T(8,128)(2,1)}, u32[]{:S(2)}, u32[]{:S(2)}) collective-permute-start(bf16[384,1024]{1,0:T(8,128)(2,1)} %collective-permute-done.25.refs_14_), channel_id=1, source_target_pairs={{0,96},{1,97},{2,98},{3,99},{4,100},{5,101},{6,102},{7,103},{8,104... | collective-permute-start | bytes 2359304 | tf_op jit(solution)/shard_map/ppermute | solution.py:65
  114.4 74.2 %collective-permute-start.29 = (bf16[512,384]{1,0:T(8,128)(2,1)S(1)}, bf16[512,384]{1,0:T(8,128)(2,1)}, u32[]{:S(2)}, u32[]{:S(2)}) collective-permute-start(bf16[512,384]{1,0:T(8,128)(2,1)S(1)} %broadcast_select_fusion.1.refs_0_), channel_id=1, source_target_pairs={{0,96},{1,97},{2,98},{3,99},{4,100},{5,101},{6,102},{7,103},{8,104... | collective-permute-start | bytes 1179656 | tf_op jit(solution)/shard_map/ppermute | solution.py:65
  116.1 72.5 %collective-permute-start.32 = (bf16[512,384]{1,0:T(8,128)(2,1)}, bf16[512,384]{1,0:T(8,128)(2,1)}, u32[]{:S(2)}, u32[]{:S(2)}) collective-permute-start(bf16[512,384]{1,0:T(8,128)(2,1)} %collective-permute-done.31.refs_4_), channel_id=1, source_target_pairs={{0,32},{1,33},{2,34},{3,35},{4,36},{5,37},{6,38},{7,39},{8,40},{9,... | collective-permute-start | bytes 1179656 | tf_op jit(solution)/shard_map/ppermute | solution.py:65
  132.1 56.6 %collective-permute-start.30 = (bf16[512,384]{1,0:T(8,128)(2,1)}, bf16[512,384]{1,0:T(8,128)(2,1)}, u32[]{:S(2)}, u32[]{:S(2)}) collective-permute-start(bf16[512,384]{1,0:T(8,128)(2,1)} %collective-permute-done.28.refs_1_), channel_id=1, source_target_pairs={{0,32},{1,33},{2,34},{3,35},{4,36},{5,37},{6,38},{7,39},{8,40},{9,... | collective-permute-start | bytes 1179656 | tf_op jit(solution)/shard_map/ppermute | solution.py:65
  133.8 54.8 %collective-permute-start.34 = (bf16[512,384]{1,0:T(8,128)(2,1)}, bf16[512,384]{1,0:T(8,128)(2,1)}, u32[]{:S(2)}, u32[]{:S(2)}) collective-permute-start(bf16[512,384]{1,0:T(8,128)(2,1)} %collective-permute-done.33.refs_6_), channel_id=1, source_target_pairs={{0,96},{1,97},{2,98},{3,99},{4,100},{5,101},{6,102},{7,103},{8,104... | collective-permute-start | bytes 1179656 | tf_op jit(solution)/shard_map/ppermute | solution.py:65
  159.5 36.5 %collective-permute-start.47 = (bf16[64,3072]{1,0:T(8,128)(2,1)}, bf16[64,3072]{1,0:T(8,128)(2,1)S(1)}, u32[]{:S(2)}, u32[]{:S(2)}) collective-permute-start(bf16[64,3072]{1,0:T(8,128)(2,1)} %param.19), channel_id=1, source_target_pairs={{0,19},{1,18},{2,17},{3,16},{4,23},{5,22},{6,21},{7,20},{8,27},{9,... | collective-permute-start | bytes 1179656 | tf_op jit(solution)/shard_map/ppermute | solution.py:65
  194.9 78.3 %collective-permute-start.38 = (bf16[256,3072]{1,0:T(8,128)(2,1)}, bf16[256,3072]{1,0:T(8,128)(2,1)S(1)}, u32[]{:S(2)}, u32[]{:S(2)}) collective-permute-start(bf16[256,3072]{1,0:T(8,128)(2,1)} %get-tuple-element.38), channel_id=1, source_target_pairs={{0,16},{1,17},{2,18},{3,19},{4,20},{5,21},{6,22},{7,23},{8,24},{9,... | collective-permute-start | bytes 4718600 | tf_op jit(solution)/shard_map/ppermute | solution.py:65
  202.7 71.9 %collective-permute-start.41 = (bf16[256,3072]{1,0:T(8,128)(2,1)}, bf16[256,3072]{1,0:T(8,128)(2,1)}, u32[]{:S(2)}, u32[]{:S(2)}) collective-permute-start(bf16[256,3072]{1,0:T(8,128)(2,1)} %get-tuple-element.42), channel_id=1, source_target_pairs={{0,16},{1,17},{2,18},{3,19},{4,20},{5,21},{6,22},{7,23},{8,24},{9,... | collective-permute-start | bytes 4718600 | tf_op jit(solution)/shard_map/ppermute | solution.py:65
  207.5 43.6 %collective-permute-start.52 = (bf16[64,3072]{1,0:T(8,128)(2,1)S(1)}, bf16[64,3072]{1,0:T(8,128)(2,1)S(1)}, u32[]{:S(2)}, u32[]{:S(2)}) collective-permute-start(bf16[64,3072]{1,0:T(8,128)(2,1)S(1)} %collective-permute-done.48.refs_1_), channel_id=1, source_target_pairs={{0,1},{1,0},{2,3},{3,2},{4,5},{5,4},{6,7},{7,6},{8,9},{9,8},{10,11... | collective-permute-start | bytes 1179656 | tf_op jit(solution)/shard_map/ppermute | solution.py:65
  214.5 51.5 %collective-permute-start.53 = (bf16[64,3072]{1,0:T(8,128)(2,1)S(1)}, bf16[64,3072]{1,0:T(8,128)(2,1)S(1)}, u32[]{:S(2)}, u32[]{:S(2)}) collective-permute-start(bf16[64,3072]{1,0:T(8,128)(2,1)S(1)} %collective-permute-done.49.refs_2_), channel_id=1, source_target_pairs={{0,1},{1,0},{2,3},{3,2},{4,5},{5,4},{6,7},{7,6},{8,9},{9,8},{10,11... | collective-permute-start | bytes 1179656 | tf_op jit(solution)/shard_map/ppermute | solution.py:65
  214.8 51.6 %collective-permute-start.54 = (bf16[64,3072]{1,0:T(8,128)(2,1)}, bf16[64,3072]{1,0:T(8,128)(2,1)}, u32[]{:S(2)}, u32[]{:S(2)}) collective-permute-start(bf16[64,3072]{1,0:T(8,128)(2,1)} %collective-permute-done.51.refs_4_), channel_id=1, source_target_pairs={{0,1},{1,0},{2,3},{3,2},{4,5},{5,4},{6,7},{7,6},{8,9},{9,8},{10,11... | collective-permute-start | bytes 1179656 | tf_op jit(solution)/shard_map/ppermute | solution.py:65
  272.7 29.8 %collective-permute-start.55 = (bf16[128,3072]{1,0:T(8,128)(2,1)}, bf16[128,3072]{1,0:T(8,128)(2,1)S(1)}, u32[]{:S(2)}, u32[]{:S(2)}) collective-permute-start(bf16[128,3072]{1,0:T(8,128)(2,1)} %get-tuple-element.48), channel_id=1, source_target_pairs={{0,16},{1,17},{2,18},{3,19},{4,20},{5,21},{6,22},{7,23},{8,24},{9,... | collective-permute-start | bytes 2359304 | tf_op jit(solution)/shard_map/ppermute | solution.py:65
  (77 other events, 1487.3 us)
